TPU v7x, 32 devices: a whole 2x2x4 slice. The times are simulated.
32 devices in a mesh: wide: 16 (over z, y, core), narrow: 2 (over x).
Axes of the slice: x: 2, y: 2, z: 4, core: 2. Of those that a mesh axis runs over, the one named last changes fastest.
Arguments:
- tokens: bfloat16 [32, 384, 768], P(('wide', 'narrow')), may hold values from -6 to 6
- masked: int32 [32, 384], P(('wide', 'narrow')), may hold values from 0 to 1, as said below
- out_grad: bfloat16 [32, 768, 768], P(('wide', 'narrow')), may hold values from -6 to 6
- slot_block: int32 [16], replicated, may hold values from 0 to 12, as said below
- weights: float32 [16, 768, 768], P('narrow')
- vectors: float32 [6144], P('narrow')
- vec_first: float32 [6144], P('narrow')
- vec_second: float32 [6144], P('narrow'), as said below
- mom_first: float32 [16, 768, 768], P('narrow', 'wide')
- mom_second: float32 [16, 768, 768], P('narrow', 'wide'), as said below
- basis_left: float32 [16, 768, 768], P('narrow', None, 'wide'), as said below
- basis_right: float32 [16, 768, 768], P('narrow'), as said below
Outputs:
- layer_out: bfloat16 [32, 768, 768], P(('wide', 'narrow'))
- in_grad: bfloat16 [32, 384, 768], P(('wide', 'narrow'))
- new_weights: float32 [16, 768, 768], P('narrow')
- new_first: float32 [16, 768, 768], P('narrow', 'wide')
- new_second: float32 [16, 768, 768], P('narrow', 'wide')
- new_vectors: float32 [6144], P('narrow')
- new_vec_first: float32 [6144], P('narrow')
- new_vec_second: float32 [6144], P('narrow')
Inputs may be any that keep to these rules, and one draw needn't show every extreme that they name: `slot_block`: each of 0 to 11 appears exactly once; every other entry is 12 and marks a slot that holds no block. `masked`: in each aligned block of 16 positions of a sequence, 5 to 12 entries are 1. `basis_left`: each slot's matrix is orthogonal. `basis_right`: each slot's matrix is orthogonal. `mom_second`: every entry is positive. `vec_second`: every entry is positive.
All inputs are finite; a program needn't handle non-finite values.
Results may differ from a plain program's by a relative error of at most 0.012.
The roundings to bfloat16 on the way count: a program that leaves them out, or rounds other values in their place, can miss the bound.
Values may be sent and summed in bfloat16 or wider, within the bound.
No kernel may reach another device: no remote copies, remote signals or barrier semaphores. Data moves between devices by JAX's collectives and lax.ppermute only.
A program may use at most 320 MiB of HBM per device.

v0:
```python
from functools import partial
import math
from typing import NamedTuple

import jax
import jax.numpy as jnp
from jax import lax
from jax.experimental import pallas as pl
from jax.experimental.pallas import tpu as pltpu
from jax.sharding import PartitionSpec as P


D = 768
HEADS = 12
FF = 3072
BLK = 16
SEQ = 384
NBLK = 12
ROWS = 2 * SEQ
FFB = FF // D
PAIR = 128
NPAIR = D // PAIR
TILE = 128
CHUNK = 256

EPS_NORM = 1e-05
EPS_ADAM = 1e-08
RATE_MATRIX = 0.05
RATE_VECTOR = 0.3
BETA = 0.5
MASK_FILL = -1e30
GELU_A = math.sqrt(2.0 / math.pi)
GELU_B = 0.044715

BF = jnp.bfloat16
F32 = jnp.float32


NT = (((1,), (1,)), ((), ()))
TN = (((0,), (0,)), ((), ()))
NN = (((1,), (0,)), ((), ()))


def mm(a, b, dims=NN):
    return lax.dot_general(a, b, dims, preferred_element_type=F32)


def any_spec():
    return pl.BlockSpec(memory_space=pl.ANY)


class Group(NamedTuple):
    arrays: tuple
    where: tuple


def xor_permute(x, axis, size, mask):
    return lax.ppermute(x, axis, [(i, i ^ mask) for i in range(size)])


def far_bits(size):
    bits = []
    bit = size // 2
    while bit:
        bits.append(bit)
        bit //= 2
    return bits


def narrow_parts(x, size):
    have = {0: x}
    for bit in far_bits(size):
        fresh = {r | bit: xor_permute(have[r], "narrow", size, bit) for r in have}
        have.update(fresh)
    return [have[r] for r in range(size)]


def wide_group(x, size, order, merge):
    bufs = [(x[None], [0])]
    for i, bit in enumerate(order):
        fresh = [(xor_permute(a, "wide", size, bit), [r | bit for r in rels]) for a, rels in bufs]
        bufs = bufs + fresh
        if i < merge:
            bufs = [(jnp.concatenate([a for a, _ in bufs], axis=0), sum((r for _, r in bufs), []))]
    where = [None] * (2 ** len(order))
    for i, (_, rels) in enumerate(bufs):
        for j, r in enumerate(rels):
            where[r] = (i, j)
    return Group(tuple(a for a, _ in bufs), tuple(where))


def scatter_sum(keep, send, nwide, steps):
    parts = [keep, xor_permute(send, "wide", nwide, 1)]
    cur = keep.shape[0]
    for axis, size, bit in steps:
        half = cur // 2
        total = total_of([p[half:cur].astype(F32) for p in parts])
        got = xor_permute(total.astype(BF), axis, size, bit)
        parts = [p[:half] for p in parts] + [got]
        cur = half
    return total_of([p[0].astype(F32) for p in parts])


def butterfly_sum(x, axis, size, order, low=None):
    for bit in order:
        sent = x if low is None else x.astype(low)
        x = x + xor_permute(sent, axis, size, bit).astype(x.dtype)
    return x


def split_refs(groups, refs):
    out = []
    at = 0
    for arrays, where in groups:
        out.append((refs[at : at + arrays], where))
        at += arrays
    return out


def group_shapes(groups):
    return tuple((len(g.arrays), g.where) for g in groups)


def group_arrays(groups):
    return [a for g in groups for a in g.arrays]


def start_slices(group, index, dst, sem, me):
    refs, where = group
    count = len(where)
    rows = D // count
    base = me & (count - 1)
    for r, (i, j) in enumerate(where):
        at = pl.multiple_of((base ^ r) * rows, rows)
        pltpu.make_async_copy(refs[i].at[j, index], dst.at[pl.ds(at, rows)], sem).start()


def start_block(meta, block, own, groups, dst, sem):
    me = meta[0]
    source = meta[2 + block]
    index = meta[2 + NBLK + block]

    @pl.when(source == 0)
    def _():
        pltpu.make_async_copy(own.at[index], dst, sem).start()

    for k, group in enumerate(groups):

        @pl.when(source == k + 1)
        def _():
            start_slices(group, index, dst, sem, me)


def start_scatter(src, keep, send, item, steps, nwide, meta, sem):
    me = meta[0]
    rows = D // nwide
    side = (item & 1) ^ meta[1]
    for r in range(nwide):
        at = 0
        for axis, _, bit in steps:
            at = at * 2 + (side if axis == "narrow" else (1 if r & bit else 0))
        dst = send if r & 1 else keep
        row = pl.multiple_of((me ^ r) * rows, rows)
        pltpu.make_async_copy(src.at[pl.ds(row, rows)], dst.at[at, item // 2], sem).start()


def wait_block(dst, sem):
    pltpu.make_async_copy(dst, dst, sem).wait()


def norm_stats(z):
    mean = jnp.mean(z, axis=-1, keepdims=True)
    cen = z - mean
    var = jnp.mean(cen * cen, axis=-1, keepdims=True)
    return cen, lax.rsqrt(var + EPS_NORM)


def norm_back(zh, r, dz):
    return r * (
        dz
        - jnp.mean(dz, axis=-1, keepdims=True)
        - zh * jnp.mean(dz * zh, axis=-1, keepdims=True)
    )


def half_swap(z):
    lane = lax.broadcasted_iota(jnp.int32, z.shape, 1) % 64
    return jnp.where(lane < 32, pltpu.roll(z, PAIR - 32, 1), pltpu.roll(z, 32, 1))


def tile_masks():
    key = lax.broadcasted_iota(jnp.int32, (TILE, 2 * TILE), 0) // BLK
    qry = lax.broadcasted_iota(jnp.int32, (TILE, 2 * TILE), 1) % TILE // BLK
    return key == qry, key < qry, key <= qry


def head_split(x):
    lane = lax.broadcasted_iota(jnp.int32, x.shape, 1)
    zero = jnp.zeros_like(x)
    return jnp.concatenate([jnp.where(lane < 64, x, zero), jnp.where(lane < 64, zero, x)], axis=0)


def head_join(xt):
    row = lax.broadcasted_iota(jnp.int32, (PAIR, TILE), 0)
    return jnp.where(row < 64, xt[:, :TILE], xt[:, TILE:])


def key_parts(noised, t, masks):
    same, before, upto = masks
    parts = []
    if t > 0:
        parts.append((SEQ, TILE * t, None))
    parts.append((SEQ + TILE * t, TILE, before if noised else upto))
    if noised:
        parts.append((TILE * t, TILE, same))
    return parts


def masked_scores(k_ref, lanes, parts, qs):
    out = []
    for start, count, mask in parts:
        s = mm(k_ref[pl.ds(start, count), lanes], qs, NT)
        out.append(s if mask is None else jnp.where(mask, s, MASK_FILL))
    return out


def total_of(items):
    total = items[0]
    for x in items[1:]:
        total = total + x
    return total


def input_rows(tok_ref, mask_ref, vp_ref, half):
    tok = tok_ref[...].astype(F32)
    if half == 1:
        return tok
    return jnp.where(mask_ref[...] == 1, vp_ref[0:1, :], tok)


def forward_kernel(shapes, meta, tok, maskc, vp, cos, sin, own, *refs):
    nw = sum(n for n, _ in shapes)
    first = split_refs(shapes, refs)
    q_ref, k_ref, v_ref, n1_ref, o_ref, lse_ref, x2_ref, n2_ref = refs[nw : nw + 8]
    wbuf, sems = refs[nw + 8 :]
    for b in range(4):
        start_block(meta, b, own, first, wbuf.at[b], sems.at[b])
    for half in range(2):
        cen, r = norm_stats(input_rows(tok, maskc, vp, half))
        n1_ref[half * SEQ : (half + 1) * SEQ, :] = (cen * r * vp[1:2, :]).astype(BF)
    for b, out in enumerate((q_ref, k_ref, v_ref)):
        wait_block(wbuf.at[b], sems.at[b])
        for half in range(2):
            rows = slice(half * SEQ, (half + 1) * SEQ)
            for c in range(D // CHUNK):
                z = mm(n1_ref[rows, :], wbuf[b, :, c * CHUNK : (c + 1) * CHUNK])
                for s in range(CHUNK // PAIR):
                    piece = z[:, s * PAIR : (s + 1) * PAIR]
                    if b < 2:
                        piece = piece * cos[...] + half_swap(piece) * sin[...]
                    if b == 0:
                        piece = piece * 0.125
                    at = c * CHUNK + s * PAIR
                    out[rows, at : at + PAIR] = piece.astype(BF)

    masks = tile_masks()

    def one_pair(p, carry):
        lanes = pl.ds(pl.multiple_of(p * PAIR, PAIR), PAIR)
        for noised in (True, False):
            for t in range(SEQ // TILE):
                row = (0 if noised else SEQ) + TILE * t
                qs = head_split(q_ref[pl.ds(row, TILE), lanes])
                parts = key_parts(noised, t, masks)
                scores = masked_scores(k_ref, lanes, parts, qs)
                tops = [jnp.max(s, axis=0, keepdims=True) for s in scores]
                top = tops[0]
                for x in tops[1:]:
                    top = jnp.maximum(top, x)
                expo = [jnp.exp(s - top) for s in scores]
                total = total_of([jnp.sum(e, axis=0, keepdims=True) for e in expo])
                mixed = total_of(
                    [
                        mm(v_ref[pl.ds(start, count), lanes], e.astype(BF), TN)
                        for (start, count, _), e in zip(parts, expo)
                    ]
                )
                mixed = mixed * (1.0 / total)
                o_ref[pl.ds(row, TILE), lanes] = head_join(mixed).T.astype(BF)
                lse = top + jnp.log(total)
                lse_ref[p, 0:1, row : row + TILE] = lse[:, :TILE]
                lse_ref[p, 1:2, row : row + TILE] = lse[:, TILE:]
        return carry

    lax.fori_loop(0, NPAIR, one_pair, 0)
    wait_block(wbuf.at[3], sems.at[3])
    for half in range(2):
        rows = slice(half * SEQ, (half + 1) * SEQ)
        x2 = input_rows(tok, maskc, vp, half) + mm(o_ref[rows, :], wbuf[3])
        x2_ref[rows, :] = x2
        cen, r = norm_stats(x2)
        n2_ref[rows, :] = (cen * r * vp[2:3, :]).astype(BF)


def run_forward(meta, tok, maskc, vp, cos, sin, own, first):
    vm = pl.BlockSpec(memory_space=pltpu.VMEM)
    sq = jax.ShapeDtypeStruct((ROWS, D), BF)
    arrays = group_arrays(first)
    return pl.pallas_call(
        partial(forward_kernel, group_shapes(first)),
        name="forward_attention",
        out_shape=(
            sq,
            sq,
            sq,
            sq,
            sq,
            jax.ShapeDtypeStruct((NPAIR, 2, ROWS), F32),
            jax.ShapeDtypeStruct((ROWS, D), F32),
            sq,
        ),
        in_specs=[pl.BlockSpec(memory_space=pltpu.SMEM)] + [vm] * 5 + [any_spec()] * (1 + len(arrays)),
        out_specs=(vm,) * 8,
        scratch_shapes=[pltpu.VMEM((4, D, D), BF), pltpu.SemaphoreType.DMA((4,))],
    )(meta, tok, maskc, vp, cos, sin, own, *arrays)


def ffn_kernel(shapes, plans, nwide, meta, n2, og, x2, vp, own, *refs):
    nw = sum(n for n, _ in shapes)
    groups = split_refs(shapes, refs)
    layer_ref, up_keep, up_send, down_keep, down_send, dn2_ref, gbias_ref = refs[nw : nw + 7]
    wup, wdown, yacc, act, dhid, gup, gdown, sems, gsem = refs[nw + 7 :]
    f = pl.program_id(0)
    slot = f % 2

    @pl.when(f == 0)
    def _():
        for b in range(FFB):
            start_block(meta, 4 + b, own, groups, wup.at[b], sems.at[b])
            start_block(meta, 8 + b, own, groups, wdown.at[b], sems.at[4 + b])
        yacc[...] = jnp.zeros_like(yacc)
        dn2_ref[...] = jnp.zeros_like(dn2_ref)
        gbias_ref[FFB : FFB + 1, :] = jnp.sum(og[...].astype(F32), axis=0, keepdims=True)

    @pl.when(f > 1)
    def _():
        wait_block(gup.at[slot], gsem.at[slot])
        wait_block(gdown.at[slot], gsem.at[2 + slot])

    wait_block(wup.at[f], sems.at[f])
    wait_block(wdown.at[f], sems.at[4 + f])
    bias = vp[pl.ds(3 + f, 1), :]
    gb = jnp.zeros((1, D), F32)
    for c in range(ROWS // CHUNK):
        rows = slice(c * CHUNK, (c + 1) * CHUNK)
        h = mm(n2[rows, :], wup[f]) + bias
        hh = h * h
        th = jnp.tanh(h * (GELU_A + (GELU_A * GELU_B) * hh))
        lift = 0.5 + 0.5 * th
        slope = lift + (0.5 * h) * (1.0 - th * th) * (GELU_A + (3.0 * GELU_A * GELU_B) * hh)
        act[rows, :] = (h * lift).astype(BF)
        dh = mm(og[rows, :], wdown[f], NT) * slope
        gb = gb + jnp.sum(dh, axis=0, keepdims=True)
        dhid[rows, :] = dh.astype(BF)
        yacc[rows, :] += mm(act[rows, :], wdown[f])
        dn2_ref[rows, :] += mm(dhid[rows, :], wup[f], NT)
    gbias_ref[pl.ds(f, 1), :] = gb
    gdown[slot] = mm(og[...], act[...], TN).astype(BF)
    start_scatter(
        gdown.at[slot], down_keep, down_send, f, plans[1], nwide, meta, gsem.at[2 + slot]
    )
    gup[slot] = mm(dhid[...], n2[...], TN).astype(BF)
    start_scatter(gup.at[slot], up_keep, up_send, f, plans[0], nwide, meta, gsem.at[slot])

    @pl.when(f == FFB - 1)
    def _():
        layer_ref[...] = (x2[...] + yacc[...] + vp[7:8, :]).astype(BF)
        for k in range(2):
            wait_block(gup.at[k], gsem.at[k])
            wait_block(gdown.at[k], gsem.at[2 + k])


def scatter_shape(nwide, count):
    return jax.ShapeDtypeStruct((nwide, count // 2, D // nwide, D), BF)


def run_ffn(meta, n2, og, x2, vp, own, groups, plans, nwide):
    def whole(shape):
        return pl.BlockSpec(shape, lambda f: (0,) * len(shape))

    arrays = group_arrays(groups)
    part = scatter_shape(nwide, FFB)
    return pl.pallas_call(
        partial(ffn_kernel, group_shapes(groups), plans, nwide),
        name="feed_forward",
        grid=(FFB,),
        out_shape=(
            jax.ShapeDtypeStruct((ROWS, D), BF),
            part,
            part,
            part,
            part,
            jax.ShapeDtypeStruct((ROWS, D), F32),
            jax.ShapeDtypeStruct((8, D), F32),
        ),
        in_specs=[
            pl.BlockSpec(memory_space=pltpu.SMEM),
            whole((ROWS, D)),
            whole((ROWS, D)),
            whole((ROWS, D)),
            whole((8, D)),
        ]
        + [any_spec()] * (1 + len(arrays)),
        out_specs=(whole((ROWS, D)),) + (any_spec(),) * 4 + (whole((ROWS, D)), whole((8, D))),
        scratch_shapes=[
            pltpu.VMEM((FFB, D, D), BF),
            pltpu.VMEM((FFB, D, D), BF),
            pltpu.VMEM((ROWS, D), F32),
            pltpu.VMEM((ROWS, D), BF),
            pltpu.VMEM((ROWS, D), BF),
            pltpu.VMEM((2, D, D), BF),
            pltpu.VMEM((2, D, D), BF),
            pltpu.SemaphoreType.DMA((2 * FFB,)),
            pltpu.SemaphoreType.DMA((4,)),
        ],
    )(meta, n2, og, x2, vp, own, *arrays)


def resid_kernel(shapes, meta, x2, dn2, og, vp, o_ref, own, *refs):
    nw = sum(n for n, _ in shapes)
    first = split_refs(shapes, refs)
    dx2_ref, do_ref, gwo_ref, gg_ref = refs[nw : nw + 4]
    wbuf, dlow, sems = refs[nw + 4 :]
    start_block(meta, 3, own, first, wbuf, sems.at[0])
    gg = jnp.zeros((1, D), F32)
    for c in range(ROWS // CHUNK):
        rows = slice(c * CHUNK, (c + 1) * CHUNK)
        cen, r = norm_stats(x2[rows, :])
        zh = cen * r
        dn = dn2[rows, :]
        gg = gg + jnp.sum(dn * zh, axis=0, keepdims=True)
        dx = og[rows, :].astype(F32) + norm_back(zh, r, dn * vp[2:3, :])
        dx2_ref[rows, :] = dx
        dlow[rows, :] = dx.astype(BF)
    gg_ref[...] = gg
    gwo_ref[...] = mm(dlow[...], o_ref[...], TN).astype(BF)
    wait_block(wbuf, sems.at[0])
    do_ref[...] = mm(dlow[...], wbuf[...], NT).astype(BF)


def run_resid(meta, x2, dn2, og, vp, mixed, own, first):
    vm = pl.BlockSpec(memory_space=pltpu.VMEM)
    arrays = group_arrays(first)
    return pl.pallas_call(
        partial(resid_kernel, group_shapes(first)),
        name="residual_back",
        out_shape=(
            jax.ShapeDtypeStruct((ROWS, D), F32),
            jax.ShapeDtypeStruct((ROWS, D), BF),
            jax.ShapeDtypeStruct((D, D), BF),
            jax.ShapeDtypeStruct((1, D), F32),
        ),
        in_specs=[pl.BlockSpec(memory_space=pltpu.SMEM)] + [vm] * 5 + [any_spec()] * (1 + len(arrays)),
        out_specs=(vm,) * 4,
        scratch_shapes=[
            pltpu.VMEM((D, D), BF),
            pltpu.VMEM((ROWS, D), BF),
            pltpu.SemaphoreType.DMA((1,)),
        ],
    )(meta, x2, dn2, og, vp, mixed, own, *arrays)


def attention_back_kernel(q, k, v, do, lse_ref, cos, sin, pq, pk, pv, dk, dv):
    masks = tile_masks()

    def one_pair(p, carry):
        lanes = pl.ds(pl.multiple_of(p * PAIR, PAIR), PAIR)
        dk[...] = jnp.zeros_like(dk)
        dv[...] = jnp.zeros_like(dv)
        for noised in (True, False):
            for t in range(SEQ // TILE):
                row = (0 if noised else SEQ) + TILE * t
                qs = head_split(q[pl.ds(row, TILE), lanes])
                ds = head_split(do[pl.ds(row, TILE), lanes])
                lse = jnp.concatenate(
                    [lse_ref[p, 0:1, row : row + TILE], lse_ref[p, 1:2, row : row + TILE]], axis=1
                )
                parts = key_parts(noised, t, masks)
                probs = [jnp.exp(s - lse) for s in masked_scores(k, lanes, parts, qs)]
                prods = []
                for (start, count, _), e in zip(parts, probs):
                    prods.append(e * mm(v[pl.ds(start, count), lanes], ds, NT))
                    dv[start : start + count, :] += mm(e.astype(BF), ds)
                dot = total_of([jnp.sum(x, axis=0, keepdims=True) for x in prods])
                dq = None
                for (start, count, _), e, x in zip(parts, probs, prods):
                    g = (x - e * dot).astype(BF)
                    dk[start : start + count, :] += mm(g, qs)
                    one = mm(k[pl.ds(start, count), lanes], g, TN)
                    dq = one if dq is None else dq + one
                dq = head_join(dq).T * 0.125
                at = TILE * t
                turn = dq * cos[at : at + TILE, :] - half_swap(dq) * sin[at : at + TILE, :]
                pq[pl.ds(row, TILE), lanes] = turn.astype(BF)
        for half in range(2):
            rows = slice(half * SEQ, (half + 1) * SEQ)
            z = dk[rows, :]
            pk[rows, lanes] = (z * cos[...] - half_swap(z) * sin[...]).astype(BF)
            pv[rows, lanes] = dv[rows, :].astype(BF)
        return carry

    lax.fori_loop(0, NPAIR, one_pair, 0)


def run_attention_back(q, k, v, do, lse, cos, sin):
    vm = pl.BlockSpec(memory_space=pltpu.VMEM)
    sq = jax.ShapeDtypeStruct((ROWS, D), BF)
    return pl.pallas_call(
        attention_back_kernel,
        name="attention_back",
        out_shape=(sq, sq, sq),
        in_specs=[vm] * 7,
        out_specs=(vm,) * 3,
        scratch_shapes=[pltpu.VMEM((ROWS, PAIR), F32), pltpu.VMEM((ROWS, PAIR), F32)],
    )(q, k, v, do, lse, cos, sin)


def qkv_grad_kernel(plans, nwide, meta, n1, pq, pk, pv, gwo, *refs):
    outs = (refs[0:2], refs[2:4])
    res, sems = refs[4:]
    start_scatter(gwo, *outs[1], 1, plans[1], nwide, meta, sems.at[3])
    for i, x in enumerate((pq, pk, pv)):
        res[i] = mm(x[...], n1[...], TN).astype(BF)
        start_scatter(
            res.at[i], *outs[i // 2], i % 2, plans[i // 2], nwide, meta, sems.at[i]
        )
    for i in range(3):
        wait_block(res.at[i], sems.at[i])
    wait_block(gwo, sems.at[3])


def run_qkv_grad(meta, n1, pq, pk, pv, gwo, plans, nwide):
    vm = pl.BlockSpec(memory_space=pltpu.VMEM)
    return pl.pallas_call(
        partial(qkv_grad_kernel, plans, nwide),
        name="qkv_grad",
        out_shape=(scatter_shape(nwide, 2),) * 4,
        in_specs=[pl.BlockSpec(memory_space=pltpu.SMEM)] + [vm] * 5,
        out_specs=(any_spec(),) * 4,
        scratch_shapes=[pltpu.VMEM((3, D, D), BF), pltpu.SemaphoreType.DMA((4,))],
    )(meta, n1, pq, pk, pv, gwo)


def input_grad_kernel(shapes, meta, tok, maskc, vp, dx2, pq, pk, pv, own, *refs):
    nw = sum(n for n, _ in shapes)
    first = split_refs(shapes, refs)
    in_ref, ge_ref, gg_ref = refs[nw : nw + 3]
    wbuf, sems = refs[nw + 3 :]
    for b in range(3):
        start_block(meta, b, own, first, wbuf.at[b], sems.at[b])
    for b in range(3):
        wait_block(wbuf.at[b], sems.at[b])
    gg = jnp.zeros((1, D), F32)
    kept = None
    for half in range(2):
        rows = slice(half * SEQ, (half + 1) * SEQ)
        dn = total_of([mm(x[rows, :], wbuf[b], NT) for b, x in enumerate((pq, pk, pv))])
        cen, r = norm_stats(input_rows(tok, maskc, vp, half))
        zh = cen * r
        gg = gg + jnp.sum(dn * zh, axis=0, keepdims=True)
        dx = dx2[rows, :] + norm_back(zh, r, dn * vp[1:2, :])
        if half == 0:
            hit = maskc[...] == 1
            ge_ref[...] = jnp.sum(jnp.where(hit, dx, 0.0), axis=0, keepdims=True)
            kept = jnp.where(hit, 0.0, dx)
        else:
            in_ref[...] = (dx + kept).astype(BF)
    gg_ref[...] = gg


def run_input_grad(meta, tok, maskc, vp, dx2, pq, pk, pv, own, first):
    vm = pl.BlockSpec(memory_space=pltpu.VMEM)
    arrays = group_arrays(first)
    return pl.pallas_call(
        partial(input_grad_kernel, group_shapes(first)),
        name="input_grad",
        out_shape=(
            jax.ShapeDtypeStruct((SEQ, D), BF),
            jax.ShapeDtypeStruct((1, D), F32),
            jax.ShapeDtypeStruct((1, D), F32),
        ),
        in_specs=[pl.BlockSpec(memory_space=pltpu.SMEM)] + [vm] * 7 + [any_spec()] * (1 + len(arrays)),
        out_specs=(vm,) * 3,
        scratch_shapes=[pltpu.VMEM((3, D, D), BF), pltpu.SemaphoreType.DMA((3,))],
    )(meta, tok, maskc, vp, dx2, pq, pk, pv, own, *arrays)


def send_kernel(scalars, direct, tree, *outs):
    outs[0][...] = direct[...].astype(BF)
    if len(outs) > 1:
        outs[1][...] = tree[...].astype(BF)


def run_send(scalars, weights, nwide, at, count, tree_at, tree_count):
    rows = D // nwide
    outs = [jax.ShapeDtypeStruct((count, D // 2, D), BF)]
    specs = [pl.BlockSpec((1, D // 2, D), lambda s, sc: (s, 0, 0))]
    if tree_count:
        outs.append(jax.ShapeDtypeStruct((tree_count, rows, D), BF))
        specs.append(
            pl.BlockSpec((1, rows, D), lambda s, sc: (jnp.minimum(s, tree_count - 1), 0, 0))
        )
    return pl.pallas_call(
        send_kernel,
        name="send_weights",
        grid_spec=pltpu.PrefetchScalarGridSpec(
            num_scalar_prefetch=1,
            grid=(count,),
            in_specs=[
                pl.BlockSpec((1, D // 2, D), lambda s, sc: (sc[2 + at + s], sc[1], 0)),
                pl.BlockSpec(
                    (1, rows, D),
                    lambda s, sc: (sc[2 + tree_at + jnp.minimum(s, max(tree_count, 1) - 1)], sc[0], 0),
                ),
            ],
            out_specs=tuple(specs),
        ),
        out_shape=tuple(outs),
    )(scalars, weights, weights)


def turn_kernel(count, sizes, shapes, meta, items, slots, *refs):
    grads = refs[: len(sizes)]
    refs = refs[len(sizes) :]
    nw = sum(n for n, _ in shapes)
    (left,) = split_refs(shapes, refs)
    out = refs[nw]
    lbuf, gbuf, lsem, gsem = refs[nw + 1 :]
    for s in range(count):
        item = items[s]
        if len(grads) == 1:
            pltpu.make_async_copy(grads[0].at[item], gbuf.at[s], gsem.at[s]).start()
        else:

            @pl.when(item < sizes[0])
            def _():
                pltpu.make_async_copy(grads[0].at[item], gbuf.at[s], gsem.at[s]).start()

            @pl.when(item >= sizes[0])
            def _():
                pltpu.make_async_copy(
                    grads[1].at[item - sizes[0]], gbuf.at[s], gsem.at[s]
                ).start()

        start_slices(left, slots[s], lbuf.at[s], lsem.at[s], meta[0])
    parts = []
    for s in range(count):
        wait_block(gbuf.at[s], gsem.at[s])
        wait_block(lbuf.at[s], lsem.at[s])
        parts.append(mm(lbuf[s], gbuf[s], NT))
    out[...] = jnp.concatenate(parts, axis=1).astype(BF)


def run_turn(meta, items, slots, grads, left):
    count = items.shape[0]
    rows = grads[0].shape[1]
    sizes = tuple(g.shape[0] for g in grads)
    smem = pl.BlockSpec(memory_space=pltpu.SMEM)
    return pl.pallas_call(
        partial(turn_kernel, count, sizes, group_shapes([left])),
        name="gradient_turn",
        out_shape=jax.ShapeDtypeStruct((D, count * rows), BF),
        in_specs=[smem] * 3 + [any_spec()] * (len(grads) + len(left.arrays)),
        out_specs=pl.BlockSpec(memory_space=pltpu.VMEM),
        scratch_shapes=[
            pltpu.VMEM((count, D, D), BF),
            pltpu.VMEM((count, rows, D), BF),
            pltpu.SemaphoreType.DMA((count,)),
            pltpu.SemaphoreType.DMA((count,)),
        ],
    )(meta, items, slots, *grads, *left.arrays)


def adam_kernel(count, chained, slots, live, grads, first, second, right, *refs):
    nf, ns, back, full = refs[2 if chained else 0 :]
    s = pl.program_id(0)
    rows = first.shape[1]

    @pl.when(s == 0)
    def _():
        for k in range(count):
            for src in range(D // rows):
                at = slice(src * rows, (src + 1) * rows)
                full[k, :, at] = grads[at, k * rows : (k + 1) * rows].astype(F32)

    @pl.when(live[s] == 1)
    def _():
        basis = right[0].astype(BF)
        turned = mm(full[s].astype(BF), basis)
        one = BETA * first[0] + (1.0 - BETA) * turned
        two = BETA * second[0] + (1.0 - BETA) * turned * turned
        nf[0] = one
        ns[0] = two
        step = one / (jnp.sqrt(two) + EPS_ADAM)
        back[0] = mm(step.astype(BF), basis, NT).astype(BF)

    @pl.when(live[s] == 0)
    def _():
        nf[...] = jnp.zeros_like(nf)
        ns[...] = jnp.zeros_like(ns)
        back[...] = jnp.zeros_like(back)


def run_adam(slots, live, grads, first, second, right, earlier):
    count = slots.shape[0]
    rows = first.shape[1]
    state = pl.BlockSpec((1, rows, D), lambda s, slots, live: (slots[s], 0, 0))
    return pl.pallas_call(
        partial(adam_kernel, count, bool(earlier)),
        name="adam_step",
        grid_spec=pltpu.PrefetchScalarGridSpec(
            num_scalar_prefetch=2,
            grid=(count,),
            in_specs=[
                pl.BlockSpec(grads.shape, lambda s, *_: (0, 0)),
                state,
                state,
                pl.BlockSpec((1, D, D), lambda s, slots, live: (slots[s], 0, 0)),
            ]
            + [any_spec()] * len(earlier),
            out_specs=(state, state, pl.BlockSpec((1, rows, D), lambda s, *_: (s, 0, 0))),
            scratch_shapes=[pltpu.VMEM((count, rows, D), F32)],
        ),
        out_shape=(
            jax.ShapeDtypeStruct(first.shape, F32),
            jax.ShapeDtypeStruct(first.shape, F32),
            jax.ShapeDtypeStruct((count, rows, D), BF),
        ),
        input_output_aliases={6: 0, 7: 1} if earlier else {},
    )(slots, live, grads, first, second, right, *earlier)


def update_kernel(shapes, half, chained, slots, live, meta, weights, *refs):
    nw = sum(n for n, _ in shapes)
    back_a, back_b, left = split_refs(shapes, refs)
    out, lbuf, bbuf, lsem, bsem = refs[nw + (1 if chained else 0) :]
    s = pl.program_id(0)
    count = pl.num_programs(0)
    me = meta[0]
    slot = s % 2

    def begin(item, where):
        @pl.when(live[item] == 1)
        def _():
            @pl.when(item < half)
            def _():
                start_slices(back_a, item, bbuf.at[where], bsem.at[where], me)

            @pl.when(item >= half)
            def _():
                start_slices(back_b, item - half, bbuf.at[where], bsem.at[where], me)

            start_slices(left, slots[item], lbuf.at[where], lsem.at[where], me)

    @pl.when(s == 0)
    def _():
        begin(0, 0)

    @pl.when(s + 1 < count)
    def _():
        begin(s + 1, 1 - slot)

    @pl.when(live[s] == 1)
    def _():
        wait_block(lbuf.at[slot], lsem.at[slot])
        wait_block(bbuf.at[slot], bsem.at[slot])
        out[0] = weights[0] - RATE_MATRIX * mm(lbuf[slot], bbuf[slot], TN)

    @pl.when(live[s] == 0)
    def _():
        out[...] = jnp.zeros_like(out)


def run_update(slots, live, meta, weights, backs, half, left, earlier):
    groups = backs + [left]
    arrays = group_arrays(groups)
    whole = pl.BlockSpec((1, D, D), lambda s, slots, *_: (slots[s], 0, 0))
    return pl.pallas_call(
        partial(update_kernel, group_shapes(groups), half, bool(earlier)),
        name="weight_update",
        grid_spec=pltpu.PrefetchScalarGridSpec(
            num_scalar_prefetch=3,
            grid=(slots.shape[0],),
            in_specs=[whole] + [any_spec()] * (len(arrays) + len(earlier)),
            out_specs=whole,
            scratch_shapes=[
                pltpu.VMEM((2, D, D), BF),
                pltpu.VMEM((2, D, D), BF),
                pltpu.SemaphoreType.DMA((2,)),
                pltpu.SemaphoreType.DMA((2,)),
            ],
        ),
        out_shape=jax.ShapeDtypeStruct(weights.shape, F32),
        input_output_aliases={4 + len(arrays): 0} if earlier else {},
    )(slots, live, meta, weights, *arrays, *earlier)


def rotary_tables():
    half_size = D // HEADS // 2
    position_col = jnp.arange(SEQ, dtype=jnp.int32).astype(F32)
    frequency = jnp.exp(
        jnp.arange(half_size, dtype=F32) * (-2.0 * math.log(10000.0) / (2 * half_size))
    )
    angles = position_col[:, None] * frequency[None, :]
    cosine = jnp.cos(angles)
    sine = jnp.sin(angles)
    return (
        jnp.concatenate([cosine, cosine, cosine, cosine], axis=1),
        jnp.concatenate([-sine, sine, -sine, sine], axis=1),
    )


def on_device(nwide, nnarrow, *args):
    return whole_step(nwide, nnarrow, *args)


def whole_step(
    nwide,
    nnarrow,
    tokens,
    masked,
    out_grad,
    slot_block,
    weights,
    vectors,
    vec_first,
    vec_second,
    mom_first,
    mom_second,
    basis_left,
    basis_right,
):
    sd = weights.shape[0]
    slots = sd * nnarrow
    w = lax.axis_index("wide").astype(jnp.int32)
    n = lax.axis_index("narrow").astype(jnp.int32)
    top = nnarrow // 2
    nbit = n // top
    far_order = far_bits(nwide)
    left_order = far_order[:1] + far_order[-2:-1] + far_order[1:-2] + far_order[-1:]
    inner = [("wide", nwide, bit) for bit in far_order[-2::-1]]
    split = [("narrow", nnarrow, top)]
    near_x = tuple(split + inner)
    near_y = tuple(inner[:1] + split + inner[1:])

    ids = jnp.arange(slots, dtype=jnp.int32)
    hits = slot_block[None, :] == jnp.arange(NBLK, dtype=jnp.int32)[:, None]
    block_slot = jnp.sum(jnp.where(hits, ids[None, :], 0), axis=1)
    earlier = (
        (slot_block[None, :] < slot_block[:, None])
        | ((slot_block[None, :] == slot_block[:, None]) & (ids[None, :] < ids[:, None]))
    ) & (ids[None, :] // sd == ids[:, None] // sd)
    slot_rank = jnp.sum(earlier.astype(jnp.int32), axis=1)
    block_rank = jnp.sum(jnp.where(hits, slot_rank[None, :], 0), axis=1)
    own_blocks = lax.dynamic_slice_in_dim(slot_block, n * sd, sd)
    own_rank = lax.dynamic_slice_in_dim(slot_rank, n * sd, sd)
    at_rank = own_rank[None, :] == jnp.arange(sd, dtype=jnp.int32)[:, None]
    sorted_slots = jnp.sum(
        jnp.where(at_rank, jnp.arange(sd, dtype=jnp.int32)[None, :], 0), axis=1
    )
    sorted_blocks = jnp.sum(jnp.where(at_rank, own_blocks[None, :], 0), axis=1)
    sorted_live = (sorted_blocks < NBLK).astype(jnp.int32)

    scalars = jnp.concatenate([w[None], (w & 1)[None], sorted_slots]).astype(jnp.int32)
    c1 = min(4, sd)
    d1 = c1 // 2
    pieces = [("d1", 0, d1, True), ("t1", d1, c1 - d1, False)]
    if sd > c1:
        mid = (sd - c1) // 2
        pieces += [("d2", c1, mid, True), ("t2", c1 + mid, sd - c1 - mid, False)]

    def spread(x, direct):
        got = narrow_parts(x, nnarrow)[1:]
        got = got[0] if len(got) == 1 else jnp.concatenate(got, axis=0)
        if direct:
            return wide_group(got, nwide, [1], 0)
        return wide_group(got, nwide, far_order, len(far_order) - 2)

    direct, tree = run_send(scalars, weights, nwide, 0, d1, d1, c1 - d1)
    early_tree = spread(tree, False)
    early_direct = spread(direct, True)
    first = [early_direct, early_tree]
    groups = list(first)
    if sd > c1:
        direct, tree = run_send(scalars, weights, nwide, c1, mid, c1 + mid, sd - c1 - mid)
        groups += [spread(direct, True), spread(tree, False)]
    own = weights.astype(BF)

    far = n ^ (block_slot // sd)
    source = jnp.zeros((NBLK,), jnp.int32)
    index = block_slot % sd
    for k, (_, at, count, _) in enumerate(pieces):
        here = (far > 0) & (block_rank >= at) & (block_rank < at + count)
        source = jnp.where(here, k + 1, source)
        index = jnp.where(here, (far - 1) * count + block_rank - at, index)
    meta = jnp.concatenate([w[None], nbit[None], source, index]).astype(jnp.int32)

    vec_rel = jnp.stack(narrow_parts(vectors.astype(BF), nnarrow))
    vec_all = vec_rel[n ^ jnp.arange(nnarrow, dtype=jnp.int32)].reshape(8, D).astype(F32)

    left = wide_group(
        basis_left.transpose(0, 2, 1).astype(BF), nwide, left_order, len(left_order) - 2
    )

    cos, sin = rotary_tables()
    tok = tokens[0]
    maskc = masked[0][:, None]
    og = out_grad[0]

    q, k, v, n1, mixed, lse, x2, n2 = run_forward(meta, tok, maskc, vec_all, cos, sin, own, first)
    layer_out, up_keep, up_send, down_keep, down_send, dn2, gbias = run_ffn(
        meta, n2, og, x2, vec_all, own, groups, (near_y, near_x), nwide
    )

    def reduced(keep, send, steps):
        total = scatter_sum(keep, send, nwide, steps)
        rest = far_bits(nnarrow)[1:]
        total = butterfly_sum(total, "narrow", nnarrow, rest, BF).astype(BF)
        return [total, xor_permute(total, "narrow", nnarrow, top)]

    gdown = reduced(down_keep, down_send, near_x)
    gup = reduced(up_keep, up_send, near_y)
    dx2, do, gwo, gg2 = run_resid(meta, x2, dn2, og, vec_all, mixed, own, first)
    pq, pk, pv = run_attention_back(q, k, v, do, lse, cos, sin)
    qk_keep, qk_send, vo_keep, vo_send = run_qkv_grad(
        meta, n1, pq, pk, pv, gwo, (near_x, near_y), nwide
    )
    gqk = reduced(qk_keep, qk_send, near_x)
    gvo = reduced(vo_keep, vo_send, near_y)
    in_grad, ge, gg1 = run_input_grad(
        meta, tok, maskc, vec_all, dx2, pq, pk, pv, own, first
    )

    chunks = [(0, c1, 0)]
    if sd > c1:
        chunks = [(c1, sd, 4)] + chunks
    state = ()
    fresh = ()
    ffn_grads = jnp.concatenate(gup + gdown, axis=0)
    att_grads = jnp.concatenate(gqk + gvo, axis=0)
    for lo, hi, base in chunks:
        grads = [ffn_grads] if base else [att_grads, ffn_grads]
        block = jnp.clip(sorted_blocks[lo:hi], base, NBLK - 1)
        width = jnp.where(block < 4, 1, 2)
        start = jnp.where(block < 4, block // 2 * 2, block // 4 * 4)
        items = start - base + ((block & 1) ^ nbit) * width + (block - start) // 2
        held = sorted_slots[lo:hi]
        live = sorted_live[lo:hi]
        turned = run_turn(meta, items, held, grads, left)
        turned = lax.all_to_all(turned, "wide", 0, 0, tiled=True)
        *state, back = run_adam(
            held, live, turned, mom_first, mom_second, basis_right, state
        )
        half = (hi - lo + 1) // 2
        merge = len(far_order) - 2
        backs = [
            wide_group(back[:half], nwide, far_order, merge),
            wide_group(back[half:], nwide, left_order, merge),
        ]
        fresh = (run_update(held, live, meta, weights, backs, half, left, fresh),)
    new_first, new_second = state
    new_weights = fresh[0]

    vec_grad = jnp.concatenate([ge, gg1, gg2, gbias[: FFB + 1]], axis=0)
    vec_grad = butterfly_sum(vec_grad, "narrow", nnarrow, far_bits(nnarrow))
    vec_grad = butterfly_sum(vec_grad, "wide", nwide, far_order[:-1])
    vec_grad = butterfly_sum(vec_grad, "wide", nwide, far_order[-1:])
    vec_owned = lax.dynamic_slice_in_dim(
        vec_grad.reshape(nnarrow, vectors.shape[0]), n, 1, axis=0
    )[0]
    vec_mean = BETA * vec_first + (1.0 - BETA) * vec_owned
    vec_square = BETA * vec_second + (1.0 - BETA) * vec_owned * vec_owned
    vec_new = vectors - RATE_VECTOR * vec_mean / (jnp.sqrt(vec_square) + EPS_ADAM)
    return (
        layer_out[None],
        in_grad[None],
        new_weights,
        new_first,
        new_second,
        vec_new,
        vec_mean,
        vec_square,
    )


def solution(mesh):
    return jax.shard_map(
        partial(on_device, mesh.shape["wide"], mesh.shape["narrow"]),
        mesh=mesh,
        in_specs=(
            P(("wide", "narrow"), None, None),
            P(("wide", "narrow"), None),
            P(("wide", "narrow"), None, None),
            P(),
            P("narrow", None, None),
            P("narrow"),
            P("narrow"),
            P("narrow"),
            P("narrow", "wide", None),
            P("narrow", "wide", None),
            P("narrow", None, "wide"),
            P("narrow", None, None),
        ),
        out_specs=(
            P(("wide", "narrow"), None, None),
            P(("wide", "narrow"), None, None),
            P("narrow", None, None),
            P("narrow", "wide", None),
            P("narrow", "wide", None),
            P("narrow"),
            P("narrow"),
            P("narrow"),
        ),
        check_vma=False,
    )
```

profile of v0, /device:TPU:0, one launch (start us, length us, event | category | flops | bytes accessed | tf_op | source)
XLA Modules:
  0.0 520.1 jit_solution(12247789775987154428)
XLA Ops:
  3.6 3.4 send_weights.2
  7.0 3.0 collective-permute-start.3
  10.0 1.9 collective-permute-start.1
  12.0 3.3 send_weights.3
  15.3 1.9 collective-permute-start.11
  17.4 2.7 collective-permute-start.4
  20.1 47.8 %collective-permute-done.11 = bf16[2,48,768]{2,1,0:T(8,128)(2,1)S(1)} collective-permute-done((bf16[2,48,768]{2,1,0:T(8,128)(2,1)}, bf16[2,48,768]{2,1,0:T(8,128)(2,1)S(1)}, u32[]{:S(2)}, u32[]{:S(2)}) %collective-permute-start.11) | collective-permute-done | bytes 147488 | tf_op jit(solution)/shard_map/ppermute | solution.py:58
  67.9 2.8 collective-permute-start.12
  70.7 1.6 collective-permute-start.5
  72.4 4.5 collective-permute-done.12
  77.7 4.4 collective-permute-done.5
  84.5 2.3 collective-permute-done.13
  89.7 8.1 %collective-permute-done.6.refs_3_ = bf16[4,2,48,768]{3,2,1,0:T(8,128)(2,1)S(1)} collective-permute-done((bf16[4,2,48,768]{3,2,1,0:T(8,128)(2,1)S(1)}, bf16[4,2,48,768]{3,2,1,0:T(8,128)(2,1)S(1)}, u32[]{:S(2)}, u32[]{:S(2)}) %collective-permute-start.6) | collective-permute-done | bytes 589856 | tf_op jit(solution)/shard_map/ppermute | solution.py:58
  99.3 7.8 %collective-permute-done.14.refs_9_ = bf16[4,2,48,768]{3,2,1,0:T(8,128)(2,1)S(1)} collective-permute-done((bf16[4,2,48,768]{3,2,1,0:T(8,128)(2,1)}, bf16[4,2,48,768]{3,2,1,0:T(8,128)(2,1)S(1)}, u32[]{:S(2)}, u32[]{:S(2)}) %collective-permute-start.14) | collective-permute-done | bytes 589856 | tf_op jit(solution)/shard_map/ppermute | solution.py:58
  111.5 9.8 %convert_element_type.501.own = bf16[8,768,768]{2,1,0:T(8,128)(2,1)} convert(f32[8,768,768]{2,1,0:T(8,128)} %weights.3) | non-fusion elementwise | flops 4718592 | bytes 28311552 | tf_op jit(solution)/shard_map/convert_element_type | solution.py:897
  127.2 22.1 %forward_attention.1 = (bf16[768,768]{1,0:T(8,128)(2,1)}, bf16[768,768]{1,0:T(8,128)(2,1)}, bf16[768,768]{1,0:T(8,128)(2,1)}, bf16[768,768]{1,0:T(8,128)(2,1)}, ...) custom-call(s32[26]{0:T(128)} %pad_add_fusion.meta, ...), custom_call_target="tpu_custom_call" | custom-call | tf_op jit(solution)/shard_map/forward_attention/pallas_call | solution.py:309
  149.4 31.9 %feed_forward.1 = (bf16[768,768]{1,0:T(8,128)(2,1)}, bf16[16,2,48,768]{3,2,1,0:T(8,128)(2,1)}, bf16[16,2,48,768]{3,2,1,0:T(8,128)(2,1)}, bf16[16,2,48,768]{3,2,1...) custom-call(s32[26]{0:T(128)} %pad_add_fusion.meta, ...), custom_call_target="tpu_custom_call" | custom-call | tf_op jit(solution)/shard_map/feed_forward/pallas_call | solution.py:393
  181.8 2.4 pad_maximum_fusion.1
  185.8 8.7 %residual_back.1 = (f32[768,768]{1,0:T(8,128)}, bf16[768,768]{1,0:T(8,128)(2,1)}, bf16[768,768]{1,0:T(8,128)(2,1)}, f32[1,768]{1,0:T(1,128)}) custom-call(s32[26]{0:T(128)} %pad_add_fusion.meta, f32[768,768]{1,0:T(8,128)} %get-tuple-element.50.x2, f32[768,768]{1,0:T(8,128)} %get-tuple-element.54.dn2, bf16[768,768]{1,0:T(8,128)(2,1)} %bitcast.46, ...), custom_call_target="tpu_custom_call" | custom-call | tf_op jit(solution)/shard_map/residual_back/pallas_call | solution.py:454
  194.5 20.0 %attention_back.1 = (bf16[768,768]{1,0:T(8,128)(2,1)}, bf16[768,768]{1,0:T(8,128)(2,1)}, bf16[768,768]{1,0:T(8,128)(2,1)}) custom-call(bf16[768,768]{1,0:T(8,128)(2,1)} %get-tuple-element.57.q, bf16[768,768]{1,0:T(8,128)(2,1)} %get-tuple-element.58.k, bf16[768,768]{1,0:T(8,128)(2,1)} %get-tuple-element.59.v, bf16[768,768]{1,0:T(8,128)(2,1)} %get-tuple-element.60.do, ...), custom_call_target="tpu_custom_call" | custom-call | tf_op jit(solution)/shard_map/attention_back/pallas_call | solution.py:518
  214.5 6.8 %qkv_grad.1 = (bf16[16,1,48,768]{3,2,1,0:T(8,128)(2,1)}, bf16[16,1,48,768]{3,2,1,0:T(8,128)(2,1)}, bf16[16,1,48,768]{3,2,1,0:T(8,128)(2,1)}, bf16[16,1,48,768]{3,2,1,0:T(8,128)(2,1)}) custom-call(s32[26]{0:T(128)} %pad_add_fusion.meta, bf16[768,768]{1,0:T(8,128)(2,1)} %get-tuple-element.66.n1, bf16[768,768]{1,0:T(8,128)(2,1)} %get-tuple-element.62.pq, ...), custom_call_target="tpu_custom_call" | custom-call | tf_op jit(solution)/shard_map/qkv_grad/pallas_call | solution.py:544
  221.4 1.8 pad_maximum_fusion.refs_2_.refs_1_.refs_8_
  225.2 1.7 add_convert_fusion
  226.9 1.7 collective-permute-start.36
  228.6 1.7 add_convert_fusion.1
  230.3 1.6 collective-permute-start.30
  233.2 7.7 %collective-permute-done.24 = bf16[8,1,48,768]{3,2,1,0:T(8,128)(2,1)S(1)} collective-permute-done((bf16[8,1,48,768]{3,2,1,0:T(8,128)(2,1)S(1)}, bf16[8,1,48,768]{3,2,1,0:T(8,128)(2,1)S(1)}, u32[]{:S(2)}, u32[]{:S(2)}) %collective-permute-start.24) | collective-permute-done | bytes 589856 | tf_op jit(solution)/shard_map/ppermute | solution.py:58
  241.0 26.5 %collective-permute-done.18 = bf16[8,1,48,768]{3,2,1,0:T(8,128)(2,1)S(1)} collective-permute-done((bf16[8,1,48,768]{3,2,1,0:T(8,128)(2,1)S(1)}, bf16[8,1,48,768]{3,2,1,0:T(8,128)(2,1)S(1)}, u32[]{:S(2)}, u32[]{:S(2)}) %collective-permute-start.18) | collective-permute-done | bytes 589856 | tf_op jit(solution)/shard_map/ppermute | solution.py:58
  267.5 1.6 collective-permute-start.25
  269.3 7.7 %collective-permute-done.43.refs_3_.refs_2_.refs_9_ = bf16[4,8,48,768]{3,2,1,0:T(8,128)(2,1)S(1)} collective-permute-done((bf16[4,8,48,768]{3,2,1,0:T(8,128)(2,1)S(1)}, bf16[4,8,48,768]{3,2,1,0:T(8,128)(2,1)S(1)}, u32[]{:S(2)}, u32[]{:S(2)}) %collective-permute-start.43) | collective-permute-done | bytes 2359328 | tf_op jit(solution)/shard_map/ppermute | solution.py:58
  281.6 1.7 collective-permute-start.31
  283.4 3.4 collective-permute-done.19
  287.9 10.2 %collective-permute-done.37 = bf16[4,2,48,768]{3,2,1,0:T(8,128)(2,1)S(1)} collective-permute-done((bf16[4,2,48,768]{3,2,1,0:T(8,128)(2,1)S(1)}, bf16[4,2,48,768]{3,2,1,0:T(8,128)(2,1)S(1)}, u32[]{:S(2)}, u32[]{:S(2)}) %collective-permute-start.37) | collective-permute-done | bytes 589856 | tf_op jit(solution)/shard_map/ppermute | solution.py:58
  304.2 6.9 %collective-permute-done.38 = bf16[2,2,48,768]{3,2,1,0:T(8,128)(2,1)S(1)} collective-permute-done((bf16[2,2,48,768]{3,2,1,0:T(8,128)(2,1)S(1)}, bf16[2,2,48,768]{3,2,1,0:T(8,128)(2,1)S(1)}, u32[]{:S(2)}, u32[]{:S(2)}) %collective-permute-start.38) | collective-permute-done | bytes 294944 | tf_op jit(solution)/shard_map/ppermute | solution.py:58
  313.6 3.5 collective-permute-done.32
  318.8 7.8 %collective-permute-done.39 = bf16[1,2,48,768]{3,2,1,0:T(8,128)(2,1)S(1)} collective-permute-done((bf16[1,2,48,768]{3,2,1,0:T(8,128)(2,1)S(1)}, bf16[1,2,48,768]{3,2,1,0:T(8,128)(2,1)S(1)}, u32[]{:S(2)}, u32[]{:S(2)}) %collective-permute-start.39) | collective-permute-done | bytes 147488 | tf_op jit(solution)/shard_map/ppermute | solution.py:58
  327.6 5.6 %collective-permute-done.33 = bf16[1,2,48,768]{3,2,1,0:T(8,128)(2,1)S(1)} collective-permute-done((bf16[1,2,48,768]{3,2,1,0:T(8,128)(2,1)S(1)}, bf16[1,2,48,768]{3,2,1,0:T(8,128)(2,1)S(1)}, u32[]{:S(2)}, u32[]{:S(2)}) %collective-permute-start.33) | collective-permute-done | bytes 147488 | tf_op jit(solution)/shard_map/ppermute | solution.py:58
  333.1 1.6 collective-permute-start.40
  338.3 2.7 collective-permute-done.34
  344.7 6.9 %gradient_turn.3 = bf16[768,192]{1,0:T(8,128)(2,1)} custom-call(s32[26]{0:T(128)} %pad_add_fusion.meta, s32[4]{0:T(128)} %get-tuple-element.102.items, s32[4]{0:T(128)} %get-tuple-element.111.slots, bf16[8,48,768]{2,1,0:T(8,128)(2,1)} %pad_maximum_fusion.4.refs_1_.refs_0_, bf16[4,8,48,768]{3,2,1,0:T(8,128)(2,1)} %copy-done, ...), custom_call_target="tpu_custom_call" | custom-call | tf_op jit(solution)/shard_map/gradient_turn/pallas_call | solution.py:669
  351.6 3.8 all-to-all-start.1
  358.1 1.6 collective-permute-start.22
  359.7 1.7 collective-permute-done.28
  363.4 6.8 %gradient_turn.2 = bf16[768,192]{1,0:T(8,128)(2,1)} custom-call(s32[26]{0:T(128)} %pad_add_fusion.meta, s32[4]{0:T(128)} %get-tuple-element.103.items, s32[4]{0:T(128)} %get-tuple-element.110.slots, bf16[4,48,768]{2,1,0:T(8,128)(2,1)} %pad_maximum_fusion.11.refs_0_, bf16[8,48,768]{2,1,0:T(8,128)(2,1)} %pad_maximum_fusion.4.refs_1_.refs_0_, ...), custom_call_target="tpu_custom_call" | custom-call | tf_op jit(solution)/shard_map/gradient_turn/pallas_call | solution.py:669
  370.3 5.9 %all-to-all-start = ((bf16[16,48,192]{2,1,0:T(8,128)(2,1)}), bf16[16,48,192]{2,1,0:T(8,128)(2,1)S(1)}, u32[]{:S(2)}, u32[]{:S(2)}) async-start(bf16[16,48,192]{2,1,0:T(8,128)(2,1)} %bitcast.50), calls=%async_computation | async-start | bytes 786432 | tf_op jit(solution)/shard_map/all_to_all | solution.py:960
  376.8 7.5 %adam_step.2 = (f32[8,48,768]{2,1,0:T(8,128)}, f32[8,48,768]{2,1,0:T(8,128)}, bf16[4,48,768]{2,1,0:T(8,128)(2,1)}) custom-call(s32[4]{0:T(128)} %get-tuple-element.111.slots, s32[4]{0:T(128)} %get-tuple-element.104.live, bf16[768,192]{1,0:T(8,128)(2,1)} %bitcast.51, f32[8,48,768]{2,1,0:T(8,128)} %first.3, f32[8,48,768]{2,1,0:T(8,128)} %second.3, ...), custom_call_target="tpu_custom_call" | custom-call | tf_op jit(solution)/shard_map/adam_step/pallas_call | solution.py:718
  384.3 4.1 all-to-all-done
  389.1 8.3 %adam_step.3 = (f32[8,48,768]{2,1,0:T(8,128)}, f32[8,48,768]{2,1,0:T(8,128)}, bf16[4,48,768]{2,1,0:T(8,128)(2,1)}) custom-call(s32[4]{0:T(128)} %get-tuple-element.110.slots, s32[4]{0:T(128)} %get-tuple-element.105.live, bf16[768,192]{1,0:T(8,128)(2,1)} %bitcast.52, f32[8,48,768]{2,1,0:T(8,128)} %first.3, ...), custom_call_target="tpu_custom_call", output_to_operand_aliasing={{0}: (6, {}), {1}: (7, {})} | custom-call | tf_op jit(solution)/shard_map/adam_step/pallas_call | solution.py:718
  398.4 1.8 collective-permute-start.46
  401.5 9.9 %input_grad.1 = (bf16[384,768]{1,0:T(8,128)(2,1)}, f32[1,768]{1,0:T(1,128)}, f32[1,768]{1,0:T(1,128)}) custom-call(s32[26]{0:T(128)} %pad_add_fusion.meta, bf16[384,768]{1,0:T(8,128)(2,1)} %bitcast.48, s32[384,1]{1,0:T(8,128)} %copy.28.maskc, f32[8,768]{1,0:T(8,128)} %reshape.367.vp, f32[768,768]{1,0:T(8,128)} %get-tuple-element.56.dx2, ...), custom_call_target="tpu_custom_call" | custom-call | tf_op jit(solution)/shard_map/input_grad/pallas_call | solution.py:584
  411.4 1.8 collective-permute-start.51
  413.3 1.6 collective-permute-done.56
  415.4 1.6 collective-permute-start.66
  417.0 3.5 collective-permute-start.61
  422.2 6.7 %collective-permute-done.47 = bf16[2,2,48,768]{3,2,1,0:T(8,128)(2,1)S(1)} collective-permute-done((bf16[2,2,48,768]{3,2,1,0:T(8,128)(2,1)S(1)}, bf16[2,2,48,768]{3,2,1,0:T(8,128)(2,1)S(1)}, u32[]{:S(2)}, u32[]{:S(2)}) %collective-permute-start.47) | collective-permute-done | bytes 294944 | tf_op jit(solution)/shard_map/ppermute | solution.py:58
  429.1 4.5 collective-permute-done.57
  436.1 4.7 collective-permute-done.67
  440.8 3.8 collective-permute-done.68
  445.5 16.3 %collective-permute-done.69 = f32[8,768]{1,0:T(8,128)S(1)} collective-permute-done((f32[8,768]{1,0:T(8,128)S(1)}, f32[8,768]{1,0:T(8,128)S(1)}, u32[]{:S(2)}, u32[]{:S(2)}) %collective-permute-start.69) | collective-permute-done | bytes 24608 | tf_op jit(solution)/shard_map/ppermute | solution.py:58
  462.2 2.1 collective-permute-start.63
  464.9 13.5 %collective-permute-done.53.refs_5_ = bf16[4,2,48,768]{3,2,1,0:T(8,128)(2,1)} collective-permute-done((bf16[4,2,48,768]{3,2,1,0:T(8,128)(2,1)S(1)}, bf16[4,2,48,768]{3,2,1,0:T(8,128)(2,1)}, u32[]{:S(2)}, u32[]{:S(2)}) %collective-permute-start.53) | collective-permute-done | bytes 589856 | tf_op jit(solution)/shard_map/ppermute | solution.py:58
  478.4 12.0 %collective-permute-done.63.refs_5_ = bf16[4,2,48,768]{3,2,1,0:T(8,128)(2,1)S(1)} collective-permute-done((bf16[4,2,48,768]{3,2,1,0:T(8,128)(2,1)S(1)}, bf16[4,2,48,768]{3,2,1,0:T(8,128)(2,1)S(1)}, u32[]{:S(2)}, u32[]{:S(2)}) %collective-permute-start.63) | collective-permute-done | bytes 589856 | tf_op jit(solution)/shard_map/ppermute | solution.py:58
  493.5 12.9 %weight_update.2.refs_12_ = f32[8,768,768]{2,1,0:T(8,128)} custom-call(s32[4]{0:T(128)} %get-tuple-element.111.slots, s32[4]{0:T(128)} %get-tuple-element.104.live, s32[26]{0:T(128)} %pad_add_fusion.meta, f32[8,768,768]{2,1,0:T(8,128)} %weights.3, bf16[4,2,48,768]{3,2,1,0:T(8,128)(2,1)} %copy-done.14, bf16[4,2,48,768]{3,2,1,0:T(8,128)(2,1)} %copy-done.27, ...), custom_call_target="tpu_custom_call" | custom-call | tf_op jit(solution)/shard_map/weight_update/pallas_call | solution.py:788
  506.5 13.4 %weight_update.3 = f32[8,768,768]{2,1,0:T(8,128)} custom-call(s32[4]{0:T(128)} %get-tuple-element.110.slots, s32[4]{0:T(128)} %get-tuple-element.105.live, s32[26]{0:T(128)} %pad_add_fusion.meta, f32[8,768,768]{2,1,0:T(8,128)} %weights.3, bf16[4,2,48,768]{3,2,1,0:T(8,128)(2,1)} %copy-done.16, ...), custom_call_target="tpu_custom_call", output_to_operand_aliasing={{}: (16, {})} | custom-call | tf_op jit(solution)/shard_map/weight_update/pallas_call | solution.py:788
  (267 shorter events, 69.1 us)
Async XLA Ops:
  7.0 10.4 %collective-permute-start.3 = (bf16[2,48,768]{2,1,0:T(8,128)(2,1)}, bf16[2,48,768]{2,1,0:T(8,128)(2,1)S(1)}, u32[]{:S(2)}, u32[]{:S(2)}) collective-permute-start(bf16[2,48,768]{2,1,0:T(8,128)(2,1)} %get-tuple-element.48), channel_id=1, source_target_pairs={{0,1},{1,0},{2,3},{3,2},{4,5},{5,4},{6,7},{7,6},{8,9},{9,8},{10,11... | collective-permute-start | bytes 442376 | tf_op jit(solution)/shard_map/ppermute | solution.py:58
  10.0 77.7 %collective-permute-start = (bf16[3072]{0:T(1024)(128)(2,1)S(1)}, bf16[3072]{0:T(1024)(128)(2,1)}, u32[]{:S(2)}, u32[]{:S(2)}) collective-permute-start(bf16[3072]{0:T(1024)(128)(2,1)S(1)} %convert_element_type.497), channel_id=1, source_target_pairs={{0,1},{1,0},{2,3},{3,2},{4,5},{5,4},{6,7},{7,6},{8,9},{9,8},{10,11... | collective-permute-start | bytes 18440 | tf_op jit(solution)/shard_map/ppermute | solution.py:58
  10.0 79.1 %collective-permute-start.1 = (bf16[2,384,768]{2,1,0:T(8,128)(2,1)}, bf16[2,384,768]{2,1,0:T(8,128)(2,1)S(1)}, u32[]{:S(2)}, u32[]{:S(2)}) collective-permute-start(bf16[2,384,768]{2,1,0:T(8,128)(2,1)} %get-tuple-element.47), channel_id=1, source_target_pairs={{0,1},{1,0},{2,3},{3,2},{4,5},{5,4},{6,7},{7,6},{8,9},{9,8},{10,11... | collective-permute-start | bytes 3538952 | tf_op jit(solution)/shard_map/ppermute | solution.py:58
  15.2 74.2 %collective-permute-start.9 = (bf16[2,384,768]{2,1,0:T(8,128)(2,1)}, bf16[2,384,768]{2,1,0:T(8,128)(2,1)}, u32[]{:S(2)}, u32[]{:S(2)}) collective-permute-start(bf16[2,384,768]{2,1,0:T(8,128)(2,1)} %get-tuple-element.51), channel_id=1, source_target_pairs={{0,1},{1,0},{2,3},{3,2},{4,5},{5,4},{6,7},{7,6},{8,9},{9,8},{10,11... | collective-permute-start | bytes 3538952 | tf_op jit(solution)/shard_map/ppermute | solution.py:58
  15.3 52.5 %collective-permute-start.11 = (bf16[2,48,768]{2,1,0:T(8,128)(2,1)}, bf16[2,48,768]{2,1,0:T(8,128)(2,1)S(1)}, u32[]{:S(2)}, u32[]{:S(2)}) collective-permute-start(bf16[2,48,768]{2,1,0:T(8,128)(2,1)} %get-tuple-element.52), channel_id=1, source_target_pairs={{0,1},{1,0},{2,3},{3,2},{4,5},{5,4},{6,7},{7,6},{8,9},{9,8},{10,11... | collective-permute-start | bytes 442376 | tf_op jit(solution)/shard_map/ppermute | solution.py:58
  17.4 53.3 %collective-permute-start.4 = (bf16[1,2,48,768]{3,2,1,0:T(8,128)(2,1)S(1)}, bf16[1,2,48,768]{3,2,1,0:T(8,128)(2,1)S(1)}, u32[]{:S(2)}, u32[]{:S(2)}) collective-permute-start(bf16[1,2,48,768]{3,2,1,0:T(8,128)(2,1)S(1)} %bitcast.53), channel_id=1, source_target_pairs={{0,16},{2,18},{4,20},{6,22},{8,24},{10,26},{12,28},{14,30},{16,0},... | collective-permute-start | bytes 442376 | tf_op jit(solution)/shard_map/ppermute | solution.py:58
  67.9 9.1 %collective-permute-start.12 = (bf16[1,2,48,768]{3,2,1,0:T(8,128)(2,1)S(1)}, bf16[1,2,48,768]{3,2,1,0:T(8,128)(2,1)S(1)}, u32[]{:S(2)}, u32[]{:S(2)}) collective-permute-start(bf16[1,2,48,768]{3,2,1,0:T(8,128)(2,1)S(1)} %bitcast.56), channel_id=1, source_target_pairs={{0,16},{2,18},{4,20},{6,22},{8,24},{10,26},{12,28},{14,30},{16,0},... | collective-permute-start | bytes 442376 | tf_op jit(solution)/shard_map/ppermute | solution.py:58
  70.7 11.3 %collective-permute-start.5 = (bf16[2,2,48,768]{3,2,1,0:T(8,128)(2,1)S(1)}, bf16[2,2,48,768]{3,2,1,0:T(8,128)(2,1)S(1)}, u32[]{:S(2)}, u32[]{:S(2)}) collective-permute-start(bf16[2,2,48,768]{3,2,1,0:T(8,128)(2,1)S(1)} %pad_maximum_fusion.9), channel_id=1, source_target_pairs={{0,8},{2,10},{4,12},{6,14},{8,0},{10,2},{12,4},{14,6},{16,24},{18,... | collective-permute-start | bytes 884744 | tf_op jit(solution)/shard_map/ppermute | solution.py:58
  77.0 9.8 %collective-permute-start.13 = (bf16[2,2,48,768]{3,2,1,0:T(8,128)(2,1)S(1)}, bf16[2,2,48,768]{3,2,1,0:T(8,128)(2,1)S(1)}, u32[]{:S(2)}, u32[]{:S(2)}) collective-permute-start(bf16[2,2,48,768]{3,2,1,0:T(8,128)(2,1)S(1)} %pad_maximum_fusion.10), channel_id=1, source_target_pairs={{0,8},{2,10},{4,12},{6,14},{8,0},{10,2},{12,4},{14,6},{16,24},{18,... | collective-permute-start | bytes 884744 | tf_op jit(solution)/shard_map/ppermute | solution.py:58
  82.1 15.7 %collective-permute-start.6 = (bf16[4,2,48,768]{3,2,1,0:T(8,128)(2,1)S(1)}, bf16[4,2,48,768]{3,2,1,0:T(8,128)(2,1)S(1)}, u32[]{:S(2)}, u32[]{:S(2)}) collective-permute-start(bf16[4,2,48,768]{3,2,1,0:T(8,128)(2,1)S(1)} %pad_maximum_fusion.2.refs_2_), channel_id=1, source_target_pairs={{0,4},{2,6},{4,0},{6,2},{8,12},{10,14},{12,8},{14,10},{16,20},{18,... | collective-permute-start | bytes 1769480 | tf_op jit(solution)/shard_map/ppermute | solution.py:58
  86.8 12.0 %collective-permute-start.7 = (bf16[4,2,48,768]{3,2,1,0:T(8,128)(2,1)S(1)}, bf16[4,2,48,768]{3,2,1,0:T(8,128)(2,1)S(1)}, u32[]{:S(2)}, u32[]{:S(2)}) collective-permute-start(bf16[4,2,48,768]{3,2,1,0:T(8,128)(2,1)S(1)} %pad_maximum_fusion.2.refs_2_), channel_id=1, source_target_pairs={{0,2},{2,0},{4,6},{6,4},{8,10},{10,8},{12,14},{14,12},{16,18},{18,... | collective-permute-start | bytes 1769480 | tf_op jit(solution)/shard_map/ppermute | solution.py:58
  87.7 19.4 %collective-permute-start.14 = (bf16[4,2,48,768]{3,2,1,0:T(8,128)(2,1)}, bf16[4,2,48,768]{3,2,1,0:T(8,128)(2,1)S(1)}, u32[]{:S(2)}, u32[]{:S(2)}) collective-permute-start(bf16[4,2,48,768]{3,2,1,0:T(8,128)(2,1)} %pad_maximum_fusion.3.refs_8_), channel_id=1, source_target_pairs={{0,4},{2,6},{4,0},{6,2},{8,12},{10,14},{12,8},{14,10},{16,20},{18,... | collective-permute-start | bytes 1769480 | tf_op jit(solution)/shard_map/ppermute | solution.py:58
  89.2 37.0 %collective-permute-start.2 = (bf16[1,2,384,768]{3,2,1,0:T(8,128)(2,1)S(1)}, bf16[1,2,384,768]{3,2,1,0:T(8,128)(2,1)S(1)}, u32[]{:S(2)}, u32[]{:S(2)}) collective-permute-start(bf16[1,2,384,768]{3,2,1,0:T(8,128)(2,1)S(1)} %bitcast.40), channel_id=1, source_target_pairs={{0,2},{2,0},{4,6},{6,4},{8,10},{10,8},{12,14},{14,12},{16,18},{18,... | collective-permute-start | bytes 3538952 | tf_op jit(solution)/shard_map/ppermute | solution.py:58
  89.4 60.0 %collective-permute-start.10 = (bf16[1,2,384,768]{3,2,1,0:T(8,128)(2,1)}, bf16[1,2,384,768]{3,2,1,0:T(8,128)(2,1)}, u32[]{:S(2)}, u32[]{:S(2)}) collective-permute-start(bf16[1,2,384,768]{3,2,1,0:T(8,128)(2,1)} %bitcast.9.refs_6_), channel_id=1, source_target_pairs={{0,2},{2,0},{4,6},{6,4},{8,10},{10,8},{12,14},{14,12},{16,18},{18,... | collective-permute-start | bytes 3538952 | tf_op jit(solution)/shard_map/ppermute | solution.py:58
  97.8 11.0 %collective-permute-start.8 = (bf16[4,2,48,768]{3,2,1,0:T(8,128)(2,1)S(1)}, bf16[4,2,48,768]{3,2,1,0:T(8,128)(2,1)S(1)}, u32[]{:S(2)}, u32[]{:S(2)}) collective-permute-start(bf16[4,2,48,768]{3,2,1,0:T(8,128)(2,1)S(1)} %collective-permute-done.6.refs_3_), channel_id=1, source_target_pairs={{0,2},{2,0},{4,6},{6,4},{8,10},{10,8},{12,14},{14,12},{16,18},{18,... | collective-permute-start | bytes 1769480 | tf_op jit(solution)/shard_map/ppermute | solution.py:58
  98.8 50.6 %collective-permute-start.15 = (bf16[4,2,48,768]{3,2,1,0:T(8,128)(2,1)}, bf16[4,2,48,768]{3,2,1,0:T(8,128)(2,1)}, u32[]{:S(2)}, u32[]{:S(2)}) collective-permute-start(bf16[4,2,48,768]{3,2,1,0:T(8,128)(2,1)} %pad_maximum_fusion.3.refs_8_), channel_id=1, source_target_pairs={{0,2},{2,0},{4,6},{6,4},{8,10},{10,8},{12,14},{14,12},{16,18},{18,... | collective-permute-start | bytes 1769480 | tf_op jit(solution)/shard_map/ppermute | solution.py:58
  107.1 42.3 %collective-permute-start.16 = (bf16[4,2,48,768]{3,2,1,0:T(8,128)(2,1)S(1)}, bf16[4,2,48,768]{3,2,1,0:T(8,128)(2,1)}, u32[]{:S(2)}, u32[]{:S(2)}) collective-permute-start(bf16[4,2,48,768]{3,2,1,0:T(8,128)(2,1)S(1)} %collective-permute-done.14.refs_9_), channel_id=1, source_target_pairs={{0,2},{2,0},{4,6},{6,4},{8,10},{10,8},{12,14},{14,12},{16,18},{18,... | collective-permute-start | bytes 1769480 | tf_op jit(solution)/shard_map/ppermute | solution.py:58
  108.8 73.0 %collective-permute-start.41 = (bf16[1,8,48,768]{3,2,1,0:T(8,128)(2,1)}, bf16[1,8,48,768]{3,2,1,0:T(8,128)(2,1)S(1)}, u32[]{:S(2)}, u32[]{:S(2)}) collective-permute-start(bf16[1,8,48,768]{3,2,1,0:T(8,128)(2,1)} %convert_bitcast_fusion), channel_id=1, source_target_pairs={{0,16},{2,18},{4,20},{6,22},{8,24},{10,26},{12,28},{14,30},{16,0},... | collective-permute-start | bytes 1769480 | tf_op jit(solution)/shard_map/ppermute | solution.py:58
  181.3 44.0 %collective-permute-start.35 = (bf16[16,2,48,768]{3,2,1,0:T(8,128)(2,1)}, bf16[16,2,48,768]{3,2,1,0:T(8,128)(2,1)}, u32[]{:S(2)}, u32[]{:S(2)}) collective-permute-start(bf16[16,2,48,768]{3,2,1,0:T(8,128)(2,1)} %get-tuple-element.75), channel_id=1, source_target_pairs={{0,2},{2,0},{4,6},{6,4},{8,10},{10,8},{12,14},{14,12},{16,18},{18,... | collective-permute-start | bytes 7077896 | tf_op jit(solution)/shard_map/ppermute | solution.py:58
  181.5 47.1 %collective-permute-start.29 = (bf16[16,2,48,768]{3,2,1,0:T(8,128)(2,1)}, bf16[16,2,48,768]{3,2,1,0:T(8,128)(2,1)}, u32[]{:S(2)}, u32[]{:S(2)}) collective-permute-start(bf16[16,2,48,768]{3,2,1,0:T(8,128)(2,1)} %get-tuple-element.73), channel_id=1, source_target_pairs={{0,2},{2,0},{4,6},{6,4},{8,10},{10,8},{12,14},{14,12},{16,18},{18,... | collective-permute-start | bytes 7077896 | tf_op jit(solution)/shard_map/ppermute | solution.py:58
  184.2 37.1 %collective-permute-start.42 = (bf16[2,8,48,768]{3,2,1,0:T(8,128)(2,1)}, bf16[2,8,48,768]{3,2,1,0:T(8,128)(2,1)}, u32[]{:S(2)}, u32[]{:S(2)}) collective-permute-start(bf16[2,8,48,768]{3,2,1,0:T(8,128)(2,1)} %pad_maximum_fusion.1), channel_id=1, source_target_pairs={{0,4},{2,6},{4,0},{6,2},{8,12},{10,14},{12,8},{14,10},{16,20},{18,... | collective-permute-start | bytes 3538952 | tf_op jit(solution)/shard_map/ppermute | solution.py:58
  223.2 53.7 %collective-permute-start.43 = (bf16[4,8,48,768]{3,2,1,0:T(8,128)(2,1)S(1)}, bf16[4,8,48,768]{3,2,1,0:T(8,128)(2,1)S(1)}, u32[]{:S(2)}, u32[]{:S(2)}) collective-permute-start(bf16[4,8,48,768]{3,2,1,0:T(8,128)(2,1)S(1)} %pad_maximum_fusion.refs_2_.refs_1_.refs_8_), channel_id=1, source_target_pairs={{0,8},{2,10},{4,12},{6,14},{8,0},{10,2},{12,4},{14,6},{16,24},{18,... | collective-permute-start | bytes 7077896 | tf_op jit(solution)/shard_map/ppermute | solution.py:58
  224.3 7.6 %collective-permute-start.17 = (bf16[16,1,48,768]{3,2,1,0:T(8,128)(2,1)S(1)}, bf16[16,1,48,768]{3,2,1,0:T(8,128)(2,1)S(1)}, u32[]{:S(2)}, u32[]{:S(2)}) collective-permute-start(bf16[16,1,48,768]{3,2,1,0:T(8,128)(2,1)S(1)} %copy-done.47), channel_id=1, source_target_pairs={{0,2},{2,0},{4,6},{6,4},{8,10},{10,8},{12,14},{14,12},{16,18},{18,... | collective-permute-start | bytes 3538952 | tf_op jit(solution)/shard_map/ppermute | solution.py:58
  224.6 16.3 %collective-permute-start.24 = (bf16[8,1,48,768]{3,2,1,0:T(8,128)(2,1)S(1)}, bf16[8,1,48,768]{3,2,1,0:T(8,128)(2,1)S(1)}, u32[]{:S(2)}, u32[]{:S(2)}) collective-permute-start(bf16[8,1,48,768]{3,2,1,0:T(8,128)(2,1)S(1)} %add_convert_fusion.4), channel_id=1, source_target_pairs={{0,4},{2,6},{4,0},{6,2},{8,12},{10,14},{12,8},{14,10},{16,20},{18,... | collective-permute-start | bytes 1769480 | tf_op jit(solution)/shard_map/ppermute | solution.py:58
  226.9 50.5 %collective-permute-start.36 = (bf16[8,2,48,768]{3,2,1,0:T(8,128)(2,1)S(1)}, bf16[8,2,48,768]{3,2,1,0:T(8,128)(2,1)S(1)}, u32[]{:S(2)}, u32[]{:S(2)}) collective-permute-start(bf16[8,2,48,768]{3,2,1,0:T(8,128)(2,1)S(1)} %add_convert_fusion), channel_id=1, source_target_pairs={{0,1},{1,0},{2,3},{3,2},{4,5},{5,4},{6,7},{7,6},{8,9},{9,8},{10,11... | collective-permute-start | bytes 3538952 | tf_op jit(solution)/shard_map/ppermute | solution.py:58
  230.3 48.7 %collective-permute-start.30 = (bf16[8,2,48,768]{3,2,1,0:T(8,128)(2,1)S(1)}, bf16[8,2,48,768]{3,2,1,0:T(8,128)(2,1)S(1)}, u32[]{:S(2)}, u32[]{:S(2)}) collective-permute-start(bf16[8,2,48,768]{3,2,1,0:T(8,128)(2,1)S(1)} %add_convert_fusion.1), channel_id=1, source_target_pairs={{0,4},{2,6},{4,0},{6,2},{8,12},{10,14},{12,8},{14,10},{16,20},{18,... | collective-permute-start | bytes 3538952 | tf_op jit(solution)/shard_map/ppermute | solution.py:58
  232.0 35.5 %collective-permute-start.18 = (bf16[8,1,48,768]{3,2,1,0:T(8,128)(2,1)S(1)}, bf16[8,1,48,768]{3,2,1,0:T(8,128)(2,1)S(1)}, u32[]{:S(2)}, u32[]{:S(2)}) collective-permute-start(bf16[8,1,48,768]{3,2,1,0:T(8,128)(2,1)S(1)} %add_convert_fusion.5), channel_id=1, source_target_pairs={{0,1},{1,0},{2,3},{3,2},{4,5},{5,4},{6,7},{7,6},{8,9},{9,8},{10,11... | collective-permute-start | bytes 1769480 | tf_op jit(solution)/shard_map/ppermute | solution.py:58
  240.9 101.0 %collective-permute-start.44 = (bf16[4,8,48,768]{3,2,1,0:T(8,128)(2,1)S(1)}, bf16[4,8,48,768]{3,2,1,0:T(8,128)(2,1)S(1)}, u32[]{:S(2)}, u32[]{:S(2)}) collective-permute-start(bf16[4,8,48,768]{3,2,1,0:T(8,128)(2,1)S(1)} %pad_maximum_fusion.refs_2_.refs_1_.refs_8_), channel_id=1, source_target_pairs={{0,2},{2,0},{4,6},{6,4},{8,10},{10,8},{12,14},{14,12},{16,18},{18,... | collective-permute-start | bytes 7077896 | tf_op jit(solution)/shard_map/ppermute | solution.py:58
  267.5 14.1 %collective-permute-start.25 = (bf16[4,1,48,768]{3,2,1,0:T(8,128)(2,1)S(1)}, bf16[4,1,48,768]{3,2,1,0:T(8,128)(2,1)S(1)}, u32[]{:S(2)}, u32[]{:S(2)}) collective-permute-start(bf16[4,1,48,768]{3,2,1,0:T(8,128)(2,1)S(1)} %add_convert_fusion.8), channel_id=1, source_target_pairs={{0,1},{1,0},{2,3},{3,2},{4,5},{5,4},{6,7},{7,6},{8,9},{9,8},{10,11... | collective-permute-start | bytes 884744 | tf_op jit(solution)/shard_map/ppermute | solution.py:58
  276.9 9.9 %collective-permute-start.19 = (bf16[4,1,48,768]{3,2,1,0:T(8,128)(2,1)S(1)}, bf16[4,1,48,768]{3,2,1,0:T(8,128)(2,1)S(1)}, u32[]{:S(2)}, u32[]{:S(2)}) collective-permute-start(bf16[4,1,48,768]{3,2,1,0:T(8,128)(2,1)S(1)} %add_convert_fusion.9), channel_id=1, source_target_pairs={{0,4},{2,6},{4,0},{6,2},{8,12},{10,14},{12,8},{14,10},{16,20},{18,... | collective-permute-start | bytes 884744 | tf_op jit(solution)/shard_map/ppermute | solution.py:58
  277.4 64.5 %collective-permute-start.45 = (bf16[4,8,48,768]{3,2,1,0:T(8,128)(2,1)S(1)}, bf16[4,8,48,768]{3,2,1,0:T(8,128)(2,1)S(1)}, u32[]{:S(2)}, u32[]{:S(2)}) collective-permute-start(bf16[4,8,48,768]{3,2,1,0:T(8,128)(2,1)S(1)} %collective-permute-done.43.refs_3_.refs_2_.refs_9_), channel_id=1, source_target_pairs={{0,2},{2,0},{4,6},{6,4},{8,10},{10,8},{12,14},{14,12},{16,18},{18,... | collective-permute-start | bytes 7077896 | tf_op jit(solution)/shard_map/ppermute | solution.py:58
  279.0 19.0 %collective-permute-start.37 = (bf16[4,2,48,768]{3,2,1,0:T(8,128)(2,1)S(1)}, bf16[4,2,48,768]{3,2,1,0:T(8,128)(2,1)S(1)}, u32[]{:S(2)}, u32[]{:S(2)}) collective-permute-start(bf16[4,2,48,768]{3,2,1,0:T(8,128)(2,1)S(1)} %add_convert_fusion.2), channel_id=1, source_target_pairs={{0,4},{2,6},{4,0},{6,2},{8,12},{10,14},{12,8},{14,10},{16,20},{18,... | collective-permute-start | bytes 1769480 | tf_op jit(solution)/shard_map/ppermute | solution.py:58
  281.6 18.6 %collective-permute-start.31 = (bf16[4,2,48,768]{3,2,1,0:T(8,128)(2,1)S(1)}, bf16[4,2,48,768]{3,2,1,0:T(8,128)(2,1)S(1)}, u32[]{:S(2)}, u32[]{:S(2)}) collective-permute-start(bf16[4,2,48,768]{3,2,1,0:T(8,128)(2,1)S(1)} %add_convert_fusion.3), channel_id=1, source_target_pairs={{0,1},{1,0},{2,3},{3,2},{4,5},{5,4},{6,7},{7,6},{8,9},{9,8},{10,11... | collective-permute-start | bytes 1769480 | tf_op jit(solution)/shard_map/ppermute | solution.py:58
  286.8 15.6 %collective-permute-start.26 = (bf16[2,1,48,768]{3,2,1,0:T(8,128)(2,1)S(1)}, bf16[2,1,48,768]{3,2,1,0:T(8,128)(2,1)S(1)}, u32[]{:S(2)}, u32[]{:S(2)}) collective-permute-start(bf16[2,1,48,768]{3,2,1,0:T(8,128)(2,1)S(1)} %add_convert_fusion.14), channel_id=1, source_target_pairs={{0,8},{2,10},{4,12},{6,14},{8,0},{10,2},{12,4},{14,6},{16,24},{18,... | collective-permute-start | bytes 442376 | tf_op jit(solution)/shard_map/ppermute | solution.py:58
  298.1 37.7 %collective-permute-start.20 = (bf16[2,1,48,768]{3,2,1,0:T(8,128)(2,1)S(1)}, bf16[2,1,48,768]{3,2,1,0:T(8,128)(2,1)S(1)}, u32[]{:S(2)}, u32[]{:S(2)}) collective-permute-start(bf16[2,1,48,768]{3,2,1,0:T(8,128)(2,1)S(1)} %add_convert_fusion.15), channel_id=1, source_target_pairs={{0,8},{2,10},{4,12},{6,14},{8,0},{10,2},{12,4},{14,6},{16,24},{18,... | collective-permute-start | bytes 442376 | tf_op jit(solution)/shard_map/ppermute | solution.py:58
  300.2 10.9 %collective-permute-start.38 = (bf16[2,2,48,768]{3,2,1,0:T(8,128)(2,1)S(1)}, bf16[2,2,48,768]{3,2,1,0:T(8,128)(2,1)S(1)}, u32[]{:S(2)}, u32[]{:S(2)}) collective-permute-start(bf16[2,2,48,768]{3,2,1,0:T(8,128)(2,1)S(1)} %add_convert_fusion.6), channel_id=1, source_target_pairs={{0,8},{2,10},{4,12},{6,14},{8,0},{10,2},{12,4},{14,6},{16,24},{18,... | collective-permute-start | bytes 884744 | tf_op jit(solution)/shard_map/ppermute | solution.py:58
  302.4 14.7 %collective-permute-start.32 = (bf16[2,2,48,768]{3,2,1,0:T(8,128)(2,1)S(1)}, bf16[2,2,48,768]{3,2,1,0:T(8,128)(2,1)S(1)}, u32[]{:S(2)}, u32[]{:S(2)}) collective-permute-start(bf16[2,2,48,768]{3,2,1,0:T(8,128)(2,1)S(1)} %add_convert_fusion.7), channel_id=1, source_target_pairs={{0,8},{2,10},{4,12},{6,14},{8,0},{10,2},{12,4},{14,6},{16,24},{18,... | collective-permute-start | bytes 884744 | tf_op jit(solution)/shard_map/ppermute | solution.py:58
  311.1 44.3 %collective-permute-start.27 = (bf16[1,1,48,768]{3,2,1,0:T(8,128)(2,1)}, bf16[1,1,48,768]{3,2,1,0:T(8,128)(2,1)}, u32[]{:S(2)}, u32[]{:S(2)}) collective-permute-start(bf16[1,1,48,768]{3,2,1,0:T(8,128)(2,1)} %add_convert_fusion.18), channel_id=1, source_target_pairs={{0,16},{2,18},{4,20},{6,22},{8,24},{10,26},{12,28},{14,30},{16,0},... | collective-permute-start | bytes 221192 | tf_op jit(solution)/shard_map/ppermute | solution.py:58
  317.1 9.4 %collective-permute-start.39 = (bf16[1,2,48,768]{3,2,1,0:T(8,128)(2,1)S(1)}, bf16[1,2,48,768]{3,2,1,0:T(8,128)(2,1)S(1)}, u32[]{:S(2)}, u32[]{:S(2)}) collective-permute-start(bf16[1,2,48,768]{3,2,1,0:T(8,128)(2,1)S(1)} %add_convert_fusion.12), channel_id=1, source_target_pairs={{0,16},{2,18},{4,20},{6,22},{8,24},{10,26},{12,28},{14,30},{16,0},... | collective-permute-start | bytes 442376 | tf_op jit(solution)/shard_map/ppermute | solution.py:58
  326.5 6.6 %collective-permute-start.33 = (bf16[1,2,48,768]{3,2,1,0:T(8,128)(2,1)S(1)}, bf16[1,2,48,768]{3,2,1,0:T(8,128)(2,1)S(1)}, u32[]{:S(2)}, u32[]{:S(2)}) collective-permute-start(bf16[1,2,48,768]{3,2,1,0:T(8,128)(2,1)S(1)} %add_convert_fusion.13), channel_id=1, source_target_pairs={{0,16},{2,18},{4,20},{6,22},{8,24},{10,26},{12,28},{14,30},{16,0},... | collective-permute-start | bytes 442376 | tf_op jit(solution)/shard_map/ppermute | solution.py:58
  338.3 18.7 %collective-permute-start.21 = (bf16[1,1,48,768]{3,2,1,0:T(8,128)(2,1)}, bf16[1,1,48,768]{3,2,1,0:T(8,128)(2,1)}, u32[]{:S(2)}, u32[]{:S(2)}) collective-permute-start(bf16[1,1,48,768]{3,2,1,0:T(8,128)(2,1)} %add_convert_fusion.19), channel_id=1, source_target_pairs={{0,16},{2,18},{4,20},{6,22},{8,24},{10,26},{12,28},{14,30},{16,0},... | collective-permute-start | bytes 221192 | tf_op jit(solution)/shard_map/ppermute | solution.py:58
  351.6 18.6 %all-to-all-start.1 = ((bf16[16,48,192]{2,1,0:T(8,128)(2,1)}), bf16[16,48,192]{2,1,0:T(8,128)(2,1)S(1)}, u32[]{:S(2)}, u32[]{:S(2)}) async-start(bf16[16,48,192]{2,1,0:T(8,128)(2,1)} %bitcast.49), calls=%async_computation.1 | async-start | bytes 786432 | tf_op jit(solution)/shard_map/all_to_all | solution.py:960
  370.3 18.1 %all-to-all-start = ((bf16[16,48,192]{2,1,0:T(8,128)(2,1)}), bf16[16,48,192]{2,1,0:T(8,128)(2,1)S(1)}, u32[]{:S(2)}, u32[]{:S(2)}) async-start(bf16[16,48,192]{2,1,0:T(8,128)(2,1)} %bitcast.50), calls=%async_computation | async-start | bytes 786432 | tf_op jit(solution)/shard_map/all_to_all | solution.py:960
  398.4 14.8 %collective-permute-start.46 = (bf16[1,2,48,768]{3,2,1,0:T(8,128)(2,1)S(1)}, bf16[1,2,48,768]{3,2,1,0:T(8,128)(2,1)S(1)}, u32[]{:S(2)}, u32[]{:S(2)}) collective-permute-start(bf16[1,2,48,768]{3,2,1,0:T(8,128)(2,1)S(1)} %get-tuple-element.98), channel_id=1, source_target_pairs={{0,16},{2,18},{4,20},{6,22},{8,24},{10,26},{12,28},{14,30},{16,0},... | collective-permute-start | bytes 442376 | tf_op jit(solution)/shard_map/ppermute | solution.py:58
  400.2 14.8 %collective-permute-start.56 = (bf16[1,2,48,768]{3,2,1,0:T(8,128)(2,1)S(1)}, bf16[1,2,48,768]{3,2,1,0:T(8,128)(2,1)S(1)}, u32[]{:S(2)}, u32[]{:S(2)}) collective-permute-start(bf16[1,2,48,768]{3,2,1,0:T(8,128)(2,1)S(1)} %get-tuple-element.96), channel_id=1, source_target_pairs={{0,16},{2,18},{4,20},{6,22},{8,24},{10,26},{12,28},{14,30},{16,0},... | collective-permute-start | bytes 442376 | tf_op jit(solution)/shard_map/ppermute | solution.py:58
  411.4 10.2 %collective-permute-start.51 = (bf16[1,2,48,768]{3,2,1,0:T(8,128)(2,1)S(1)}, bf16[1,2,48,768]{3,2,1,0:T(8,128)(2,1)S(1)}, u32[]{:S(2)}, u32[]{:S(2)}) collective-permute-start(bf16[1,2,48,768]{3,2,1,0:T(8,128)(2,1)S(1)} %get-tuple-element.97), channel_id=1, source_target_pairs={{0,16},{2,18},{4,20},{6,22},{8,24},{10,26},{12,28},{14,30},{16,0},... | collective-permute-start | bytes 442376 | tf_op jit(solution)/shard_map/ppermute | solution.py:58
  413.2 15.8 %collective-permute-start.47 = (bf16[2,2,48,768]{3,2,1,0:T(8,128)(2,1)S(1)}, bf16[2,2,48,768]{3,2,1,0:T(8,128)(2,1)S(1)}, u32[]{:S(2)}, u32[]{:S(2)}) collective-permute-start(bf16[2,2,48,768]{3,2,1,0:T(8,128)(2,1)S(1)} %pad_maximum_fusion.12), channel_id=1, source_target_pairs={{0,8},{2,10},{4,12},{6,14},{8,0},{10,2},{12,4},{14,6},{16,24},{18,... | collective-permute-start | bytes 884744 | tf_op jit(solution)/shard_map/ppermute | solution.py:58
  415.0 18.7 %collective-permute-start.57 = (bf16[2,2,48,768]{3,2,1,0:T(8,128)(2,1)S(1)}, bf16[2,2,48,768]{3,2,1,0:T(8,128)(2,1)S(1)}, u32[]{:S(2)}, u32[]{:S(2)}) collective-permute-start(bf16[2,2,48,768]{3,2,1,0:T(8,128)(2,1)S(1)} %pad_maximum_fusion.14), channel_id=1, source_target_pairs={{0,8},{2,10},{4,12},{6,14},{8,0},{10,2},{12,4},{14,6},{16,24},{18,... | collective-permute-start | bytes 884744 | tf_op jit(solution)/shard_map/ppermute | solution.py:58
  415.4 20.5 %collective-permute-start.66 = (f32[8,768]{1,0:T(8,128)S(1)}, f32[8,768]{1,0:T(8,128)S(1)}, u32[]{:S(2)}, u32[]{:S(2)}) collective-permute-start(f32[8,768]{1,0:T(8,128)S(1)} %pad_maximum_fusion.18), channel_id=1, source_target_pairs={{0,1},{1,0},{2,3},{3,2},{4,5},{5,4},{6,7},{7,6},{8,9},{9,8},{10,11... | collective-permute-start | bytes 73736 | tf_op jit(solution)/shard_map/ppermute | solution.py:58
  417.0 17.7 %collective-permute-start.61 = (bf16[1,2,48,768]{3,2,1,0:T(8,128)(2,1)S(1)}, bf16[1,2,48,768]{3,2,1,0:T(8,128)(2,1)S(1)}, u32[]{:S(2)}, u32[]{:S(2)}) collective-permute-start(bf16[1,2,48,768]{3,2,1,0:T(8,128)(2,1)S(1)} %get-tuple-element.95), channel_id=1, source_target_pairs={{0,16},{2,18},{4,20},{6,22},{8,24},{10,26},{12,28},{14,30},{16,0},... | collective-permute-start | bytes 442376 | tf_op jit(solution)/shard_map/ppermute | solution.py:58
  421.6 40.3 %collective-permute-start.52 = (bf16[2,2,48,768]{3,2,1,0:T(8,128)(2,1)S(1)}, bf16[2,2,48,768]{3,2,1,0:T(8,128)(2,1)S(1)}, u32[]{:S(2)}, u32[]{:S(2)}) collective-permute-start(bf16[2,2,48,768]{3,2,1,0:T(8,128)(2,1)S(1)} %pad_maximum_fusion.13), channel_id=1, source_target_pairs={{0,4},{2,6},{4,0},{6,2},{8,12},{10,14},{12,8},{14,10},{16,20},{18,... | collective-permute-start | bytes 884744 | tf_op jit(solution)/shard_map/ppermute | solution.py:58
  429.0 35.2 %collective-permute-start.48 = (bf16[4,2,48,768]{3,2,1,0:T(8,128)(2,1)S(1)}, bf16[4,2,48,768]{3,2,1,0:T(8,128)(2,1)}, u32[]{:S(2)}, u32[]{:S(2)}) collective-permute-start(bf16[4,2,48,768]{3,2,1,0:T(8,128)(2,1)S(1)} %pad_maximum_fusion.5.refs_0_), channel_id=1, source_target_pairs={{0,4},{2,6},{4,0},{6,2},{8,12},{10,14},{12,8},{14,10},{16,20},{18,... | collective-permute-start | bytes 1769480 | tf_op jit(solution)/shard_map/ppermute | solution.py:58
  433.7 31.1 %collective-permute-start.58 = (bf16[4,2,48,768]{3,2,1,0:T(8,128)(2,1)S(1)}, bf16[4,2,48,768]{3,2,1,0:T(8,128)(2,1)S(1)}, u32[]{:S(2)}, u32[]{:S(2)}) collective-permute-start(bf16[4,2,48,768]{3,2,1,0:T(8,128)(2,1)S(1)} %pad_maximum_fusion.7.refs_0_), channel_id=1, source_target_pairs={{0,4},{2,6},{4,0},{6,2},{8,12},{10,14},{12,8},{14,10},{16,20},{18,... | collective-permute-start | bytes 1769480 | tf_op jit(solution)/shard_map/ppermute | solution.py:58
  434.7 27.4 %collective-permute-start.62 = (bf16[2,2,48,768]{3,2,1,0:T(8,128)(2,1)S(1)}, bf16[2,2,48,768]{3,2,1,0:T(8,128)(2,1)S(1)}, u32[]{:S(2)}, u32[]{:S(2)}) collective-permute-start(bf16[2,2,48,768]{3,2,1,0:T(8,128)(2,1)S(1)} %pad_maximum_fusion.15), channel_id=1, source_target_pairs={{0,4},{2,6},{4,0},{6,2},{8,12},{10,14},{12,8},{14,10},{16,20},{18,... | collective-permute-start | bytes 884744 | tf_op jit(solution)/shard_map/ppermute | solution.py:58
  444.6 17.2 %collective-permute-start.69 = (f32[8,768]{1,0:T(8,128)S(1)}, f32[8,768]{1,0:T(8,128)S(1)}, u32[]{:S(2)}, u32[]{:S(2)}) collective-permute-start(f32[8,768]{1,0:T(8,128)S(1)} %add.447), channel_id=1, source_target_pairs={{0,4},{2,6},{4,0},{6,2},{8,12},{10,14},{12,8},{14,10},{16,20},{18,... | collective-permute-start | bytes 73736 | tf_op jit(solution)/shard_map/ppermute | solution.py:58
  462.0 16.4 %collective-permute-start.53 = (bf16[4,2,48,768]{3,2,1,0:T(8,128)(2,1)S(1)}, bf16[4,2,48,768]{3,2,1,0:T(8,128)(2,1)}, u32[]{:S(2)}, u32[]{:S(2)}) collective-permute-start(bf16[4,2,48,768]{3,2,1,0:T(8,128)(2,1)S(1)} %pad_maximum_fusion.6.refs_4_), channel_id=1, source_target_pairs={{0,8},{2,10},{4,12},{6,14},{8,0},{10,2},{12,4},{14,6},{16,24},{18,... | collective-permute-start | bytes 1769480 | tf_op jit(solution)/shard_map/ppermute | solution.py:58
  462.2 28.3 %collective-permute-start.63 = (bf16[4,2,48,768]{3,2,1,0:T(8,128)(2,1)S(1)}, bf16[4,2,48,768]{3,2,1,0:T(8,128)(2,1)S(1)}, u32[]{:S(2)}, u32[]{:S(2)}) collective-permute-start(bf16[4,2,48,768]{3,2,1,0:T(8,128)(2,1)S(1)} %pad_maximum_fusion.8.refs_4_), channel_id=1, source_target_pairs={{0,8},{2,10},{4,12},{6,14},{8,0},{10,2},{12,4},{14,6},{16,24},{18,... | collective-permute-start | bytes 1769480 | tf_op jit(solution)/shard_map/ppermute | solution.py:58
  464.3 26.2 %collective-permute-start.59 = (bf16[4,2,48,768]{3,2,1,0:T(8,128)(2,1)S(1)}, bf16[4,2,48,768]{3,2,1,0:T(8,128)(2,1)S(1)}, u32[]{:S(2)}, u32[]{:S(2)}) collective-permute-start(bf16[4,2,48,768]{3,2,1,0:T(8,128)(2,1)S(1)} %pad_maximum_fusion.7.refs_0_), channel_id=1, source_target_pairs={{0,2},{2,0},{4,6},{6,4},{8,10},{10,8},{12,14},{14,12},{16,18},{18,... | collective-permute-start | bytes 1769480 | tf_op jit(solution)/shard_map/ppermute | solution.py:58
  464.3 26.7 %collective-permute-start.64 = (bf16[4,2,48,768]{3,2,1,0:T(8,128)(2,1)S(1)}, bf16[4,2,48,768]{3,2,1,0:T(8,128)(2,1)S(1)}, u32[]{:S(2)}, u32[]{:S(2)}) collective-permute-start(bf16[4,2,48,768]{3,2,1,0:T(8,128)(2,1)S(1)} %pad_maximum_fusion.8.refs_4_), channel_id=1, source_target_pairs={{0,2},{2,0},{4,6},{6,4},{8,10},{10,8},{12,14},{14,12},{16,18},{18,... | collective-permute-start | bytes 1769480 | tf_op jit(solution)/shard_map/ppermute | solution.py:58
  464.8 26.3 %collective-permute-start.60 = (bf16[4,2,48,768]{3,2,1,0:T(8,128)(2,1)S(1)}, bf16[4,2,48,768]{3,2,1,0:T(8,128)(2,1)S(1)}, u32[]{:S(2)}, u32[]{:S(2)}) collective-permute-start(bf16[4,2,48,768]{3,2,1,0:T(8,128)(2,1)S(1)} %collective-permute-done.58.refs_1_), channel_id=1, source_target_pairs={{0,2},{2,0},{4,6},{6,4},{8,10},{10,8},{12,14},{14,12},{16,18},{18,... | collective-permute-start | bytes 1769480 | tf_op jit(solution)/shard_map/ppermute | solution.py:58
  478.4 28.0 %collective-permute-start.49 = (bf16[4,2,48,768]{3,2,1,0:T(8,128)(2,1)S(1)}, bf16[4,2,48,768]{3,2,1,0:T(8,128)(2,1)}, u32[]{:S(2)}, u32[]{:S(2)}) collective-permute-start(bf16[4,2,48,768]{3,2,1,0:T(8,128)(2,1)S(1)} %pad_maximum_fusion.5.refs_0_), channel_id=1, source_target_pairs={{0,2},{2,0},{4,6},{6,4},{8,10},{10,8},{12,14},{14,12},{16,18},{18,... | collective-permute-start | bytes 1769480 | tf_op jit(solution)/shard_map/ppermute | solution.py:58
  490.5 16.0 %collective-permute-start.54 = (bf16[4,2,48,768]{3,2,1,0:T(8,128)(2,1)S(1)}, bf16[4,2,48,768]{3,2,1,0:T(8,128)(2,1)}, u32[]{:S(2)}, u32[]{:S(2)}) collective-permute-start(bf16[4,2,48,768]{3,2,1,0:T(8,128)(2,1)S(1)} %pad_maximum_fusion.6.refs_4_), channel_id=1, source_target_pairs={{0,2},{2,0},{4,6},{6,4},{8,10},{10,8},{12,14},{14,12},{16,18},{18,... | collective-permute-start | bytes 1769480 | tf_op jit(solution)/shard_map/ppermute | solution.py:58
  491.0 15.5 %collective-permute-start.50 = (bf16[4,2,48,768]{3,2,1,0:T(8,128)(2,1)}, bf16[4,2,48,768]{3,2,1,0:T(8,128)(2,1)}, u32[]{:S(2)}, u32[]{:S(2)}) collective-permute-start(bf16[4,2,48,768]{3,2,1,0:T(8,128)(2,1)} %collective-permute-done.48.refs_1_), channel_id=1, source_target_pairs={{0,2},{2,0},{4,6},{6,4},{8,10},{10,8},{12,14},{14,12},{16,18},{18,... | collective-permute-start | bytes 1769480 | tf_op jit(solution)/shard_map/ppermute | solution.py:58
  492.6 13.8 %collective-permute-start.55 = (bf16[4,2,48,768]{3,2,1,0:T(8,128)(2,1)}, bf16[4,2,48,768]{3,2,1,0:T(8,128)(2,1)}, u32[]{:S(2)}, u32[]{:S(2)}) collective-permute-start(bf16[4,2,48,768]{3,2,1,0:T(8,128)(2,1)} %collective-permute-done.53.refs_5_), channel_id=1, source_target_pairs={{0,2},{2,0},{4,6},{6,4},{8,10},{10,8},{12,14},{14,12},{16,18},{18,... | collective-permute-start | bytes 1769480 | tf_op jit(solution)/shard_map/ppermute | solution.py:58
  (57 other events, 851.1 us)
where the time goes:
time: 528 us; the launch traced here: 520 us
  waiting for transfers between devices  230 us (44%)
  Pallas kernels  162 us (31%)
  starting transfers between devices  71.3 us (14%)
  other arithmetic  42.1 us (8%)
  local copies, waits for them, and re-layouts  13.5 us (3%)
    ppermute x71, waiting for transfers between devices, xor_permute(): return lax.ppermute(x, axis, [(i, i ^ mask) for i in range(size)])  226 us
    ppermute x71, starting transfers between devices, xor_permute(): return lax.ppermute(x, axis, [(i, i ^ mask) for i in range(size)])  61.6 us
    pallas_call x1, Pallas kernels, run_ffn(): pl.pallas_call(partial(ffn_kernel, group_shapes(groups), plans, nwide), n...  31.9 us
    pallas_call x2, Pallas kernels, run_update(): pl.pallas_call(partial(update_kernel, group_shapes(groups), half, bool(ea...  26.2 us
    pallas_call x1, Pallas kernels, run_forward(): pl.pallas_call(partial(forward_kernel, group_shapes(first)), name='forwar...  22.1 us
    pallas_call x1, Pallas kernels, run_attention_back(): pl.pallas_call(attention_back_kernel, name='attention_back', out_shape=(s...  20 us
    pallas_call x2, Pallas kernels, run_adam(): pl.pallas_call(partial(adam_kernel, count, bool(earlier)), name='adam_ste...  15.7 us
    pallas_call x2, Pallas kernels, run_turn(): pl.pallas_call(partial(turn_kernel, count, sizes, group_shapes([left])),...  13.7 us
  transfers between devices with their start and end apart: 73, of which 29 were waited for; matrix products, arithmetic and copies ran while one was open for 9% of the time, Pallas kernels for 26%

commit v1 on v0

--- a/solution.py
+++ b/solution.py
@@ -908,9 +908,8 @@
     vec_rel = jnp.stack(narrow_parts(vectors.astype(BF), nnarrow))
     vec_all = vec_rel[n ^ jnp.arange(nnarrow, dtype=jnp.int32)].reshape(8, D).astype(F32)
 
-    left = wide_group(
-        basis_left.transpose(0, 2, 1).astype(BF), nwide, left_order, len(left_order) - 2
-    )
+    left = basis_left.transpose(0, 2, 1).astype(BF)
+    left = wide_group(left, nwide, left_order, len(left_order) - 2)
 
     cos, sin = rotary_tables()
     tok = tokens[0]

time: 528 us -> 528 us (level)
  no operation moved by 1% of the time
where the time goes in v1:
time: 528 us; the launch traced here: 520 us
  waiting for transfers between devices  230 us (44%)
  Pallas kernels  162 us (31%)
  starting transfers between devices  71.3 us (14%)
  other arithmetic  42.1 us (8%)
  local copies, waits for them, and re-layouts  13.5 us (3%)
    ppermute x71, waiting for transfers between devices, xor_permute(): return lax.ppermute(x, axis, [(i, i ^ mask) for i in range(size)])  226 us
    ppermute x71, starting transfers between devices, xor_permute(): return lax.ppermute(x, axis, [(i, i ^ mask) for i in range(size)])  61.6 us
    pallas_call x1, Pallas kernels, run_ffn(): pl.pallas_call(partial(ffn_kernel, group_shapes(groups), plans, nwide), n...  31.9 us
    pallas_call x2, Pallas kernels, run_update(): pl.pallas_call(partial(update_kernel, group_shapes(groups), half, bool(ea...  26.2 us
    pallas_call x1, Pallas kernels, run_forward(): pl.pallas_call(partial(forward_kernel, group_shapes(first)), name='forwar...  22.1 us
    pallas_call x1, Pallas kernels, run_attention_back(): pl.pallas_call(attention_back_kernel, name='attention_back', out_shape=(s...  20 us
    pallas_call x2, Pallas kernels, run_adam(): pl.pallas_call(partial(adam_kernel, count, bool(earlier)), name='adam_ste...  15.7 us
    pallas_call x2, Pallas kernels, run_turn(): pl.pallas_call(partial(turn_kernel, count, sizes, group_shapes([left])),...  13.7 us
  transfers between devices with their start and end apart: 73, of which 29 were waited for; matrix products, arithmetic and copies ran while one was open for 9% of the time, Pallas kernels for 26%

profile of v1, /device:TPU:0, one launch (start us, length us, event | category | flops | bytes accessed | tf_op | source)
XLA Modules:
  0.0 520.1 jit_solution(12247789775987154428)
XLA Ops:
  3.6 3.4 send_weights.2
  7.0 3.0 collective-permute-start.3
  10.0 1.9 collective-permute-start.1
  12.0 3.3 send_weights.3
  15.3 1.9 collective-permute-start.11
  17.4 2.7 collective-permute-start.4
  20.1 47.8 %collective-permute-done.11 = bf16[2,48,768]{2,1,0:T(8,128)(2,1)S(1)} collective-permute-done((bf16[2,48,768]{2,1,0:T(8,128)(2,1)}, bf16[2,48,768]{2,1,0:T(8,128)(2,1)S(1)}, u32[]{:S(2)}, u32[]{:S(2)}) %collective-permute-start.11) | collective-permute-done | bytes 147488 | tf_op jit(solution)/shard_map/ppermute | solution.py:58
  67.9 2.8 collective-permute-start.12
  70.7 1.6 collective-permute-start.5
  72.4 4.5 collective-permute-done.12
  77.7 4.4 collective-permute-done.5
  84.5 2.3 collective-permute-done.13
  89.7 8.1 %collective-permute-done.6.refs_3_ = bf16[4,2,48,768]{3,2,1,0:T(8,128)(2,1)S(1)} collective-permute-done((bf16[4,2,48,768]{3,2,1,0:T(8,128)(2,1)S(1)}, bf16[4,2,48,768]{3,2,1,0:T(8,128)(2,1)S(1)}, u32[]{:S(2)}, u32[]{:S(2)}) %collective-permute-start.6) | collective-permute-done | bytes 589856 | tf_op jit(solution)/shard_map/ppermute | solution.py:58
  99.3 7.8 %collective-permute-done.14.refs_9_ = bf16[4,2,48,768]{3,2,1,0:T(8,128)(2,1)S(1)} collective-permute-done((bf16[4,2,48,768]{3,2,1,0:T(8,128)(2,1)}, bf16[4,2,48,768]{3,2,1,0:T(8,128)(2,1)S(1)}, u32[]{:S(2)}, u32[]{:S(2)}) %collective-permute-start.14) | collective-permute-done | bytes 589856 | tf_op jit(solution)/shard_map/ppermute | solution.py:58
  111.5 9.8 %convert_element_type.501.own = bf16[8,768,768]{2,1,0:T(8,128)(2,1)} convert(f32[8,768,768]{2,1,0:T(8,128)} %weights.3) | non-fusion elementwise | flops 4718592 | bytes 28311552 | tf_op jit(solution)/shard_map/convert_element_type | solution.py:897
  127.2 22.1 %forward_attention.1 = (bf16[768,768]{1,0:T(8,128)(2,1)}, bf16[768,768]{1,0:T(8,128)(2,1)}, bf16[768,768]{1,0:T(8,128)(2,1)}, bf16[768,768]{1,0:T(8,128)(2,1)}, ...) custom-call(s32[26]{0:T(128)} %pad_add_fusion.meta, ...), custom_call_target="tpu_custom_call" | custom-call | tf_op jit(solution)/shard_map/forward_attention/pallas_call | solution.py:309
  149.4 31.9 %feed_forward.1 = (bf16[768,768]{1,0:T(8,128)(2,1)}, bf16[16,2,48,768]{3,2,1,0:T(8,128)(2,1)}, bf16[16,2,48,768]{3,2,1,0:T(8,128)(2,1)}, bf16[16,2,48,768]{3,2,1...) custom-call(s32[26]{0:T(128)} %pad_add_fusion.meta, ...), custom_call_target="tpu_custom_call" | custom-call | tf_op jit(solution)/shard_map/feed_forward/pallas_call | solution.py:393
  181.8 2.4 pad_maximum_fusion.1
  185.8 8.7 %residual_back.1 = (f32[768,768]{1,0:T(8,128)}, bf16[768,768]{1,0:T(8,128)(2,1)}, bf16[768,768]{1,0:T(8,128)(2,1)}, f32[1,768]{1,0:T(1,128)}) custom-call(s32[26]{0:T(128)} %pad_add_fusion.meta, f32[768,768]{1,0:T(8,128)} %get-tuple-element.50.x2, f32[768,768]{1,0:T(8,128)} %get-tuple-element.54.dn2, bf16[768,768]{1,0:T(8,128)(2,1)} %bitcast.46, ...), custom_call_target="tpu_custom_call" | custom-call | tf_op jit(solution)/shard_map/residual_back/pallas_call | solution.py:454
  194.5 20.0 %attention_back.1 = (bf16[768,768]{1,0:T(8,128)(2,1)}, bf16[768,768]{1,0:T(8,128)(2,1)}, bf16[768,768]{1,0:T(8,128)(2,1)}) custom-call(bf16[768,768]{1,0:T(8,128)(2,1)} %get-tuple-element.57.q, bf16[768,768]{1,0:T(8,128)(2,1)} %get-tuple-element.58.k, bf16[768,768]{1,0:T(8,128)(2,1)} %get-tuple-element.59.v, bf16[768,768]{1,0:T(8,128)(2,1)} %get-tuple-element.60.do, ...), custom_call_target="tpu_custom_call" | custom-call | tf_op jit(solution)/shard_map/attention_back/pallas_call | solution.py:518
  214.5 6.8 %qkv_grad.1 = (bf16[16,1,48,768]{3,2,1,0:T(8,128)(2,1)}, bf16[16,1,48,768]{3,2,1,0:T(8,128)(2,1)}, bf16[16,1,48,768]{3,2,1,0:T(8,128)(2,1)}, bf16[16,1,48,768]{3,2,1,0:T(8,128)(2,1)}) custom-call(s32[26]{0:T(128)} %pad_add_fusion.meta, bf16[768,768]{1,0:T(8,128)(2,1)} %get-tuple-element.66.n1, bf16[768,768]{1,0:T(8,128)(2,1)} %get-tuple-element.62.pq, ...), custom_call_target="tpu_custom_call" | custom-call | tf_op jit(solution)/shard_map/qkv_grad/pallas_call | solution.py:544
  221.4 1.8 pad_maximum_fusion.refs_2_.refs_1_.refs_8_
  225.2 1.7 add_convert_fusion
  226.9 1.7 collective-permute-start.36
  228.6 1.7 add_convert_fusion.1
  230.3 1.6 collective-permute-start.30
  233.2 7.7 %collective-permute-done.24 = bf16[8,1,48,768]{3,2,1,0:T(8,128)(2,1)S(1)} collective-permute-done((bf16[8,1,48,768]{3,2,1,0:T(8,128)(2,1)S(1)}, bf16[8,1,48,768]{3,2,1,0:T(8,128)(2,1)S(1)}, u32[]{:S(2)}, u32[]{:S(2)}) %collective-permute-start.24) | collective-permute-done | bytes 589856 | tf_op jit(solution)/shard_map/ppermute | solution.py:58
  241.0 26.5 %collective-permute-done.18 = bf16[8,1,48,768]{3,2,1,0:T(8,128)(2,1)S(1)} collective-permute-done((bf16[8,1,48,768]{3,2,1,0:T(8,128)(2,1)S(1)}, bf16[8,1,48,768]{3,2,1,0:T(8,128)(2,1)S(1)}, u32[]{:S(2)}, u32[]{:S(2)}) %collective-permute-start.18) | collective-permute-done | bytes 589856 | tf_op jit(solution)/shard_map/ppermute | solution.py:58
  267.5 1.6 collective-permute-start.25
  269.3 7.7 %collective-permute-done.43.refs_3_.refs_2_.refs_9_ = bf16[4,8,48,768]{3,2,1,0:T(8,128)(2,1)S(1)} collective-permute-done((bf16[4,8,48,768]{3,2,1,0:T(8,128)(2,1)S(1)}, bf16[4,8,48,768]{3,2,1,0:T(8,128)(2,1)S(1)}, u32[]{:S(2)}, u32[]{:S(2)}) %collective-permute-start.43) | collective-permute-done | bytes 2359328 | tf_op jit(solution)/shard_map/ppermute | solution.py:58
  281.6 1.7 collective-permute-start.31
  283.4 3.4 collective-permute-done.19
  287.9 10.2 %collective-permute-done.37 = bf16[4,2,48,768]{3,2,1,0:T(8,128)(2,1)S(1)} collective-permute-done((bf16[4,2,48,768]{3,2,1,0:T(8,128)(2,1)S(1)}, bf16[4,2,48,768]{3,2,1,0:T(8,128)(2,1)S(1)}, u32[]{:S(2)}, u32[]{:S(2)}) %collective-permute-start.37) | collective-permute-done | bytes 589856 | tf_op jit(solution)/shard_map/ppermute | solution.py:58
  304.2 6.9 %collective-permute-done.38 = bf16[2,2,48,768]{3,2,1,0:T(8,128)(2,1)S(1)} collective-permute-done((bf16[2,2,48,768]{3,2,1,0:T(8,128)(2,1)S(1)}, bf16[2,2,48,768]{3,2,1,0:T(8,128)(2,1)S(1)}, u32[]{:S(2)}, u32[]{:S(2)}) %collective-permute-start.38) | collective-permute-done | bytes 294944 | tf_op jit(solution)/shard_map/ppermute | solution.py:58
  313.6 3.5 collective-permute-done.32
  318.8 7.8 %collective-permute-done.39 = bf16[1,2,48,768]{3,2,1,0:T(8,128)(2,1)S(1)} collective-permute-done((bf16[1,2,48,768]{3,2,1,0:T(8,128)(2,1)S(1)}, bf16[1,2,48,768]{3,2,1,0:T(8,128)(2,1)S(1)}, u32[]{:S(2)}, u32[]{:S(2)}) %collective-permute-start.39) | collective-permute-done | bytes 147488 | tf_op jit(solution)/shard_map/ppermute | solution.py:58
  327.6 5.6 %collective-permute-done.33 = bf16[1,2,48,768]{3,2,1,0:T(8,128)(2,1)S(1)} collective-permute-done((bf16[1,2,48,768]{3,2,1,0:T(8,128)(2,1)S(1)}, bf16[1,2,48,768]{3,2,1,0:T(8,128)(2,1)S(1)}, u32[]{:S(2)}, u32[]{:S(2)}) %collective-permute-start.33) | collective-permute-done | bytes 147488 | tf_op jit(solution)/shard_map/ppermute | solution.py:58
  333.1 1.6 collective-permute-start.40
  338.3 2.7 collective-permute-done.34
  344.7 6.9 %gradient_turn.3 = bf16[768,192]{1,0:T(8,128)(2,1)} custom-call(s32[26]{0:T(128)} %pad_add_fusion.meta, s32[4]{0:T(128)} %get-tuple-element.102.items, s32[4]{0:T(128)} %get-tuple-element.111.slots, bf16[8,48,768]{2,1,0:T(8,128)(2,1)} %pad_maximum_fusion.4.refs_1_.refs_0_, bf16[4,8,48,768]{3,2,1,0:T(8,128)(2,1)} %copy-done, ...), custom_call_target="tpu_custom_call" | custom-call | tf_op jit(solution)/shard_map/gradient_turn/pallas_call | solution.py:669
  351.6 3.8 all-to-all-start.1
  358.1 1.6 collective-permute-start.22
  359.7 1.7 collective-permute-done.28
  363.4 6.8 %gradient_turn.2 = bf16[768,192]{1,0:T(8,128)(2,1)} custom-call(s32[26]{0:T(128)} %pad_add_fusion.meta, s32[4]{0:T(128)} %get-tuple-element.103.items, s32[4]{0:T(128)} %get-tuple-element.110.slots, bf16[4,48,768]{2,1,0:T(8,128)(2,1)} %pad_maximum_fusion.11.refs_0_, bf16[8,48,768]{2,1,0:T(8,128)(2,1)} %pad_maximum_fusion.4.refs_1_.refs_0_, ...), custom_call_target="tpu_custom_call" | custom-call | tf_op jit(solution)/shard_map/gradient_turn/pallas_call | solution.py:669
  370.3 5.9 %all-to-all-start = ((bf16[16,48,192]{2,1,0:T(8,128)(2,1)}), bf16[16,48,192]{2,1,0:T(8,128)(2,1)S(1)}, u32[]{:S(2)}, u32[]{:S(2)}) async-start(bf16[16,48,192]{2,1,0:T(8,128)(2,1)} %bitcast.50), calls=%async_computation | async-start | bytes 786432 | tf_op jit(solution)/shard_map/all_to_all | solution.py:959
  376.8 7.5 %adam_step.2 = (f32[8,48,768]{2,1,0:T(8,128)}, f32[8,48,768]{2,1,0:T(8,128)}, bf16[4,48,768]{2,1,0:T(8,128)(2,1)}) custom-call(s32[4]{0:T(128)} %get-tuple-element.111.slots, s32[4]{0:T(128)} %get-tuple-element.104.live, bf16[768,192]{1,0:T(8,128)(2,1)} %bitcast.51, f32[8,48,768]{2,1,0:T(8,128)} %first.3, f32[8,48,768]{2,1,0:T(8,128)} %second.3, ...), custom_call_target="tpu_custom_call" | custom-call | tf_op jit(solution)/shard_map/adam_step/pallas_call | solution.py:718
  384.3 4.1 all-to-all-done
  389.1 8.3 %adam_step.3 = (f32[8,48,768]{2,1,0:T(8,128)}, f32[8,48,768]{2,1,0:T(8,128)}, bf16[4,48,768]{2,1,0:T(8,128)(2,1)}) custom-call(s32[4]{0:T(128)} %get-tuple-element.110.slots, s32[4]{0:T(128)} %get-tuple-element.105.live, bf16[768,192]{1,0:T(8,128)(2,1)} %bitcast.52, f32[8,48,768]{2,1,0:T(8,128)} %first.3, ...), custom_call_target="tpu_custom_call", output_to_operand_aliasing={{0}: (6, {}), {1}: (7, {})} | custom-call | tf_op jit(solution)/shard_map/adam_step/pallas_call | solution.py:718
  398.4 1.8 collective-permute-start.46
  401.5 9.9 %input_grad.1 = (bf16[384,768]{1,0:T(8,128)(2,1)}, f32[1,768]{1,0:T(1,128)}, f32[1,768]{1,0:T(1,128)}) custom-call(s32[26]{0:T(128)} %pad_add_fusion.meta, bf16[384,768]{1,0:T(8,128)(2,1)} %bitcast.48, s32[384,1]{1,0:T(8,128)} %copy.28.maskc, f32[8,768]{1,0:T(8,128)} %reshape.367.vp, f32[768,768]{1,0:T(8,128)} %get-tuple-element.56.dx2, ...), custom_call_target="tpu_custom_call" | custom-call | tf_op jit(solution)/shard_map/input_grad/pallas_call | solution.py:584
  411.4 1.8 collective-permute-start.51
  413.3 1.6 collective-permute-done.56
  415.4 1.6 collective-permute-start.66
  417.0 3.5 collective-permute-start.61
  422.2 6.7 %collective-permute-done.47 = bf16[2,2,48,768]{3,2,1,0:T(8,128)(2,1)S(1)} collective-permute-done((bf16[2,2,48,768]{3,2,1,0:T(8,128)(2,1)S(1)}, bf16[2,2,48,768]{3,2,1,0:T(8,128)(2,1)S(1)}, u32[]{:S(2)}, u32[]{:S(2)}) %collective-permute-start.47) | collective-permute-done | bytes 294944 | tf_op jit(solution)/shard_map/ppermute | solution.py:58
  429.1 4.5 collective-permute-done.57
  436.1 4.7 collective-permute-done.67
  440.8 3.8 collective-permute-done.68
  445.5 16.3 %collective-permute-done.69 = f32[8,768]{1,0:T(8,128)S(1)} collective-permute-done((f32[8,768]{1,0:T(8,128)S(1)}, f32[8,768]{1,0:T(8,128)S(1)}, u32[]{:S(2)}, u32[]{:S(2)}) %collective-permute-start.69) | collective-permute-done | bytes 24608 | tf_op jit(solution)/shard_map/ppermute | solution.py:58
  462.2 2.1 collective-permute-start.63
  464.9 13.5 %collective-permute-done.53.refs_5_ = bf16[4,2,48,768]{3,2,1,0:T(8,128)(2,1)} collective-permute-done((bf16[4,2,48,768]{3,2,1,0:T(8,128)(2,1)S(1)}, bf16[4,2,48,768]{3,2,1,0:T(8,128)(2,1)}, u32[]{:S(2)}, u32[]{:S(2)}) %collective-permute-start.53) | collective-permute-done | bytes 589856 | tf_op jit(solution)/shard_map/ppermute | solution.py:58
  478.4 12.0 %collective-permute-done.63.refs_5_ = bf16[4,2,48,768]{3,2,1,0:T(8,128)(2,1)S(1)} collective-permute-done((bf16[4,2,48,768]{3,2,1,0:T(8,128)(2,1)S(1)}, bf16[4,2,48,768]{3,2,1,0:T(8,128)(2,1)S(1)}, u32[]{:S(2)}, u32[]{:S(2)}) %collective-permute-start.63) | collective-permute-done | bytes 589856 | tf_op jit(solution)/shard_map/ppermute | solution.py:58
  493.5 12.9 %weight_update.2.refs_12_ = f32[8,768,768]{2,1,0:T(8,128)} custom-call(s32[4]{0:T(128)} %get-tuple-element.111.slots, s32[4]{0:T(128)} %get-tuple-element.104.live, s32[26]{0:T(128)} %pad_add_fusion.meta, f32[8,768,768]{2,1,0:T(8,128)} %weights.3, bf16[4,2,48,768]{3,2,1,0:T(8,128)(2,1)} %copy-done.14, bf16[4,2,48,768]{3,2,1,0:T(8,128)(2,1)} %copy-done.27, ...), custom_call_target="tpu_custom_call" | custom-call | tf_op jit(solution)/shard_map/weight_update/pallas_call | solution.py:788
  506.5 13.4 %weight_update.3 = f32[8,768,768]{2,1,0:T(8,128)} custom-call(s32[4]{0:T(128)} %get-tuple-element.110.slots, s32[4]{0:T(128)} %get-tuple-element.105.live, s32[26]{0:T(128)} %pad_add_fusion.meta, f32[8,768,768]{2,1,0:T(8,128)} %weights.3, bf16[4,2,48,768]{3,2,1,0:T(8,128)(2,1)} %copy-done.16, ...), custom_call_target="tpu_custom_call", output_to_operand_aliasing={{}: (16, {})} | custom-call | tf_op jit(solution)/shard_map/weight_update/pallas_call | solution.py:788
  (267 shorter events, 69.1 us)
Async XLA Ops:
  7.0 10.4 %collective-permute-start.3 = (bf16[2,48,768]{2,1,0:T(8,128)(2,1)}, bf16[2,48,768]{2,1,0:T(8,128)(2,1)S(1)}, u32[]{:S(2)}, u32[]{:S(2)}) collective-permute-start(bf16[2,48,768]{2,1,0:T(8,128)(2,1)} %get-tuple-element.48), channel_id=1, source_target_pairs={{0,1},{1,0},{2,3},{3,2},{4,5},{5,4},{6,7},{7,6},{8,9},{9,8},{10,11... | collective-permute-start | bytes 442376 | tf_op jit(solution)/shard_map/ppermute | solution.py:58
  10.0 77.7 %collective-permute-start = (bf16[3072]{0:T(1024)(128)(2,1)S(1)}, bf16[3072]{0:T(1024)(128)(2,1)}, u32[]{:S(2)}, u32[]{:S(2)}) collective-permute-start(bf16[3072]{0:T(1024)(128)(2,1)S(1)} %convert_element_type.497), channel_id=1, source_target_pairs={{0,1},{1,0},{2,3},{3,2},{4,5},{5,4},{6,7},{7,6},{8,9},{9,8},{10,11... | collective-permute-start | bytes 18440 | tf_op jit(solution)/shard_map/ppermute | solution.py:58
  10.0 79.1 %collective-permute-start.1 = (bf16[2,384,768]{2,1,0:T(8,128)(2,1)}, bf16[2,384,768]{2,1,0:T(8,128)(2,1)S(1)}, u32[]{:S(2)}, u32[]{:S(2)}) collective-permute-start(bf16[2,384,768]{2,1,0:T(8,128)(2,1)} %get-tuple-element.47), channel_id=1, source_target_pairs={{0,1},{1,0},{2,3},{3,2},{4,5},{5,4},{6,7},{7,6},{8,9},{9,8},{10,11... | collective-permute-start | bytes 3538952 | tf_op jit(solution)/shard_map/ppermute | solution.py:58
  15.2 74.2 %collective-permute-start.9 = (bf16[2,384,768]{2,1,0:T(8,128)(2,1)}, bf16[2,384,768]{2,1,0:T(8,128)(2,1)}, u32[]{:S(2)}, u32[]{:S(2)}) collective-permute-start(bf16[2,384,768]{2,1,0:T(8,128)(2,1)} %get-tuple-element.51), channel_id=1, source_target_pairs={{0,1},{1,0},{2,3},{3,2},{4,5},{5,4},{6,7},{7,6},{8,9},{9,8},{10,11... | collective-permute-start | bytes 3538952 | tf_op jit(solution)/shard_map/ppermute | solution.py:58
  15.3 52.5 %collective-permute-start.11 = (bf16[2,48,768]{2,1,0:T(8,128)(2,1)}, bf16[2,48,768]{2,1,0:T(8,128)(2,1)S(1)}, u32[]{:S(2)}, u32[]{:S(2)}) collective-permute-start(bf16[2,48,768]{2,1,0:T(8,128)(2,1)} %get-tuple-element.52), channel_id=1, source_target_pairs={{0,1},{1,0},{2,3},{3,2},{4,5},{5,4},{6,7},{7,6},{8,9},{9,8},{10,11... | collective-permute-start | bytes 442376 | tf_op jit(solution)/shard_map/ppermute | solution.py:58
  17.4 53.3 %collective-permute-start.4 = (bf16[1,2,48,768]{3,2,1,0:T(8,128)(2,1)S(1)}, bf16[1,2,48,768]{3,2,1,0:T(8,128)(2,1)S(1)}, u32[]{:S(2)}, u32[]{:S(2)}) collective-permute-start(bf16[1,2,48,768]{3,2,1,0:T(8,128)(2,1)S(1)} %bitcast.53), channel_id=1, source_target_pairs={{0,16},{2,18},{4,20},{6,22},{8,24},{10,26},{12,28},{14,30},{16,0},... | collective-permute-start | bytes 442376 | tf_op jit(solution)/shard_map/ppermute | solution.py:58
  67.9 9.1 %collective-permute-start.12 = (bf16[1,2,48,768]{3,2,1,0:T(8,128)(2,1)S(1)}, bf16[1,2,48,768]{3,2,1,0:T(8,128)(2,1)S(1)}, u32[]{:S(2)}, u32[]{:S(2)}) collective-permute-start(bf16[1,2,48,768]{3,2,1,0:T(8,128)(2,1)S(1)} %bitcast.56), channel_id=1, source_target_pairs={{0,16},{2,18},{4,20},{6,22},{8,24},{10,26},{12,28},{14,30},{16,0},... | collective-permute-start | bytes 442376 | tf_op jit(solution)/shard_map/ppermute | solution.py:58
  70.7 11.3 %collective-permute-start.5 = (bf16[2,2,48,768]{3,2,1,0:T(8,128)(2,1)S(1)}, bf16[2,2,48,768]{3,2,1,0:T(8,128)(2,1)S(1)}, u32[]{:S(2)}, u32[]{:S(2)}) collective-permute-start(bf16[2,2,48,768]{3,2,1,0:T(8,128)(2,1)S(1)} %pad_maximum_fusion.9), channel_id=1, source_target_pairs={{0,8},{2,10},{4,12},{6,14},{8,0},{10,2},{12,4},{14,6},{16,24},{18,... | collective-permute-start | bytes 884744 | tf_op jit(solution)/shard_map/ppermute | solution.py:58
  77.0 9.8 %collective-permute-start.13 = (bf16[2,2,48,768]{3,2,1,0:T(8,128)(2,1)S(1)}, bf16[2,2,48,768]{3,2,1,0:T(8,128)(2,1)S(1)}, u32[]{:S(2)}, u32[]{:S(2)}) collective-permute-start(bf16[2,2,48,768]{3,2,1,0:T(8,128)(2,1)S(1)} %pad_maximum_fusion.10), channel_id=1, source_target_pairs={{0,8},{2,10},{4,12},{6,14},{8,0},{10,2},{12,4},{14,6},{16,24},{18,... | collective-permute-start | bytes 884744 | tf_op jit(solution)/shard_map/ppermute | solution.py:58
  82.1 15.7 %collective-permute-start.6 = (bf16[4,2,48,768]{3,2,1,0:T(8,128)(2,1)S(1)}, bf16[4,2,48,768]{3,2,1,0:T(8,128)(2,1)S(1)}, u32[]{:S(2)}, u32[]{:S(2)}) collective-permute-start(bf16[4,2,48,768]{3,2,1,0:T(8,128)(2,1)S(1)} %pad_maximum_fusion.2.refs_2_), channel_id=1, source_target_pairs={{0,4},{2,6},{4,0},{6,2},{8,12},{10,14},{12,8},{14,10},{16,20},{18,... | collective-permute-start | bytes 1769480 | tf_op jit(solution)/shard_map/ppermute | solution.py:58
  86.8 12.0 %collective-permute-start.7 = (bf16[4,2,48,768]{3,2,1,0:T(8,128)(2,1)S(1)}, bf16[4,2,48,768]{3,2,1,0:T(8,128)(2,1)S(1)}, u32[]{:S(2)}, u32[]{:S(2)}) collective-permute-start(bf16[4,2,48,768]{3,2,1,0:T(8,128)(2,1)S(1)} %pad_maximum_fusion.2.refs_2_), channel_id=1, source_target_pairs={{0,2},{2,0},{4,6},{6,4},{8,10},{10,8},{12,14},{14,12},{16,18},{18,... | collective-permute-start | bytes 1769480 | tf_op jit(solution)/shard_map/ppermute | solution.py:58
  87.7 19.4 %collective-permute-start.14 = (bf16[4,2,48,768]{3,2,1,0:T(8,128)(2,1)}, bf16[4,2,48,768]{3,2,1,0:T(8,128)(2,1)S(1)}, u32[]{:S(2)}, u32[]{:S(2)}) collective-permute-start(bf16[4,2,48,768]{3,2,1,0:T(8,128)(2,1)} %pad_maximum_fusion.3.refs_8_), channel_id=1, source_target_pairs={{0,4},{2,6},{4,0},{6,2},{8,12},{10,14},{12,8},{14,10},{16,20},{18,... | collective-permute-start | bytes 1769480 | tf_op jit(solution)/shard_map/ppermute | solution.py:58
  89.2 37.0 %collective-permute-start.2 = (bf16[1,2,384,768]{3,2,1,0:T(8,128)(2,1)S(1)}, bf16[1,2,384,768]{3,2,1,0:T(8,128)(2,1)S(1)}, u32[]{:S(2)}, u32[]{:S(2)}) collective-permute-start(bf16[1,2,384,768]{3,2,1,0:T(8,128)(2,1)S(1)} %bitcast.40), channel_id=1, source_target_pairs={{0,2},{2,0},{4,6},{6,4},{8,10},{10,8},{12,14},{14,12},{16,18},{18,... | collective-permute-start | bytes 3538952 | tf_op jit(solution)/shard_map/ppermute | solution.py:58
  89.4 60.0 %collective-permute-start.10 = (bf16[1,2,384,768]{3,2,1,0:T(8,128)(2,1)}, bf16[1,2,384,768]{3,2,1,0:T(8,128)(2,1)}, u32[]{:S(2)}, u32[]{:S(2)}) collective-permute-start(bf16[1,2,384,768]{3,2,1,0:T(8,128)(2,1)} %bitcast.9.refs_6_), channel_id=1, source_target_pairs={{0,2},{2,0},{4,6},{6,4},{8,10},{10,8},{12,14},{14,12},{16,18},{18,... | collective-permute-start | bytes 3538952 | tf_op jit(solution)/shard_map/ppermute | solution.py:58
  97.8 11.0 %collective-permute-start.8 = (bf16[4,2,48,768]{3,2,1,0:T(8,128)(2,1)S(1)}, bf16[4,2,48,768]{3,2,1,0:T(8,128)(2,1)S(1)}, u32[]{:S(2)}, u32[]{:S(2)}) collective-permute-start(bf16[4,2,48,768]{3,2,1,0:T(8,128)(2,1)S(1)} %collective-permute-done.6.refs_3_), channel_id=1, source_target_pairs={{0,2},{2,0},{4,6},{6,4},{8,10},{10,8},{12,14},{14,12},{16,18},{18,... | collective-permute-start | bytes 1769480 | tf_op jit(solution)/shard_map/ppermute | solution.py:58
  98.8 50.6 %collective-permute-start.15 = (bf16[4,2,48,768]{3,2,1,0:T(8,128)(2,1)}, bf16[4,2,48,768]{3,2,1,0:T(8,128)(2,1)}, u32[]{:S(2)}, u32[]{:S(2)}) collective-permute-start(bf16[4,2,48,768]{3,2,1,0:T(8,128)(2,1)} %pad_maximum_fusion.3.refs_8_), channel_id=1, source_target_pairs={{0,2},{2,0},{4,6},{6,4},{8,10},{10,8},{12,14},{14,12},{16,18},{18,... | collective-permute-start | bytes 1769480 | tf_op jit(solution)/shard_map/ppermute | solution.py:58
  107.1 42.3 %collective-permute-start.16 = (bf16[4,2,48,768]{3,2,1,0:T(8,128)(2,1)S(1)}, bf16[4,2,48,768]{3,2,1,0:T(8,128)(2,1)}, u32[]{:S(2)}, u32[]{:S(2)}) collective-permute-start(bf16[4,2,48,768]{3,2,1,0:T(8,128)(2,1)S(1)} %collective-permute-done.14.refs_9_), channel_id=1, source_target_pairs={{0,2},{2,0},{4,6},{6,4},{8,10},{10,8},{12,14},{14,12},{16,18},{18,... | collective-permute-start | bytes 1769480 | tf_op jit(solution)/shard_map/ppermute | solution.py:58
  108.8 73.0 %collective-permute-start.41 = (bf16[1,8,48,768]{3,2,1,0:T(8,128)(2,1)}, bf16[1,8,48,768]{3,2,1,0:T(8,128)(2,1)S(1)}, u32[]{:S(2)}, u32[]{:S(2)}) collective-permute-start(bf16[1,8,48,768]{3,2,1,0:T(8,128)(2,1)} %convert_bitcast_fusion), channel_id=1, source_target_pairs={{0,16},{2,18},{4,20},{6,22},{8,24},{10,26},{12,28},{14,30},{16,0},... | collective-permute-start | bytes 1769480 | tf_op jit(solution)/shard_map/ppermute | solution.py:58
  181.3 44.0 %collective-permute-start.35 = (bf16[16,2,48,768]{3,2,1,0:T(8,128)(2,1)}, bf16[16,2,48,768]{3,2,1,0:T(8,128)(2,1)}, u32[]{:S(2)}, u32[]{:S(2)}) collective-permute-start(bf16[16,2,48,768]{3,2,1,0:T(8,128)(2,1)} %get-tuple-element.75), channel_id=1, source_target_pairs={{0,2},{2,0},{4,6},{6,4},{8,10},{10,8},{12,14},{14,12},{16,18},{18,... | collective-permute-start | bytes 7077896 | tf_op jit(solution)/shard_map/ppermute | solution.py:58
  181.5 47.1 %collective-permute-start.29 = (bf16[16,2,48,768]{3,2,1,0:T(8,128)(2,1)}, bf16[16,2,48,768]{3,2,1,0:T(8,128)(2,1)}, u32[]{:S(2)}, u32[]{:S(2)}) collective-permute-start(bf16[16,2,48,768]{3,2,1,0:T(8,128)(2,1)} %get-tuple-element.73), channel_id=1, source_target_pairs={{0,2},{2,0},{4,6},{6,4},{8,10},{10,8},{12,14},{14,12},{16,18},{18,... | collective-permute-start | bytes 7077896 | tf_op jit(solution)/shard_map/ppermute | solution.py:58
  184.2 37.1 %collective-permute-start.42 = (bf16[2,8,48,768]{3,2,1,0:T(8,128)(2,1)}, bf16[2,8,48,768]{3,2,1,0:T(8,128)(2,1)}, u32[]{:S(2)}, u32[]{:S(2)}) collective-permute-start(bf16[2,8,48,768]{3,2,1,0:T(8,128)(2,1)} %pad_maximum_fusion.1), channel_id=1, source_target_pairs={{0,4},{2,6},{4,0},{6,2},{8,12},{10,14},{12,8},{14,10},{16,20},{18,... | collective-permute-start | bytes 3538952 | tf_op jit(solution)/shard_map/ppermute | solution.py:58
  223.2 53.7 %collective-permute-start.43 = (bf16[4,8,48,768]{3,2,1,0:T(8,128)(2,1)S(1)}, bf16[4,8,48,768]{3,2,1,0:T(8,128)(2,1)S(1)}, u32[]{:S(2)}, u32[]{:S(2)}) collective-permute-start(bf16[4,8,48,768]{3,2,1,0:T(8,128)(2,1)S(1)} %pad_maximum_fusion.refs_2_.refs_1_.refs_8_), channel_id=1, source_target_pairs={{0,8},{2,10},{4,12},{6,14},{8,0},{10,2},{12,4},{14,6},{16,24},{18,... | collective-permute-start | bytes 7077896 | tf_op jit(solution)/shard_map/ppermute | solution.py:58
  224.3 7.6 %collective-permute-start.17 = (bf16[16,1,48,768]{3,2,1,0:T(8,128)(2,1)S(1)}, bf16[16,1,48,768]{3,2,1,0:T(8,128)(2,1)S(1)}, u32[]{:S(2)}, u32[]{:S(2)}) collective-permute-start(bf16[16,1,48,768]{3,2,1,0:T(8,128)(2,1)S(1)} %copy-done.47), channel_id=1, source_target_pairs={{0,2},{2,0},{4,6},{6,4},{8,10},{10,8},{12,14},{14,12},{16,18},{18,... | collective-permute-start | bytes 3538952 | tf_op jit(solution)/shard_map/ppermute | solution.py:58
  224.6 16.3 %collective-permute-start.24 = (bf16[8,1,48,768]{3,2,1,0:T(8,128)(2,1)S(1)}, bf16[8,1,48,768]{3,2,1,0:T(8,128)(2,1)S(1)}, u32[]{:S(2)}, u32[]{:S(2)}) collective-permute-start(bf16[8,1,48,768]{3,2,1,0:T(8,128)(2,1)S(1)} %add_convert_fusion.4), channel_id=1, source_target_pairs={{0,4},{2,6},{4,0},{6,2},{8,12},{10,14},{12,8},{14,10},{16,20},{18,... | collective-permute-start | bytes 1769480 | tf_op jit(solution)/shard_map/ppermute | solution.py:58
  226.9 50.5 %collective-permute-start.36 = (bf16[8,2,48,768]{3,2,1,0:T(8,128)(2,1)S(1)}, bf16[8,2,48,768]{3,2,1,0:T(8,128)(2,1)S(1)}, u32[]{:S(2)}, u32[]{:S(2)}) collective-permute-start(bf16[8,2,48,768]{3,2,1,0:T(8,128)(2,1)S(1)} %add_convert_fusion), channel_id=1, source_target_pairs={{0,1},{1,0},{2,3},{3,2},{4,5},{5,4},{6,7},{7,6},{8,9},{9,8},{10,11... | collective-permute-start | bytes 3538952 | tf_op jit(solution)/shard_map/ppermute | solution.py:58
  230.3 48.7 %collective-permute-start.30 = (bf16[8,2,48,768]{3,2,1,0:T(8,128)(2,1)S(1)}, bf16[8,2,48,768]{3,2,1,0:T(8,128)(2,1)S(1)}, u32[]{:S(2)}, u32[]{:S(2)}) collective-permute-start(bf16[8,2,48,768]{3,2,1,0:T(8,128)(2,1)S(1)} %add_convert_fusion.1), channel_id=1, source_target_pairs={{0,4},{2,6},{4,0},{6,2},{8,12},{10,14},{12,8},{14,10},{16,20},{18,... | collective-permute-start | bytes 3538952 | tf_op jit(solution)/shard_map/ppermute | solution.py:58
  232.0 35.5 %collective-permute-start.18 = (bf16[8,1,48,768]{3,2,1,0:T(8,128)(2,1)S(1)}, bf16[8,1,48,768]{3,2,1,0:T(8,128)(2,1)S(1)}, u32[]{:S(2)}, u32[]{:S(2)}) collective-permute-start(bf16[8,1,48,768]{3,2,1,0:T(8,128)(2,1)S(1)} %add_convert_fusion.5), channel_id=1, source_target_pairs={{0,1},{1,0},{2,3},{3,2},{4,5},{5,4},{6,7},{7,6},{8,9},{9,8},{10,11... | collective-permute-start | bytes 1769480 | tf_op jit(solution)/shard_map/ppermute | solution.py:58
  240.9 101.0 %collective-permute-start.44 = (bf16[4,8,48,768]{3,2,1,0:T(8,128)(2,1)S(1)}, bf16[4,8,48,768]{3,2,1,0:T(8,128)(2,1)S(1)}, u32[]{:S(2)}, u32[]{:S(2)}) collective-permute-start(bf16[4,8,48,768]{3,2,1,0:T(8,128)(2,1)S(1)} %pad_maximum_fusion.refs_2_.refs_1_.refs_8_), channel_id=1, source_target_pairs={{0,2},{2,0},{4,6},{6,4},{8,10},{10,8},{12,14},{14,12},{16,18},{18,... | collective-permute-start | bytes 7077896 | tf_op jit(solution)/shard_map/ppermute | solution.py:58
  267.5 14.1 %collective-permute-start.25 = (bf16[4,1,48,768]{3,2,1,0:T(8,128)(2,1)S(1)}, bf16[4,1,48,768]{3,2,1,0:T(8,128)(2,1)S(1)}, u32[]{:S(2)}, u32[]{:S(2)}) collective-permute-start(bf16[4,1,48,768]{3,2,1,0:T(8,128)(2,1)S(1)} %add_convert_fusion.8), channel_id=1, source_target_pairs={{0,1},{1,0},{2,3},{3,2},{4,5},{5,4},{6,7},{7,6},{8,9},{9,8},{10,11... | collective-permute-start | bytes 884744 | tf_op jit(solution)/shard_map/ppermute | solution.py:58
  276.9 9.9 %collective-permute-start.19 = (bf16[4,1,48,768]{3,2,1,0:T(8,128)(2,1)S(1)}, bf16[4,1,48,768]{3,2,1,0:T(8,128)(2,1)S(1)}, u32[]{:S(2)}, u32[]{:S(2)}) collective-permute-start(bf16[4,1,48,768]{3,2,1,0:T(8,128)(2,1)S(1)} %add_convert_fusion.9), channel_id=1, source_target_pairs={{0,4},{2,6},{4,0},{6,2},{8,12},{10,14},{12,8},{14,10},{16,20},{18,... | collective-permute-start | bytes 884744 | tf_op jit(solution)/shard_map/ppermute | solution.py:58
  277.4 64.5 %collective-permute-start.45 = (bf16[4,8,48,768]{3,2,1,0:T(8,128)(2,1)S(1)}, bf16[4,8,48,768]{3,2,1,0:T(8,128)(2,1)S(1)}, u32[]{:S(2)}, u32[]{:S(2)}) collective-permute-start(bf16[4,8,48,768]{3,2,1,0:T(8,128)(2,1)S(1)} %collective-permute-done.43.refs_3_.refs_2_.refs_9_), channel_id=1, source_target_pairs={{0,2},{2,0},{4,6},{6,4},{8,10},{10,8},{12,14},{14,12},{16,18},{18,... | collective-permute-start | bytes 7077896 | tf_op jit(solution)/shard_map/ppermute | solution.py:58
  279.0 19.0 %collective-permute-start.37 = (bf16[4,2,48,768]{3,2,1,0:T(8,128)(2,1)S(1)}, bf16[4,2,48,768]{3,2,1,0:T(8,128)(2,1)S(1)}, u32[]{:S(2)}, u32[]{:S(2)}) collective-permute-start(bf16[4,2,48,768]{3,2,1,0:T(8,128)(2,1)S(1)} %add_convert_fusion.2), channel_id=1, source_target_pairs={{0,4},{2,6},{4,0},{6,2},{8,12},{10,14},{12,8},{14,10},{16,20},{18,... | collective-permute-start | bytes 1769480 | tf_op jit(solution)/shard_map/ppermute | solution.py:58
  281.6 18.6 %collective-permute-start.31 = (bf16[4,2,48,768]{3,2,1,0:T(8,128)(2,1)S(1)}, bf16[4,2,48,768]{3,2,1,0:T(8,128)(2,1)S(1)}, u32[]{:S(2)}, u32[]{:S(2)}) collective-permute-start(bf16[4,2,48,768]{3,2,1,0:T(8,128)(2,1)S(1)} %add_convert_fusion.3), channel_id=1, source_target_pairs={{0,1},{1,0},{2,3},{3,2},{4,5},{5,4},{6,7},{7,6},{8,9},{9,8},{10,11... | collective-permute-start | bytes 1769480 | tf_op jit(solution)/shard_map/ppermute | solution.py:58
  286.8 15.6 %collective-permute-start.26 = (bf16[2,1,48,768]{3,2,1,0:T(8,128)(2,1)S(1)}, bf16[2,1,48,768]{3,2,1,0:T(8,128)(2,1)S(1)}, u32[]{:S(2)}, u32[]{:S(2)}) collective-permute-start(bf16[2,1,48,768]{3,2,1,0:T(8,128)(2,1)S(1)} %add_convert_fusion.14), channel_id=1, source_target_pairs={{0,8},{2,10},{4,12},{6,14},{8,0},{10,2},{12,4},{14,6},{16,24},{18,... | collective-permute-start | bytes 442376 | tf_op jit(solution)/shard_map/ppermute | solution.py:58
  298.1 37.7 %collective-permute-start.20 = (bf16[2,1,48,768]{3,2,1,0:T(8,128)(2,1)S(1)}, bf16[2,1,48,768]{3,2,1,0:T(8,128)(2,1)S(1)}, u32[]{:S(2)}, u32[]{:S(2)}) collective-permute-start(bf16[2,1,48,768]{3,2,1,0:T(8,128)(2,1)S(1)} %add_convert_fusion.15), channel_id=1, source_target_pairs={{0,8},{2,10},{4,12},{6,14},{8,0},{10,2},{12,4},{14,6},{16,24},{18,... | collective-permute-start | bytes 442376 | tf_op jit(solution)/shard_map/ppermute | solution.py:58
  300.2 10.9 %collective-permute-start.38 = (bf16[2,2,48,768]{3,2,1,0:T(8,128)(2,1)S(1)}, bf16[2,2,48,768]{3,2,1,0:T(8,128)(2,1)S(1)}, u32[]{:S(2)}, u32[]{:S(2)}) collective-permute-start(bf16[2,2,48,768]{3,2,1,0:T(8,128)(2,1)S(1)} %add_convert_fusion.6), channel_id=1, source_target_pairs={{0,8},{2,10},{4,12},{6,14},{8,0},{10,2},{12,4},{14,6},{16,24},{18,... | collective-permute-start | bytes 884744 | tf_op jit(solution)/shard_map/ppermute | solution.py:58
  302.4 14.7 %collective-permute-start.32 = (bf16[2,2,48,768]{3,2,1,0:T(8,128)(2,1)S(1)}, bf16[2,2,48,768]{3,2,1,0:T(8,128)(2,1)S(1)}, u32[]{:S(2)}, u32[]{:S(2)}) collective-permute-start(bf16[2,2,48,768]{3,2,1,0:T(8,128)(2,1)S(1)} %add_convert_fusion.7), channel_id=1, source_target_pairs={{0,8},{2,10},{4,12},{6,14},{8,0},{10,2},{12,4},{14,6},{16,24},{18,... | collective-permute-start | bytes 884744 | tf_op jit(solution)/shard_map/ppermute | solution.py:58
  311.1 44.3 %collective-permute-start.27 = (bf16[1,1,48,768]{3,2,1,0:T(8,128)(2,1)}, bf16[1,1,48,768]{3,2,1,0:T(8,128)(2,1)}, u32[]{:S(2)}, u32[]{:S(2)}) collective-permute-start(bf16[1,1,48,768]{3,2,1,0:T(8,128)(2,1)} %add_convert_fusion.18), channel_id=1, source_target_pairs={{0,16},{2,18},{4,20},{6,22},{8,24},{10,26},{12,28},{14,30},{16,0},... | collective-permute-start | bytes 221192 | tf_op jit(solution)/shard_map/ppermute | solution.py:58
  317.1 9.4 %collective-permute-start.39 = (bf16[1,2,48,768]{3,2,1,0:T(8,128)(2,1)S(1)}, bf16[1,2,48,768]{3,2,1,0:T(8,128)(2,1)S(1)}, u32[]{:S(2)}, u32[]{:S(2)}) collective-permute-start(bf16[1,2,48,768]{3,2,1,0:T(8,128)(2,1)S(1)} %add_convert_fusion.12), channel_id=1, source_target_pairs={{0,16},{2,18},{4,20},{6,22},{8,24},{10,26},{12,28},{14,30},{16,0},... | collective-permute-start | bytes 442376 | tf_op jit(solution)/shard_map/ppermute | solution.py:58
  326.5 6.6 %collective-permute-start.33 = (bf16[1,2,48,768]{3,2,1,0:T(8,128)(2,1)S(1)}, bf16[1,2,48,768]{3,2,1,0:T(8,128)(2,1)S(1)}, u32[]{:S(2)}, u32[]{:S(2)}) collective-permute-start(bf16[1,2,48,768]{3,2,1,0:T(8,128)(2,1)S(1)} %add_convert_fusion.13), channel_id=1, source_target_pairs={{0,16},{2,18},{4,20},{6,22},{8,24},{10,26},{12,28},{14,30},{16,0},... | collective-permute-start | bytes 442376 | tf_op jit(solution)/shard_map/ppermute | solution.py:58
  338.3 18.7 %collective-permute-start.21 = (bf16[1,1,48,768]{3,2,1,0:T(8,128)(2,1)}, bf16[1,1,48,768]{3,2,1,0:T(8,128)(2,1)}, u32[]{:S(2)}, u32[]{:S(2)}) collective-permute-start(bf16[1,1,48,768]{3,2,1,0:T(8,128)(2,1)} %add_convert_fusion.19), channel_id=1, source_target_pairs={{0,16},{2,18},{4,20},{6,22},{8,24},{10,26},{12,28},{14,30},{16,0},... | collective-permute-start | bytes 221192 | tf_op jit(solution)/shard_map/ppermute | solution.py:58
  351.6 18.6 %all-to-all-start.1 = ((bf16[16,48,192]{2,1,0:T(8,128)(2,1)}), bf16[16,48,192]{2,1,0:T(8,128)(2,1)S(1)}, u32[]{:S(2)}, u32[]{:S(2)}) async-start(bf16[16,48,192]{2,1,0:T(8,128)(2,1)} %bitcast.49), calls=%async_computation.1 | async-start | bytes 786432 | tf_op jit(solution)/shard_map/all_to_all | solution.py:959
  370.3 18.1 %all-to-all-start = ((bf16[16,48,192]{2,1,0:T(8,128)(2,1)}), bf16[16,48,192]{2,1,0:T(8,128)(2,1)S(1)}, u32[]{:S(2)}, u32[]{:S(2)}) async-start(bf16[16,48,192]{2,1,0:T(8,128)(2,1)} %bitcast.50), calls=%async_computation | async-start | bytes 786432 | tf_op jit(solution)/shard_map/all_to_all | solution.py:959
  398.4 14.8 %collective-permute-start.46 = (bf16[1,2,48,768]{3,2,1,0:T(8,128)(2,1)S(1)}, bf16[1,2,48,768]{3,2,1,0:T(8,128)(2,1)S(1)}, u32[]{:S(2)}, u32[]{:S(2)}) collective-permute-start(bf16[1,2,48,768]{3,2,1,0:T(8,128)(2,1)S(1)} %get-tuple-element.98), channel_id=1, source_target_pairs={{0,16},{2,18},{4,20},{6,22},{8,24},{10,26},{12,28},{14,30},{16,0},... | collective-permute-start | bytes 442376 | tf_op jit(solution)/shard_map/ppermute | solution.py:58
  400.2 14.8 %collective-permute-start.56 = (bf16[1,2,48,768]{3,2,1,0:T(8,128)(2,1)S(1)}, bf16[1,2,48,768]{3,2,1,0:T(8,128)(2,1)S(1)}, u32[]{:S(2)}, u32[]{:S(2)}) collective-permute-start(bf16[1,2,48,768]{3,2,1,0:T(8,128)(2,1)S(1)} %get-tuple-element.96), channel_id=1, source_target_pairs={{0,16},{2,18},{4,20},{6,22},{8,24},{10,26},{12,28},{14,30},{16,0},... | collective-permute-start | bytes 442376 | tf_op jit(solution)/shard_map/ppermute | solution.py:58
  411.4 10.2 %collective-permute-start.51 = (bf16[1,2,48,768]{3,2,1,0:T(8,128)(2,1)S(1)}, bf16[1,2,48,768]{3,2,1,0:T(8,128)(2,1)S(1)}, u32[]{:S(2)}, u32[]{:S(2)}) collective-permute-start(bf16[1,2,48,768]{3,2,1,0:T(8,128)(2,1)S(1)} %get-tuple-element.97), channel_id=1, source_target_pairs={{0,16},{2,18},{4,20},{6,22},{8,24},{10,26},{12,28},{14,30},{16,0},... | collective-permute-start | bytes 442376 | tf_op jit(solution)/shard_map/ppermute | solution.py:58
  413.2 15.8 %collective-permute-start.47 = (bf16[2,2,48,768]{3,2,1,0:T(8,128)(2,1)S(1)}, bf16[2,2,48,768]{3,2,1,0:T(8,128)(2,1)S(1)}, u32[]{:S(2)}, u32[]{:S(2)}) collective-permute-start(bf16[2,2,48,768]{3,2,1,0:T(8,128)(2,1)S(1)} %pad_maximum_fusion.12), channel_id=1, source_target_pairs={{0,8},{2,10},{4,12},{6,14},{8,0},{10,2},{12,4},{14,6},{16,24},{18,... | collective-permute-start | bytes 884744 | tf_op jit(solution)/shard_map/ppermute | solution.py:58
  415.0 18.7 %collective-permute-start.57 = (bf16[2,2,48,768]{3,2,1,0:T(8,128)(2,1)S(1)}, bf16[2,2,48,768]{3,2,1,0:T(8,128)(2,1)S(1)}, u32[]{:S(2)}, u32[]{:S(2)}) collective-permute-start(bf16[2,2,48,768]{3,2,1,0:T(8,128)(2,1)S(1)} %pad_maximum_fusion.14), channel_id=1, source_target_pairs={{0,8},{2,10},{4,12},{6,14},{8,0},{10,2},{12,4},{14,6},{16,24},{18,... | collective-permute-start | bytes 884744 | tf_op jit(solution)/shard_map/ppermute | solution.py:58
  415.4 20.5 %collective-permute-start.66 = (f32[8,768]{1,0:T(8,128)S(1)}, f32[8,768]{1,0:T(8,128)S(1)}, u32[]{:S(2)}, u32[]{:S(2)}) collective-permute-start(f32[8,768]{1,0:T(8,128)S(1)} %pad_maximum_fusion.18), channel_id=1, source_target_pairs={{0,1},{1,0},{2,3},{3,2},{4,5},{5,4},{6,7},{7,6},{8,9},{9,8},{10,11... | collective-permute-start | bytes 73736 | tf_op jit(solution)/shard_map/ppermute | solution.py:58
  417.0 17.7 %collective-permute-start.61 = (bf16[1,2,48,768]{3,2,1,0:T(8,128)(2,1)S(1)}, bf16[1,2,48,768]{3,2,1,0:T(8,128)(2,1)S(1)}, u32[]{:S(2)}, u32[]{:S(2)}) collective-permute-start(bf16[1,2,48,768]{3,2,1,0:T(8,128)(2,1)S(1)} %get-tuple-element.95), channel_id=1, source_target_pairs={{0,16},{2,18},{4,20},{6,22},{8,24},{10,26},{12,28},{14,30},{16,0},... | collective-permute-start | bytes 442376 | tf_op jit(solution)/shard_map/ppermute | solution.py:58
  421.6 40.3 %collective-permute-start.52 = (bf16[2,2,48,768]{3,2,1,0:T(8,128)(2,1)S(1)}, bf16[2,2,48,768]{3,2,1,0:T(8,128)(2,1)S(1)}, u32[]{:S(2)}, u32[]{:S(2)}) collective-permute-start(bf16[2,2,48,768]{3,2,1,0:T(8,128)(2,1)S(1)} %pad_maximum_fusion.13), channel_id=1, source_target_pairs={{0,4},{2,6},{4,0},{6,2},{8,12},{10,14},{12,8},{14,10},{16,20},{18,... | collective-permute-start | bytes 884744 | tf_op jit(solution)/shard_map/ppermute | solution.py:58
  429.0 35.2 %collective-permute-start.48 = (bf16[4,2,48,768]{3,2,1,0:T(8,128)(2,1)S(1)}, bf16[4,2,48,768]{3,2,1,0:T(8,128)(2,1)}, u32[]{:S(2)}, u32[]{:S(2)}) collective-permute-start(bf16[4,2,48,768]{3,2,1,0:T(8,128)(2,1)S(1)} %pad_maximum_fusion.5.refs_0_), channel_id=1, source_target_pairs={{0,4},{2,6},{4,0},{6,2},{8,12},{10,14},{12,8},{14,10},{16,20},{18,... | collective-permute-start | bytes 1769480 | tf_op jit(solution)/shard_map/ppermute | solution.py:58
  433.7 31.1 %collective-permute-start.58 = (bf16[4,2,48,768]{3,2,1,0:T(8,128)(2,1)S(1)}, bf16[4,2,48,768]{3,2,1,0:T(8,128)(2,1)S(1)}, u32[]{:S(2)}, u32[]{:S(2)}) collective-permute-start(bf16[4,2,48,768]{3,2,1,0:T(8,128)(2,1)S(1)} %pad_maximum_fusion.7.refs_0_), channel_id=1, source_target_pairs={{0,4},{2,6},{4,0},{6,2},{8,12},{10,14},{12,8},{14,10},{16,20},{18,... | collective-permute-start | bytes 1769480 | tf_op jit(solution)/shard_map/ppermute | solution.py:58
  434.7 27.4 %collective-permute-start.62 = (bf16[2,2,48,768]{3,2,1,0:T(8,128)(2,1)S(1)}, bf16[2,2,48,768]{3,2,1,0:T(8,128)(2,1)S(1)}, u32[]{:S(2)}, u32[]{:S(2)}) collective-permute-start(bf16[2,2,48,768]{3,2,1,0:T(8,128)(2,1)S(1)} %pad_maximum_fusion.15), channel_id=1, source_target_pairs={{0,4},{2,6},{4,0},{6,2},{8,12},{10,14},{12,8},{14,10},{16,20},{18,... | collective-permute-start | bytes 884744 | tf_op jit(solution)/shard_map/ppermute | solution.py:58
  444.6 17.2 %collective-permute-start.69 = (f32[8,768]{1,0:T(8,128)S(1)}, f32[8,768]{1,0:T(8,128)S(1)}, u32[]{:S(2)}, u32[]{:S(2)}) collective-permute-start(f32[8,768]{1,0:T(8,128)S(1)} %add.447), channel_id=1, source_target_pairs={{0,4},{2,6},{4,0},{6,2},{8,12},{10,14},{12,8},{14,10},{16,20},{18,... | collective-permute-start | bytes 73736 | tf_op jit(solution)/shard_map/ppermute | solution.py:58
  462.0 16.4 %collective-permute-start.53 = (bf16[4,2,48,768]{3,2,1,0:T(8,128)(2,1)S(1)}, bf16[4,2,48,768]{3,2,1,0:T(8,128)(2,1)}, u32[]{:S(2)}, u32[]{:S(2)}) collective-permute-start(bf16[4,2,48,768]{3,2,1,0:T(8,128)(2,1)S(1)} %pad_maximum_fusion.6.refs_4_), channel_id=1, source_target_pairs={{0,8},{2,10},{4,12},{6,14},{8,0},{10,2},{12,4},{14,6},{16,24},{18,... | collective-permute-start | bytes 1769480 | tf_op jit(solution)/shard_map/ppermute | solution.py:58
  462.2 28.3 %collective-permute-start.63 = (bf16[4,2,48,768]{3,2,1,0:T(8,128)(2,1)S(1)}, bf16[4,2,48,768]{3,2,1,0:T(8,128)(2,1)S(1)}, u32[]{:S(2)}, u32[]{:S(2)}) collective-permute-start(bf16[4,2,48,768]{3,2,1,0:T(8,128)(2,1)S(1)} %pad_maximum_fusion.8.refs_4_), channel_id=1, source_target_pairs={{0,8},{2,10},{4,12},{6,14},{8,0},{10,2},{12,4},{14,6},{16,24},{18,... | collective-permute-start | bytes 1769480 | tf_op jit(solution)/shard_map/ppermute | solution.py:58
  464.3 26.2 %collective-permute-start.59 = (bf16[4,2,48,768]{3,2,1,0:T(8,128)(2,1)S(1)}, bf16[4,2,48,768]{3,2,1,0:T(8,128)(2,1)S(1)}, u32[]{:S(2)}, u32[]{:S(2)}) collective-permute-start(bf16[4,2,48,768]{3,2,1,0:T(8,128)(2,1)S(1)} %pad_maximum_fusion.7.refs_0_), channel_id=1, source_target_pairs={{0,2},{2,0},{4,6},{6,4},{8,10},{10,8},{12,14},{14,12},{16,18},{18,... | collective-permute-start | bytes 1769480 | tf_op jit(solution)/shard_map/ppermute | solution.py:58
  464.3 26.7 %collective-permute-start.64 = (bf16[4,2,48,768]{3,2,1,0:T(8,128)(2,1)S(1)}, bf16[4,2,48,768]{3,2,1,0:T(8,128)(2,1)S(1)}, u32[]{:S(2)}, u32[]{:S(2)}) collective-permute-start(bf16[4,2,48,768]{3,2,1,0:T(8,128)(2,1)S(1)} %pad_maximum_fusion.8.refs_4_), channel_id=1, source_target_pairs={{0,2},{2,0},{4,6},{6,4},{8,10},{10,8},{12,14},{14,12},{16,18},{18,... | collective-permute-start | bytes 1769480 | tf_op jit(solution)/shard_map/ppermute | solution.py:58
  464.8 26.3 %collective-permute-start.60 = (bf16[4,2,48,768]{3,2,1,0:T(8,128)(2,1)S(1)}, bf16[4,2,48,768]{3,2,1,0:T(8,128)(2,1)S(1)}, u32[]{:S(2)}, u32[]{:S(2)}) collective-permute-start(bf16[4,2,48,768]{3,2,1,0:T(8,128)(2,1)S(1)} %collective-permute-done.58.refs_1_), channel_id=1, source_target_pairs={{0,2},{2,0},{4,6},{6,4},{8,10},{10,8},{12,14},{14,12},{16,18},{18,... | collective-permute-start | bytes 1769480 | tf_op jit(solution)/shard_map/ppermute | solution.py:58
  478.4 28.0 %collective-permute-start.49 = (bf16[4,2,48,768]{3,2,1,0:T(8,128)(2,1)S(1)}, bf16[4,2,48,768]{3,2,1,0:T(8,128)(2,1)}, u32[]{:S(2)}, u32[]{:S(2)}) collective-permute-start(bf16[4,2,48,768]{3,2,1,0:T(8,128)(2,1)S(1)} %pad_maximum_fusion.5.refs_0_), channel_id=1, source_target_pairs={{0,2},{2,0},{4,6},{6,4},{8,10},{10,8},{12,14},{14,12},{16,18},{18,... | collective-permute-start | bytes 1769480 | tf_op jit(solution)/shard_map/ppermute | solution.py:58
  490.5 16.0 %collective-permute-start.54 = (bf16[4,2,48,768]{3,2,1,0:T(8,128)(2,1)S(1)}, bf16[4,2,48,768]{3,2,1,0:T(8,128)(2,1)}, u32[]{:S(2)}, u32[]{:S(2)}) collective-permute-start(bf16[4,2,48,768]{3,2,1,0:T(8,128)(2,1)S(1)} %pad_maximum_fusion.6.refs_4_), channel_id=1, source_target_pairs={{0,2},{2,0},{4,6},{6,4},{8,10},{10,8},{12,14},{14,12},{16,18},{18,... | collective-permute-start | bytes 1769480 | tf_op jit(solution)/shard_map/ppermute | solution.py:58
  491.0 15.5 %collective-permute-start.50 = (bf16[4,2,48,768]{3,2,1,0:T(8,128)(2,1)}, bf16[4,2,48,768]{3,2,1,0:T(8,128)(2,1)}, u32[]{:S(2)}, u32[]{:S(2)}) collective-permute-start(bf16[4,2,48,768]{3,2,1,0:T(8,128)(2,1)} %collective-permute-done.48.refs_1_), channel_id=1, source_target_pairs={{0,2},{2,0},{4,6},{6,4},{8,10},{10,8},{12,14},{14,12},{16,18},{18,... | collective-permute-start | bytes 1769480 | tf_op jit(solution)/shard_map/ppermute | solution.py:58
  492.6 13.8 %collective-permute-start.55 = (bf16[4,2,48,768]{3,2,1,0:T(8,128)(2,1)}, bf16[4,2,48,768]{3,2,1,0:T(8,128)(2,1)}, u32[]{:S(2)}, u32[]{:S(2)}) collective-permute-start(bf16[4,2,48,768]{3,2,1,0:T(8,128)(2,1)} %collective-permute-done.53.refs_5_), channel_id=1, source_target_pairs={{0,2},{2,0},{4,6},{6,4},{8,10},{10,8},{12,14},{14,12},{16,18},{18,... | collective-permute-start | bytes 1769480 | tf_op jit(solution)/shard_map/ppermute | solution.py:58
  (57 other events, 851.1 us)

commit v2 on v1

--- a/solution.py
+++ b/solution.py
@@ -238,13 +238,19 @@
     return jnp.where(mask_ref[...] == 1, vp_ref[0:1, :], tok)
 
 
-def forward_kernel(shapes, meta, tok, maskc, vp, cos, sin, own, *refs):
+def start_blocks(meta, count, own, groups, dst, sems):
+    def begin(b, carry):
+        start_block(meta, b, own, groups, dst.at[b], sems.at[b])
+        return carry
+
+    lax.fori_loop(0, count, begin, 0)
+
+
+def qkv_kernel(shapes, meta, tok, maskc, vp, cos, sin, own, *refs):
     nw = sum(n for n, _ in shapes)
     first = split_refs(shapes, refs)
-    q_ref, k_ref, v_ref, n1_ref, o_ref, lse_ref, x2_ref, n2_ref = refs[nw : nw + 8]
-    wbuf, sems = refs[nw + 8 :]
-    for b in range(4):
-        start_block(meta, b, own, first, wbuf.at[b], sems.at[b])
+    q_ref, k_ref, v_ref, n1_ref, wbuf, sems = refs[nw:]
+    start_blocks(meta, 3, own, first, wbuf, sems)
     for half in range(2):
         cen, r = norm_stats(input_rows(tok, maskc, vp, half))
         n1_ref[half * SEQ : (half + 1) * SEQ, :] = (cen * r * vp[1:2, :]).astype(BF)
@@ -263,6 +269,25 @@
                     at = c * CHUNK + s * PAIR
                     out[rows, at : at + PAIR] = piece.astype(BF)
 
+
+def run_qkv(meta, tok, maskc, vp, cos, sin, own, first):
+    vm = pl.BlockSpec(memory_space=pltpu.VMEM)
+    arrays = group_arrays(first)
+    return pl.pallas_call(
+        partial(qkv_kernel, group_shapes(first)),
+        name="project_qkv",
+        out_shape=(jax.ShapeDtypeStruct((ROWS, D), BF),) * 4,
+        in_specs=[pl.BlockSpec(memory_space=pltpu.SMEM)] + [vm] * 5 + [any_spec()] * (1 + len(arrays)),
+        out_specs=(vm,) * 4,
+        scratch_shapes=[pltpu.VMEM((3, D, D), BF), pltpu.SemaphoreType.DMA((3,))],
+    )(meta, tok, maskc, vp, cos, sin, own, *arrays)
+
+
+def forward_kernel(shapes, meta, tok, maskc, vp, q_ref, k_ref, v_ref, own, *refs):
+    nw = sum(n for n, _ in shapes)
+    first = split_refs(shapes, refs)
+    o_ref, lse_ref, x2_ref, n2_ref, wbuf, sems = refs[nw:]
+    start_block(meta, 3, own, first, wbuf, sems.at[0])
     masks = tile_masks()
 
     def one_pair(p, carry):
@@ -293,16 +318,16 @@
         return carry
 
     lax.fori_loop(0, NPAIR, one_pair, 0)
-    wait_block(wbuf.at[3], sems.at[3])
+    wait_block(wbuf, sems.at[0])
     for half in range(2):
         rows = slice(half * SEQ, (half + 1) * SEQ)
-        x2 = input_rows(tok, maskc, vp, half) + mm(o_ref[rows, :], wbuf[3])
+        x2 = input_rows(tok, maskc, vp, half) + mm(o_ref[rows, :], wbuf[...])
         x2_ref[rows, :] = x2
         cen, r = norm_stats(x2)
         n2_ref[rows, :] = (cen * r * vp[2:3, :]).astype(BF)
 
 
-def run_forward(meta, tok, maskc, vp, cos, sin, own, first):
+def run_forward(meta, tok, maskc, vp, q, k, v, own, first):
     vm = pl.BlockSpec(memory_space=pltpu.VMEM)
     sq = jax.ShapeDtypeStruct((ROWS, D), BF)
     arrays = group_arrays(first)
@@ -311,18 +336,14 @@
         name="forward_attention",
         out_shape=(
             sq,
-            sq,
-            sq,
-            sq,
-            sq,
             jax.ShapeDtypeStruct((NPAIR, 2, ROWS), F32),
             jax.ShapeDtypeStruct((ROWS, D), F32),
             sq,
         ),
-        in_specs=[pl.BlockSpec(memory_space=pltpu.SMEM)] + [vm] * 5 + [any_spec()] * (1 + len(arrays)),
-        out_specs=(vm,) * 8,
-        scratch_shapes=[pltpu.VMEM((4, D, D), BF), pltpu.SemaphoreType.DMA((4,))],
-    )(meta, tok, maskc, vp, cos, sin, own, *arrays)
+        in_specs=[pl.BlockSpec(memory_space=pltpu.SMEM)] + [vm] * 6 + [any_spec()] * (1 + len(arrays)),
+        out_specs=(vm,) * 4,
+        scratch_shapes=[pltpu.VMEM((D, D), BF), pltpu.SemaphoreType.DMA((1,))],
+    )(meta, tok, maskc, vp, q, k, v, own, *arrays)
 
 
 def ffn_kernel(shapes, plans, nwide, meta, n2, og, x2, vp, own, *refs):
@@ -335,9 +356,12 @@
 
     @pl.when(f == 0)
     def _():
-        for b in range(FFB):
+        def begin(b, carry):
             start_block(meta, 4 + b, own, groups, wup.at[b], sems.at[b])
             start_block(meta, 8 + b, own, groups, wdown.at[b], sems.at[4 + b])
+            return carry
+
+        lax.fori_loop(0, FFB, begin, 0)
         yacc[...] = jnp.zeros_like(yacc)
         dn2_ref[...] = jnp.zeros_like(dn2_ref)
         gbias_ref[FFB : FFB + 1, :] = jnp.sum(og[...].astype(F32), axis=0, keepdims=True)
@@ -556,8 +580,7 @@
     first = split_refs(shapes, refs)
     in_ref, ge_ref, gg_ref = refs[nw : nw + 3]
     wbuf, sems = refs[nw + 3 :]
-    for b in range(3):
-        start_block(meta, b, own, first, wbuf.at[b], sems.at[b])
+    start_blocks(meta, 3, own, first, wbuf, sems)
     for b in range(3):
         wait_block(wbuf.at[b], sems.at[b])
     gg = jnp.zeros((1, D), F32)
@@ -636,23 +659,21 @@
     (left,) = split_refs(shapes, refs)
     out = refs[nw]
     lbuf, gbuf, lsem, gsem = refs[nw + 1 :]
-    for s in range(count):
+
+    def begin(s, carry):
         item = items[s]
-        if len(grads) == 1:
-            pltpu.make_async_copy(grads[0].at[item], gbuf.at[s], gsem.at[s]).start()
-        else:
-
-            @pl.when(item < sizes[0])
-            def _():
-                pltpu.make_async_copy(grads[0].at[item], gbuf.at[s], gsem.at[s]).start()
-
-            @pl.when(item >= sizes[0])
-            def _():
-                pltpu.make_async_copy(
-                    grads[1].at[item - sizes[0]], gbuf.at[s], gsem.at[s]
-                ).start()
-
+        at = 0
+        for ref, size in zip(grads, sizes):
+
+            @pl.when((item >= at) & (item < at + size))
+            def _(ref=ref, at=at):
+                pltpu.make_async_copy(ref.at[item - at], gbuf.at[s], gsem.at[s]).start()
+
+            at += size
         start_slices(left, slots[s], lbuf.at[s], lsem.at[s], meta[0])
+        return carry
+
+    lax.fori_loop(0, count, begin, 0)
     parts = []
     for s in range(count):
         wait_block(gbuf.at[s], gsem.at[s])
@@ -916,7 +937,8 @@
     maskc = masked[0][:, None]
     og = out_grad[0]
 
-    q, k, v, n1, mixed, lse, x2, n2 = run_forward(meta, tok, maskc, vec_all, cos, sin, own, first)
+    q, k, v, n1 = run_qkv(meta, tok, maskc, vec_all, cos, sin, own, first)
+    mixed, lse, x2, n2 = run_forward(meta, tok, maskc, vec_all, q, k, v, own, first)
     layer_out, up_keep, up_send, down_keep, down_send, dn2, gbias = run_ffn(
         meta, n2, og, x2, vec_all, own, groups, (near_y, near_x), nwide
     )
@@ -972,7 +994,8 @@
 
     vec_grad = jnp.concatenate([ge, gg1, gg2, gbias[: FFB + 1]], axis=0)
     vec_grad = butterfly_sum(vec_grad, "narrow", nnarrow, far_bits(nnarrow))
-    vec_grad = butterfly_sum(vec_grad, "wide", nwide, far_order[:-1])
+    for bit in far_order[:-1]:
+        vec_grad = butterfly_sum(vec_grad, "wide", nwide, [bit])
     vec_grad = butterfly_sum(vec_grad, "wide", nwide, far_order[-1:])
     vec_owned = lax.dynamic_slice_in_dim(
         vec_grad.reshape(nnarrow, vectors.shape[0]), n, 1, axis=0

time: 528 us -> 528 us (level)
    pallas_call x0 -> x1, Pallas kernels: none -> 8.16 us  [run_qkv(): pl.pallas_call(partial(qkv_kernel, group_shapes(first)), name='project_qk...]
    pallas_call x1, Pallas kernels: 22.1 us -> 16.6 us  [run_forward(): pl.pallas_call(partial(forward_kernel, group_shapes(first)), name='forwar...]
where the time goes in v2:
time: 528 us; the launch traced here: 520 us
  waiting for transfers between devices  230 us (44%)
  Pallas kernels  162 us (31%)
  starting transfers between devices  71.2 us (13%)
  other arithmetic  42 us (8%)
  local copies, waits for them, and re-layouts  13.5 us (3%)
    ppermute x71, waiting for transfers between devices, xor_permute(): return lax.ppermute(x, axis, [(i, i ^ mask) for i in range(size)])  226 us
    ppermute x71, starting transfers between devices, xor_permute(): return lax.ppermute(x, axis, [(i, i ^ mask) for i in range(size)])  61.5 us
    pallas_call x1, Pallas kernels, run_ffn(): pl.pallas_call(partial(ffn_kernel, group_shapes(groups), plans, nwide), n...  31.8 us
    pallas_call x2, Pallas kernels, run_update(): pl.pallas_call(partial(update_kernel, group_shapes(groups), half, bool(ea...  26 us
    pallas_call x1, Pallas kernels, run_attention_back(): pl.pallas_call(attention_back_kernel, name='attention_back', out_shape=(s...  20 us
    pallas_call x1, Pallas kernels, run_forward(): pl.pallas_call(partial(forward_kernel, group_shapes(first)), name='forwar...  16.6 us
    pallas_call x2, Pallas kernels, run_adam(): pl.pallas_call(partial(adam_kernel, count, bool(earlier)), name='adam_ste...  15.7 us
    convert_element_type x16, other arithmetic, scatter_sum(): got = xor_permute(total.astype(BF), axis, size, bit)  12.5 us
  transfers between devices with their start and end apart: 73, of which 29 were waited for; matrix products, arithmetic and copies ran while one was open for 9% of the time, Pallas kernels for 26%

profile of v2, /device:TPU:0, one launch (start us, length us, event | category | flops | bytes accessed | tf_op | source)
XLA Modules:
  0.0 520.4 jit_solution(14336192593117160649)
XLA Ops:
  3.6 3.4 send_weights.2
  7.0 3.0 collective-permute-start.3
  10.0 1.9 collective-permute-start.1
  12.0 3.3 send_weights.3
  15.3 1.9 collective-permute-start.11
  17.4 2.7 collective-permute-start.4
  20.1 47.8 %collective-permute-done.11 = bf16[2,48,768]{2,1,0:T(8,128)(2,1)S(1)} collective-permute-done((bf16[2,48,768]{2,1,0:T(8,128)(2,1)}, bf16[2,48,768]{2,1,0:T(8,128)(2,1)S(1)}, u32[]{:S(2)}, u32[]{:S(2)}) %collective-permute-start.11) | collective-permute-done | bytes 147488 | tf_op jit(solution)/shard_map/ppermute | solution.py:58
  67.9 2.8 collective-permute-start.12
  70.7 1.6 collective-permute-start.5
  72.4 4.5 collective-permute-done.12
  77.7 4.4 collective-permute-done.5
  84.5 2.3 collective-permute-done.13
  89.7 8.1 %collective-permute-done.6.refs_3_ = bf16[4,2,48,768]{3,2,1,0:T(8,128)(2,1)S(1)} collective-permute-done((bf16[4,2,48,768]{3,2,1,0:T(8,128)(2,1)S(1)}, bf16[4,2,48,768]{3,2,1,0:T(8,128)(2,1)S(1)}, u32[]{:S(2)}, u32[]{:S(2)}) %collective-permute-start.6) | collective-permute-done | bytes 589856 | tf_op jit(solution)/shard_map/ppermute | solution.py:58
  99.3 7.8 %collective-permute-done.14.refs_9_ = bf16[4,2,48,768]{3,2,1,0:T(8,128)(2,1)S(1)} collective-permute-done((bf16[4,2,48,768]{3,2,1,0:T(8,128)(2,1)}, bf16[4,2,48,768]{3,2,1,0:T(8,128)(2,1)S(1)}, u32[]{:S(2)}, u32[]{:S(2)}) %collective-permute-start.14) | collective-permute-done | bytes 589856 | tf_op jit(solution)/shard_map/ppermute | solution.py:58
  111.5 9.8 %convert_element_type.501.own = bf16[8,768,768]{2,1,0:T(8,128)(2,1)} convert(f32[8,768,768]{2,1,0:T(8,128)} %weights.3) | non-fusion elementwise | flops 4718592 | bytes 28311552 | tf_op jit(solution)/shard_map/convert_element_type | solution.py:918
  127.2 8.2 %project_qkv.1 = (bf16[768,768]{1,0:T(8,128)(2,1)}, bf16[768,768]{1,0:T(8,128)(2,1)}, bf16[768,768]{1,0:T(8,128)(2,1)}, bf16[768,768]{1,0:T(8,128)(2,1)}) custom-call(s32[26]{0:T(128)} %pad_add_fusion.meta, bf16[384,768]{1,0:T(8,128)(2,1)} %bitcast.46, s32[384,1]{1,0:T(8,128)} %copy.31.maskc, f32[8,768]{1,0:T(8,128)} %reshape.367.vp, ...), custom_call_target="tpu_custom_call" | custom-call | tf_op jit(solution)/shard_map/project_qkv/pallas_call | solution.py:276
  135.3 16.6 %forward_attention.1 = (bf16[768,768]{1,0:T(8,128)(2,1)}, f32[6,2,768]{2,1,0:T(2,128)}, f32[768,768]{1,0:T(8,128)}, bf16[768,768]{1,0:T(8,128)(2,1)}) custom-call(s32[26]{0:T(128)} %pad_add_fusion.meta, bf16[384,768]{1,0:T(8,128)(2,1)} %bitcast.47, s32[384,1]{1,0:T(8,128)} %copy.31.maskc, f32[8,768]{1,0:T(8,128)} %reshape.367.vp, ...), custom_call_target="tpu_custom_call" | custom-call | tf_op jit(solution)/shard_map/forward_attention/pallas_call | solution.py:334
  152.0 31.8 %feed_forward.1 = (bf16[768,768]{1,0:T(8,128)(2,1)}, bf16[16,2,48,768]{3,2,1,0:T(8,128)(2,1)}, bf16[16,2,48,768]{3,2,1,0:T(8,128)(2,1)}, bf16[16,2,48,768]{3,2,1...) custom-call(s32[26]{0:T(128)} %pad_add_fusion.meta, ...), custom_call_target="tpu_custom_call" | custom-call | tf_op jit(solution)/shard_map/feed_forward/pallas_call | solution.py:417
  184.4 2.4 pad_maximum_fusion.1
  188.3 8.7 %residual_back.1 = (f32[768,768]{1,0:T(8,128)}, bf16[768,768]{1,0:T(8,128)(2,1)}, bf16[768,768]{1,0:T(8,128)(2,1)}, f32[1,768]{1,0:T(1,128)}) custom-call(s32[26]{0:T(128)} %pad_add_fusion.meta, f32[768,768]{1,0:T(8,128)} %get-tuple-element.53.x2, f32[768,768]{1,0:T(8,128)} %get-tuple-element.57.dn2, bf16[768,768]{1,0:T(8,128)(2,1)} %bitcast.50, ...), custom_call_target="tpu_custom_call" | custom-call | tf_op jit(solution)/shard_map/residual_back/pallas_call | solution.py:478
  197.1 20.0 %attention_back.1 = (bf16[768,768]{1,0:T(8,128)(2,1)}, bf16[768,768]{1,0:T(8,128)(2,1)}, bf16[768,768]{1,0:T(8,128)(2,1)}) custom-call(bf16[768,768]{1,0:T(8,128)(2,1)} %get-tuple-element.49.q_ref.q, bf16[768,768]{1,0:T(8,128)(2,1)} %get-tuple-element.50.k_ref.k, bf16[768,768]{1,0:T(8,128)(2,1)} %get-tuple-element.51.v_ref.v, ...), custom_call_target="tpu_custom_call" | custom-call | tf_op jit(solution)/shard_map/attention_back/pallas_call | solution.py:542
  217.1 6.8 %qkv_grad.1 = (bf16[16,1,48,768]{3,2,1,0:T(8,128)(2,1)}, bf16[16,1,48,768]{3,2,1,0:T(8,128)(2,1)}, bf16[16,1,48,768]{3,2,1,0:T(8,128)(2,1)}, bf16[16,1,48,768]{3,2,1,0:T(8,128)(2,1)}) custom-call(s32[26]{0:T(128)} %pad_add_fusion.meta, bf16[768,768]{1,0:T(8,128)(2,1)} %get-tuple-element.66.n1, bf16[768,768]{1,0:T(8,128)(2,1)} %get-tuple-element.62.pq, ...), custom_call_target="tpu_custom_call" | custom-call | tf_op jit(solution)/shard_map/qkv_grad/pallas_call | solution.py:568
  224.0 1.8 pad_maximum_fusion.refs_2_.refs_1_.refs_8_
  227.8 1.7 add_convert_fusion
  229.5 1.6 collective-permute-start.36
  231.1 1.7 add_convert_fusion.1
  235.7 7.8 %collective-permute-done.24 = bf16[8,1,48,768]{3,2,1,0:T(8,128)(2,1)S(1)} collective-permute-done((bf16[8,1,48,768]{3,2,1,0:T(8,128)(2,1)S(1)}, bf16[8,1,48,768]{3,2,1,0:T(8,128)(2,1)S(1)}, u32[]{:S(2)}, u32[]{:S(2)}) %collective-permute-start.24) | collective-permute-done | bytes 589856 | tf_op jit(solution)/shard_map/ppermute | solution.py:58
  243.6 26.5 %collective-permute-done.18 = bf16[8,1,48,768]{3,2,1,0:T(8,128)(2,1)S(1)} collective-permute-done((bf16[8,1,48,768]{3,2,1,0:T(8,128)(2,1)S(1)}, bf16[8,1,48,768]{3,2,1,0:T(8,128)(2,1)S(1)}, u32[]{:S(2)}, u32[]{:S(2)}) %collective-permute-start.18) | collective-permute-done | bytes 589856 | tf_op jit(solution)/shard_map/ppermute | solution.py:58
  270.1 1.6 collective-permute-start.25
  271.8 7.7 %collective-permute-done.43.refs_3_.refs_2_.refs_9_ = bf16[4,8,48,768]{3,2,1,0:T(8,128)(2,1)S(1)} collective-permute-done((bf16[4,8,48,768]{3,2,1,0:T(8,128)(2,1)S(1)}, bf16[4,8,48,768]{3,2,1,0:T(8,128)(2,1)S(1)}, u32[]{:S(2)}, u32[]{:S(2)}) %collective-permute-start.43) | collective-permute-done | bytes 2359328 | tf_op jit(solution)/shard_map/ppermute | solution.py:58
  280.0 1.6 add_convert_fusion.2
  284.2 1.6 collective-permute-start.31
  285.9 3.4 collective-permute-done.19
  290.4 10.2 %collective-permute-done.37 = bf16[4,2,48,768]{3,2,1,0:T(8,128)(2,1)S(1)} collective-permute-done((bf16[4,2,48,768]{3,2,1,0:T(8,128)(2,1)S(1)}, bf16[4,2,48,768]{3,2,1,0:T(8,128)(2,1)S(1)}, u32[]{:S(2)}, u32[]{:S(2)}) %collective-permute-start.37) | collective-permute-done | bytes 589856 | tf_op jit(solution)/shard_map/ppermute | solution.py:58
  306.8 6.9 %collective-permute-done.38 = bf16[2,2,48,768]{3,2,1,0:T(8,128)(2,1)S(1)} collective-permute-done((bf16[2,2,48,768]{3,2,1,0:T(8,128)(2,1)S(1)}, bf16[2,2,48,768]{3,2,1,0:T(8,128)(2,1)S(1)}, u32[]{:S(2)}, u32[]{:S(2)}) %collective-permute-start.38) | collective-permute-done | bytes 294944 | tf_op jit(solution)/shard_map/ppermute | solution.py:58
  316.2 3.5 collective-permute-done.32
  321.3 7.8 %collective-permute-done.39 = bf16[1,2,48,768]{3,2,1,0:T(8,128)(2,1)S(1)} collective-permute-done((bf16[1,2,48,768]{3,2,1,0:T(8,128)(2,1)S(1)}, bf16[1,2,48,768]{3,2,1,0:T(8,128)(2,1)S(1)}, u32[]{:S(2)}, u32[]{:S(2)}) %collective-permute-start.39) | collective-permute-done | bytes 147488 | tf_op jit(solution)/shard_map/ppermute | solution.py:58
  330.1 5.6 %collective-permute-done.33 = bf16[1,2,48,768]{3,2,1,0:T(8,128)(2,1)S(1)} collective-permute-done((bf16[1,2,48,768]{3,2,1,0:T(8,128)(2,1)S(1)}, bf16[1,2,48,768]{3,2,1,0:T(8,128)(2,1)S(1)}, u32[]{:S(2)}, u32[]{:S(2)}) %collective-permute-start.33) | collective-permute-done | bytes 147488 | tf_op jit(solution)/shard_map/ppermute | solution.py:58
  335.7 1.6 collective-permute-start.40
  340.9 2.7 collective-permute-done.34
  347.2 5.9 %gradient_turn.3 = bf16[768,192]{1,0:T(8,128)(2,1)} custom-call(s32[26]{0:T(128)} %pad_add_fusion.meta, s32[4]{0:T(128)} %get-tuple-element.102.items, s32[4]{0:T(128)} %get-tuple-element.111.slots, bf16[8,48,768]{2,1,0:T(8,128)(2,1)} %pad_maximum_fusion.4.refs_1_.refs_0_, bf16[4,8,48,768]{3,2,1,0:T(8,128)(2,1)} %copy-done, ...), custom_call_target="tpu_custom_call" | custom-call | tf_op jit(solution)/shard_map/gradient_turn/pallas_call | solution.py:690
  353.1 3.8 all-to-all-start.1
  359.6 1.6 collective-permute-start.22
  361.2 1.7 collective-permute-done.28
  364.9 5.9 %gradient_turn.2 = bf16[768,192]{1,0:T(8,128)(2,1)} custom-call(s32[26]{0:T(128)} %pad_add_fusion.meta, s32[4]{0:T(128)} %get-tuple-element.103.items, s32[4]{0:T(128)} %get-tuple-element.110.slots, bf16[4,48,768]{2,1,0:T(8,128)(2,1)} %pad_maximum_fusion.11.refs_0_, bf16[8,48,768]{2,1,0:T(8,128)(2,1)} %pad_maximum_fusion.4.refs_1_.refs_0_, ...), custom_call_target="tpu_custom_call" | custom-call | tf_op jit(solution)/shard_map/gradient_turn/pallas_call | solution.py:690
  370.8 5.9 %all-to-all-start = ((bf16[16,48,192]{2,1,0:T(8,128)(2,1)}), bf16[16,48,192]{2,1,0:T(8,128)(2,1)S(1)}, u32[]{:S(2)}, u32[]{:S(2)}) async-start(bf16[16,48,192]{2,1,0:T(8,128)(2,1)} %bitcast.52), calls=%async_computation | async-start | bytes 786432 | tf_op jit(solution)/shard_map/all_to_all | solution.py:981
  377.3 7.5 %adam_step.2 = (f32[8,48,768]{2,1,0:T(8,128)}, f32[8,48,768]{2,1,0:T(8,128)}, bf16[4,48,768]{2,1,0:T(8,128)(2,1)}) custom-call(s32[4]{0:T(128)} %get-tuple-element.111.slots, s32[4]{0:T(128)} %get-tuple-element.104.live, bf16[768,192]{1,0:T(8,128)(2,1)} %bitcast.53, f32[8,48,768]{2,1,0:T(8,128)} %first.3, f32[8,48,768]{2,1,0:T(8,128)} %second.3, ...), custom_call_target="tpu_custom_call" | custom-call | tf_op jit(solution)/shard_map/adam_step/pallas_call | solution.py:739
  384.8 4.1 all-to-all-done
  389.6 8.3 %adam_step.3 = (f32[8,48,768]{2,1,0:T(8,128)}, f32[8,48,768]{2,1,0:T(8,128)}, bf16[4,48,768]{2,1,0:T(8,128)(2,1)}) custom-call(s32[4]{0:T(128)} %get-tuple-element.110.slots, s32[4]{0:T(128)} %get-tuple-element.105.live, bf16[768,192]{1,0:T(8,128)(2,1)} %bitcast.54, f32[8,48,768]{2,1,0:T(8,128)} %first.3, ...), custom_call_target="tpu_custom_call", output_to_operand_aliasing={{0}: (6, {}), {1}: (7, {})} | custom-call | tf_op jit(solution)/shard_map/adam_step/pallas_call | solution.py:739
  398.9 1.8 collective-permute-start.46
  402.0 9.9 %input_grad.1 = (bf16[384,768]{1,0:T(8,128)(2,1)}, f32[1,768]{1,0:T(1,128)}, f32[1,768]{1,0:T(1,128)}) custom-call(s32[26]{0:T(128)} %pad_add_fusion.meta, bf16[384,768]{1,0:T(8,128)(2,1)} %bitcast.48, s32[384,1]{1,0:T(8,128)} %copy.31.maskc, f32[8,768]{1,0:T(8,128)} %reshape.367.vp, f32[768,768]{1,0:T(8,128)} %get-tuple-element.59.dx2, ...), custom_call_target="tpu_custom_call" | custom-call | tf_op jit(solution)/shard_map/input_grad/pallas_call | solution.py:607
  411.9 1.8 collective-permute-start.51
  413.9 1.6 collective-permute-done.56
  417.6 3.5 collective-permute-start.61
  422.8 6.7 %collective-permute-done.47 = bf16[2,2,48,768]{3,2,1,0:T(8,128)(2,1)S(1)} collective-permute-done((bf16[2,2,48,768]{3,2,1,0:T(8,128)(2,1)S(1)}, bf16[2,2,48,768]{3,2,1,0:T(8,128)(2,1)S(1)}, u32[]{:S(2)}, u32[]{:S(2)}) %collective-permute-start.47) | collective-permute-done | bytes 294944 | tf_op jit(solution)/shard_map/ppermute | solution.py:58
  429.7 4.5 collective-permute-done.57
  436.6 4.7 collective-permute-done.67
  441.3 3.8 collective-permute-done.68
  446.0 16.3 %collective-permute-done.69 = f32[8,768]{1,0:T(8,128)S(1)} collective-permute-done((f32[8,768]{1,0:T(8,128)S(1)}, f32[8,768]{1,0:T(8,128)S(1)}, u32[]{:S(2)}, u32[]{:S(2)}) %collective-permute-start.69) | collective-permute-done | bytes 24608 | tf_op jit(solution)/shard_map/ppermute | solution.py:58
  462.7 2.1 collective-permute-start.63
  465.4 13.5 %collective-permute-done.53.refs_5_ = bf16[4,2,48,768]{3,2,1,0:T(8,128)(2,1)} collective-permute-done((bf16[4,2,48,768]{3,2,1,0:T(8,128)(2,1)S(1)}, bf16[4,2,48,768]{3,2,1,0:T(8,128)(2,1)}, u32[]{:S(2)}, u32[]{:S(2)}) %collective-permute-start.53) | collective-permute-done | bytes 589856 | tf_op jit(solution)/shard_map/ppermute | solution.py:58
  478.9 12.0 %collective-permute-done.63.refs_5_ = bf16[4,2,48,768]{3,2,1,0:T(8,128)(2,1)S(1)} collective-permute-done((bf16[4,2,48,768]{3,2,1,0:T(8,128)(2,1)S(1)}, bf16[4,2,48,768]{3,2,1,0:T(8,128)(2,1)S(1)}, u32[]{:S(2)}, u32[]{:S(2)}) %collective-permute-start.63) | collective-permute-done | bytes 589856 | tf_op jit(solution)/shard_map/ppermute | solution.py:58
  494.1 12.6 %weight_update.2.refs_12_ = f32[8,768,768]{2,1,0:T(8,128)} custom-call(s32[4]{0:T(128)} %get-tuple-element.111.slots, s32[4]{0:T(128)} %get-tuple-element.104.live, s32[26]{0:T(128)} %pad_add_fusion.meta, f32[8,768,768]{2,1,0:T(8,128)} %weights.3, bf16[4,2,48,768]{3,2,1,0:T(8,128)(2,1)} %copy-done.14, bf16[4,2,48,768]{3,2,1,0:T(8,128)(2,1)} %copy-done.27, ...), custom_call_target="tpu_custom_call" | custom-call | tf_op jit(solution)/shard_map/weight_update/pallas_call | solution.py:809
  506.8 13.4 %weight_update.3 = f32[8,768,768]{2,1,0:T(8,128)} custom-call(s32[4]{0:T(128)} %get-tuple-element.110.slots, s32[4]{0:T(128)} %get-tuple-element.105.live, s32[26]{0:T(128)} %pad_add_fusion.meta, f32[8,768,768]{2,1,0:T(8,128)} %weights.3, bf16[4,2,48,768]{3,2,1,0:T(8,128)(2,1)} %copy-done.16, ...), custom_call_target="tpu_custom_call", output_to_operand_aliasing={{}: (16, {})} | custom-call | tf_op jit(solution)/shard_map/weight_update/pallas_call | solution.py:809
  (268 shorter events, 70.6 us)
Async XLA Ops:
  7.0 10.4 %collective-permute-start.3 = (bf16[2,48,768]{2,1,0:T(8,128)(2,1)}, bf16[2,48,768]{2,1,0:T(8,128)(2,1)S(1)}, u32[]{:S(2)}, u32[]{:S(2)}) collective-permute-start(bf16[2,48,768]{2,1,0:T(8,128)(2,1)} %get-tuple-element.48), channel_id=1, source_target_pairs={{0,1},{1,0},{2,3},{3,2},{4,5},{5,4},{6,7},{7,6},{8,9},{9,8},{10,11... | collective-permute-start | bytes 442376 | tf_op jit(solution)/shard_map/ppermute | solution.py:58
  10.0 77.7 %collective-permute-start = (bf16[3072]{0:T(1024)(128)(2,1)S(1)}, bf16[3072]{0:T(1024)(128)(2,1)}, u32[]{:S(2)}, u32[]{:S(2)}) collective-permute-start(bf16[3072]{0:T(1024)(128)(2,1)S(1)} %convert_element_type.497), channel_id=1, source_target_pairs={{0,1},{1,0},{2,3},{3,2},{4,5},{5,4},{6,7},{7,6},{8,9},{9,8},{10,11... | collective-permute-start | bytes 18440 | tf_op jit(solution)/shard_map/ppermute | solution.py:58
  10.0 79.1 %collective-permute-start.1 = (bf16[2,384,768]{2,1,0:T(8,128)(2,1)}, bf16[2,384,768]{2,1,0:T(8,128)(2,1)S(1)}, u32[]{:S(2)}, u32[]{:S(2)}) collective-permute-start(bf16[2,384,768]{2,1,0:T(8,128)(2,1)} %get-tuple-element.47), channel_id=1, source_target_pairs={{0,1},{1,0},{2,3},{3,2},{4,5},{5,4},{6,7},{7,6},{8,9},{9,8},{10,11... | collective-permute-start | bytes 3538952 | tf_op jit(solution)/shard_map/ppermute | solution.py:58
  15.2 74.2 %collective-permute-start.9 = (bf16[2,384,768]{2,1,0:T(8,128)(2,1)}, bf16[2,384,768]{2,1,0:T(8,128)(2,1)}, u32[]{:S(2)}, u32[]{:S(2)}) collective-permute-start(bf16[2,384,768]{2,1,0:T(8,128)(2,1)} %get-tuple-element.54), channel_id=1, source_target_pairs={{0,1},{1,0},{2,3},{3,2},{4,5},{5,4},{6,7},{7,6},{8,9},{9,8},{10,11... | collective-permute-start | bytes 3538952 | tf_op jit(solution)/shard_map/ppermute | solution.py:58
  15.3 52.5 %collective-permute-start.11 = (bf16[2,48,768]{2,1,0:T(8,128)(2,1)}, bf16[2,48,768]{2,1,0:T(8,128)(2,1)S(1)}, u32[]{:S(2)}, u32[]{:S(2)}) collective-permute-start(bf16[2,48,768]{2,1,0:T(8,128)(2,1)} %get-tuple-element.55), channel_id=1, source_target_pairs={{0,1},{1,0},{2,3},{3,2},{4,5},{5,4},{6,7},{7,6},{8,9},{9,8},{10,11... | collective-permute-start | bytes 442376 | tf_op jit(solution)/shard_map/ppermute | solution.py:58
  17.4 53.3 %collective-permute-start.4 = (bf16[1,2,48,768]{3,2,1,0:T(8,128)(2,1)S(1)}, bf16[1,2,48,768]{3,2,1,0:T(8,128)(2,1)S(1)}, u32[]{:S(2)}, u32[]{:S(2)}) collective-permute-start(bf16[1,2,48,768]{3,2,1,0:T(8,128)(2,1)S(1)} %bitcast.55), channel_id=1, source_target_pairs={{0,16},{2,18},{4,20},{6,22},{8,24},{10,26},{12,28},{14,30},{16,0},... | collective-permute-start | bytes 442376 | tf_op jit(solution)/shard_map/ppermute | solution.py:58
  67.9 9.1 %collective-permute-start.12 = (bf16[1,2,48,768]{3,2,1,0:T(8,128)(2,1)S(1)}, bf16[1,2,48,768]{3,2,1,0:T(8,128)(2,1)S(1)}, u32[]{:S(2)}, u32[]{:S(2)}) collective-permute-start(bf16[1,2,48,768]{3,2,1,0:T(8,128)(2,1)S(1)} %bitcast.58), channel_id=1, source_target_pairs={{0,16},{2,18},{4,20},{6,22},{8,24},{10,26},{12,28},{14,30},{16,0},... | collective-permute-start | bytes 442376 | tf_op jit(solution)/shard_map/ppermute | solution.py:58
  70.7 11.3 %collective-permute-start.5 = (bf16[2,2,48,768]{3,2,1,0:T(8,128)(2,1)S(1)}, bf16[2,2,48,768]{3,2,1,0:T(8,128)(2,1)S(1)}, u32[]{:S(2)}, u32[]{:S(2)}) collective-permute-start(bf16[2,2,48,768]{3,2,1,0:T(8,128)(2,1)S(1)} %pad_maximum_fusion.9), channel_id=1, source_target_pairs={{0,8},{2,10},{4,12},{6,14},{8,0},{10,2},{12,4},{14,6},{16,24},{18,... | collective-permute-start | bytes 884744 | tf_op jit(solution)/shard_map/ppermute | solution.py:58
  77.0 9.8 %collective-permute-start.13 = (bf16[2,2,48,768]{3,2,1,0:T(8,128)(2,1)S(1)}, bf16[2,2,48,768]{3,2,1,0:T(8,128)(2,1)S(1)}, u32[]{:S(2)}, u32[]{:S(2)}) collective-permute-start(bf16[2,2,48,768]{3,2,1,0:T(8,128)(2,1)S(1)} %pad_maximum_fusion.10), channel_id=1, source_target_pairs={{0,8},{2,10},{4,12},{6,14},{8,0},{10,2},{12,4},{14,6},{16,24},{18,... | collective-permute-start | bytes 884744 | tf_op jit(solution)/shard_map/ppermute | solution.py:58
  82.1 15.7 %collective-permute-start.6 = (bf16[4,2,48,768]{3,2,1,0:T(8,128)(2,1)S(1)}, bf16[4,2,48,768]{3,2,1,0:T(8,128)(2,1)S(1)}, u32[]{:S(2)}, u32[]{:S(2)}) collective-permute-start(bf16[4,2,48,768]{3,2,1,0:T(8,128)(2,1)S(1)} %pad_maximum_fusion.2.refs_2_), channel_id=1, source_target_pairs={{0,4},{2,6},{4,0},{6,2},{8,12},{10,14},{12,8},{14,10},{16,20},{18,... | collective-permute-start | bytes 1769480 | tf_op jit(solution)/shard_map/ppermute | solution.py:58
  86.8 12.0 %collective-permute-start.7 = (bf16[4,2,48,768]{3,2,1,0:T(8,128)(2,1)S(1)}, bf16[4,2,48,768]{3,2,1,0:T(8,128)(2,1)S(1)}, u32[]{:S(2)}, u32[]{:S(2)}) collective-permute-start(bf16[4,2,48,768]{3,2,1,0:T(8,128)(2,1)S(1)} %pad_maximum_fusion.2.refs_2_), channel_id=1, source_target_pairs={{0,2},{2,0},{4,6},{6,4},{8,10},{10,8},{12,14},{14,12},{16,18},{18,... | collective-permute-start | bytes 1769480 | tf_op jit(solution)/shard_map/ppermute | solution.py:58
  87.7 19.4 %collective-permute-start.14 = (bf16[4,2,48,768]{3,2,1,0:T(8,128)(2,1)}, bf16[4,2,48,768]{3,2,1,0:T(8,128)(2,1)S(1)}, u32[]{:S(2)}, u32[]{:S(2)}) collective-permute-start(bf16[4,2,48,768]{3,2,1,0:T(8,128)(2,1)} %pad_maximum_fusion.3.refs_8_), channel_id=1, source_target_pairs={{0,4},{2,6},{4,0},{6,2},{8,12},{10,14},{12,8},{14,10},{16,20},{18,... | collective-permute-start | bytes 1769480 | tf_op jit(solution)/shard_map/ppermute | solution.py:58
  89.2 37.0 %collective-permute-start.2 = (bf16[1,2,384,768]{3,2,1,0:T(8,128)(2,1)S(1)}, bf16[1,2,384,768]{3,2,1,0:T(8,128)(2,1)S(1)}, u32[]{:S(2)}, u32[]{:S(2)}) collective-permute-start(bf16[1,2,384,768]{3,2,1,0:T(8,128)(2,1)S(1)} %bitcast.40), channel_id=1, source_target_pairs={{0,2},{2,0},{4,6},{6,4},{8,10},{10,8},{12,14},{14,12},{16,18},{18,... | collective-permute-start | bytes 3538952 | tf_op jit(solution)/shard_map/ppermute | solution.py:58
  89.4 62.6 %collective-permute-start.10 = (bf16[1,2,384,768]{3,2,1,0:T(8,128)(2,1)}, bf16[1,2,384,768]{3,2,1,0:T(8,128)(2,1)}, u32[]{:S(2)}, u32[]{:S(2)}) collective-permute-start(bf16[1,2,384,768]{3,2,1,0:T(8,128)(2,1)} %bitcast.9.refs_6_), channel_id=1, source_target_pairs={{0,2},{2,0},{4,6},{6,4},{8,10},{10,8},{12,14},{14,12},{16,18},{18,... | collective-permute-start | bytes 3538952 | tf_op jit(solution)/shard_map/ppermute | solution.py:58
  97.8 11.0 %collective-permute-start.8 = (bf16[4,2,48,768]{3,2,1,0:T(8,128)(2,1)S(1)}, bf16[4,2,48,768]{3,2,1,0:T(8,128)(2,1)S(1)}, u32[]{:S(2)}, u32[]{:S(2)}) collective-permute-start(bf16[4,2,48,768]{3,2,1,0:T(8,128)(2,1)S(1)} %collective-permute-done.6.refs_3_), channel_id=1, source_target_pairs={{0,2},{2,0},{4,6},{6,4},{8,10},{10,8},{12,14},{14,12},{16,18},{18,... | collective-permute-start | bytes 1769480 | tf_op jit(solution)/shard_map/ppermute | solution.py:58
  98.8 53.1 %collective-permute-start.15 = (bf16[4,2,48,768]{3,2,1,0:T(8,128)(2,1)}, bf16[4,2,48,768]{3,2,1,0:T(8,128)(2,1)}, u32[]{:S(2)}, u32[]{:S(2)}) collective-permute-start(bf16[4,2,48,768]{3,2,1,0:T(8,128)(2,1)} %pad_maximum_fusion.3.refs_8_), channel_id=1, source_target_pairs={{0,2},{2,0},{4,6},{6,4},{8,10},{10,8},{12,14},{14,12},{16,18},{18,... | collective-permute-start | bytes 1769480 | tf_op jit(solution)/shard_map/ppermute | solution.py:58
  107.1 44.9 %collective-permute-start.16 = (bf16[4,2,48,768]{3,2,1,0:T(8,128)(2,1)S(1)}, bf16[4,2,48,768]{3,2,1,0:T(8,128)(2,1)}, u32[]{:S(2)}, u32[]{:S(2)}) collective-permute-start(bf16[4,2,48,768]{3,2,1,0:T(8,128)(2,1)S(1)} %collective-permute-done.14.refs_9_), channel_id=1, source_target_pairs={{0,2},{2,0},{4,6},{6,4},{8,10},{10,8},{12,14},{14,12},{16,18},{18,... | collective-permute-start | bytes 1769480 | tf_op jit(solution)/shard_map/ppermute | solution.py:58
  108.9 75.6 %collective-permute-start.41 = (bf16[1,8,48,768]{3,2,1,0:T(8,128)(2,1)}, bf16[1,8,48,768]{3,2,1,0:T(8,128)(2,1)S(1)}, u32[]{:S(2)}, u32[]{:S(2)}) collective-permute-start(bf16[1,8,48,768]{3,2,1,0:T(8,128)(2,1)} %convert_bitcast_fusion), channel_id=1, source_target_pairs={{0,16},{2,18},{4,20},{6,22},{8,24},{10,26},{12,28},{14,30},{16,0},... | collective-permute-start | bytes 1769480 | tf_op jit(solution)/shard_map/ppermute | solution.py:58
  183.8 43.9 %collective-permute-start.35 = (bf16[16,2,48,768]{3,2,1,0:T(8,128)(2,1)}, bf16[16,2,48,768]{3,2,1,0:T(8,128)(2,1)}, u32[]{:S(2)}, u32[]{:S(2)}) collective-permute-start(bf16[16,2,48,768]{3,2,1,0:T(8,128)(2,1)} %get-tuple-element.75), channel_id=1, source_target_pairs={{0,2},{2,0},{4,6},{6,4},{8,10},{10,8},{12,14},{14,12},{16,18},{18,... | collective-permute-start | bytes 7077896 | tf_op jit(solution)/shard_map/ppermute | solution.py:58
  184.1 47.0 %collective-permute-start.29 = (bf16[16,2,48,768]{3,2,1,0:T(8,128)(2,1)}, bf16[16,2,48,768]{3,2,1,0:T(8,128)(2,1)}, u32[]{:S(2)}, u32[]{:S(2)}) collective-permute-start(bf16[16,2,48,768]{3,2,1,0:T(8,128)(2,1)} %get-tuple-element.73), channel_id=1, source_target_pairs={{0,2},{2,0},{4,6},{6,4},{8,10},{10,8},{12,14},{14,12},{16,18},{18,... | collective-permute-start | bytes 7077896 | tf_op jit(solution)/shard_map/ppermute | solution.py:58
  186.8 37.1 %collective-permute-start.42 = (bf16[2,8,48,768]{3,2,1,0:T(8,128)(2,1)}, bf16[2,8,48,768]{3,2,1,0:T(8,128)(2,1)}, u32[]{:S(2)}, u32[]{:S(2)}) collective-permute-start(bf16[2,8,48,768]{3,2,1,0:T(8,128)(2,1)} %pad_maximum_fusion.1), channel_id=1, source_target_pairs={{0,4},{2,6},{4,0},{6,2},{8,12},{10,14},{12,8},{14,10},{16,20},{18,... | collective-permute-start | bytes 3538952 | tf_op jit(solution)/shard_map/ppermute | solution.py:58
  225.8 53.7 %collective-permute-start.43 = (bf16[4,8,48,768]{3,2,1,0:T(8,128)(2,1)S(1)}, bf16[4,8,48,768]{3,2,1,0:T(8,128)(2,1)S(1)}, u32[]{:S(2)}, u32[]{:S(2)}) collective-permute-start(bf16[4,8,48,768]{3,2,1,0:T(8,128)(2,1)S(1)} %pad_maximum_fusion.refs_2_.refs_1_.refs_8_), channel_id=1, source_target_pairs={{0,8},{2,10},{4,12},{6,14},{8,0},{10,2},{12,4},{14,6},{16,24},{18,... | collective-permute-start | bytes 7077896 | tf_op jit(solution)/shard_map/ppermute | solution.py:58
  226.9 7.6 %collective-permute-start.17 = (bf16[16,1,48,768]{3,2,1,0:T(8,128)(2,1)S(1)}, bf16[16,1,48,768]{3,2,1,0:T(8,128)(2,1)S(1)}, u32[]{:S(2)}, u32[]{:S(2)}) collective-permute-start(bf16[16,1,48,768]{3,2,1,0:T(8,128)(2,1)S(1)} %copy-done.47), channel_id=1, source_target_pairs={{0,2},{2,0},{4,6},{6,4},{8,10},{10,8},{12,14},{14,12},{16,18},{18,... | collective-permute-start | bytes 3538952 | tf_op jit(solution)/shard_map/ppermute | solution.py:58
  227.2 16.3 %collective-permute-start.24 = (bf16[8,1,48,768]{3,2,1,0:T(8,128)(2,1)S(1)}, bf16[8,1,48,768]{3,2,1,0:T(8,128)(2,1)S(1)}, u32[]{:S(2)}, u32[]{:S(2)}) collective-permute-start(bf16[8,1,48,768]{3,2,1,0:T(8,128)(2,1)S(1)} %add_convert_fusion.4), channel_id=1, source_target_pairs={{0,4},{2,6},{4,0},{6,2},{8,12},{10,14},{12,8},{14,10},{16,20},{18,... | collective-permute-start | bytes 1769480 | tf_op jit(solution)/shard_map/ppermute | solution.py:58
  229.5 50.5 %collective-permute-start.36 = (bf16[8,2,48,768]{3,2,1,0:T(8,128)(2,1)S(1)}, bf16[8,2,48,768]{3,2,1,0:T(8,128)(2,1)S(1)}, u32[]{:S(2)}, u32[]{:S(2)}) collective-permute-start(bf16[8,2,48,768]{3,2,1,0:T(8,128)(2,1)S(1)} %add_convert_fusion), channel_id=1, source_target_pairs={{0,1},{1,0},{2,3},{3,2},{4,5},{5,4},{6,7},{7,6},{8,9},{9,8},{10,11... | collective-permute-start | bytes 3538952 | tf_op jit(solution)/shard_map/ppermute | solution.py:58
  232.8 48.8 %collective-permute-start.30 = (bf16[8,2,48,768]{3,2,1,0:T(8,128)(2,1)S(1)}, bf16[8,2,48,768]{3,2,1,0:T(8,128)(2,1)S(1)}, u32[]{:S(2)}, u32[]{:S(2)}) collective-permute-start(bf16[8,2,48,768]{3,2,1,0:T(8,128)(2,1)S(1)} %add_convert_fusion.1), channel_id=1, source_target_pairs={{0,4},{2,6},{4,0},{6,2},{8,12},{10,14},{12,8},{14,10},{16,20},{18,... | collective-permute-start | bytes 3538952 | tf_op jit(solution)/shard_map/ppermute | solution.py:58
  234.6 35.5 %collective-permute-start.18 = (bf16[8,1,48,768]{3,2,1,0:T(8,128)(2,1)S(1)}, bf16[8,1,48,768]{3,2,1,0:T(8,128)(2,1)S(1)}, u32[]{:S(2)}, u32[]{:S(2)}) collective-permute-start(bf16[8,1,48,768]{3,2,1,0:T(8,128)(2,1)S(1)} %add_convert_fusion.5), channel_id=1, source_target_pairs={{0,1},{1,0},{2,3},{3,2},{4,5},{5,4},{6,7},{7,6},{8,9},{9,8},{10,11... | collective-permute-start | bytes 1769480 | tf_op jit(solution)/shard_map/ppermute | solution.py:58
  243.5 101.0 %collective-permute-start.44 = (bf16[4,8,48,768]{3,2,1,0:T(8,128)(2,1)S(1)}, bf16[4,8,48,768]{3,2,1,0:T(8,128)(2,1)S(1)}, u32[]{:S(2)}, u32[]{:S(2)}) collective-permute-start(bf16[4,8,48,768]{3,2,1,0:T(8,128)(2,1)S(1)} %pad_maximum_fusion.refs_2_.refs_1_.refs_8_), channel_id=1, source_target_pairs={{0,2},{2,0},{4,6},{6,4},{8,10},{10,8},{12,14},{14,12},{16,18},{18,... | collective-permute-start | bytes 7077896 | tf_op jit(solution)/shard_map/ppermute | solution.py:58
  270.1 14.1 %collective-permute-start.25 = (bf16[4,1,48,768]{3,2,1,0:T(8,128)(2,1)S(1)}, bf16[4,1,48,768]{3,2,1,0:T(8,128)(2,1)S(1)}, u32[]{:S(2)}, u32[]{:S(2)}) collective-permute-start(bf16[4,1,48,768]{3,2,1,0:T(8,128)(2,1)S(1)} %add_convert_fusion.8), channel_id=1, source_target_pairs={{0,1},{1,0},{2,3},{3,2},{4,5},{5,4},{6,7},{7,6},{8,9},{9,8},{10,11... | collective-permute-start | bytes 884744 | tf_op jit(solution)/shard_map/ppermute | solution.py:58
  279.5 9.9 %collective-permute-start.19 = (bf16[4,1,48,768]{3,2,1,0:T(8,128)(2,1)S(1)}, bf16[4,1,48,768]{3,2,1,0:T(8,128)(2,1)S(1)}, u32[]{:S(2)}, u32[]{:S(2)}) collective-permute-start(bf16[4,1,48,768]{3,2,1,0:T(8,128)(2,1)S(1)} %add_convert_fusion.9), channel_id=1, source_target_pairs={{0,4},{2,6},{4,0},{6,2},{8,12},{10,14},{12,8},{14,10},{16,20},{18,... | collective-permute-start | bytes 884744 | tf_op jit(solution)/shard_map/ppermute | solution.py:58
  280.0 64.5 %collective-permute-start.45 = (bf16[4,8,48,768]{3,2,1,0:T(8,128)(2,1)S(1)}, bf16[4,8,48,768]{3,2,1,0:T(8,128)(2,1)S(1)}, u32[]{:S(2)}, u32[]{:S(2)}) collective-permute-start(bf16[4,8,48,768]{3,2,1,0:T(8,128)(2,1)S(1)} %collective-permute-done.43.refs_3_.refs_2_.refs_9_), channel_id=1, source_target_pairs={{0,2},{2,0},{4,6},{6,4},{8,10},{10,8},{12,14},{14,12},{16,18},{18,... | collective-permute-start | bytes 7077896 | tf_op jit(solution)/shard_map/ppermute | solution.py:58
  281.6 19.0 %collective-permute-start.37 = (bf16[4,2,48,768]{3,2,1,0:T(8,128)(2,1)S(1)}, bf16[4,2,48,768]{3,2,1,0:T(8,128)(2,1)S(1)}, u32[]{:S(2)}, u32[]{:S(2)}) collective-permute-start(bf16[4,2,48,768]{3,2,1,0:T(8,128)(2,1)S(1)} %add_convert_fusion.2), channel_id=1, source_target_pairs={{0,4},{2,6},{4,0},{6,2},{8,12},{10,14},{12,8},{14,10},{16,20},{18,... | collective-permute-start | bytes 1769480 | tf_op jit(solution)/shard_map/ppermute | solution.py:58
  284.2 18.6 %collective-permute-start.31 = (bf16[4,2,48,768]{3,2,1,0:T(8,128)(2,1)S(1)}, bf16[4,2,48,768]{3,2,1,0:T(8,128)(2,1)S(1)}, u32[]{:S(2)}, u32[]{:S(2)}) collective-permute-start(bf16[4,2,48,768]{3,2,1,0:T(8,128)(2,1)S(1)} %add_convert_fusion.3), channel_id=1, source_target_pairs={{0,1},{1,0},{2,3},{3,2},{4,5},{5,4},{6,7},{7,6},{8,9},{9,8},{10,11... | collective-permute-start | bytes 1769480 | tf_op jit(solution)/shard_map/ppermute | solution.py:58
  289.4 15.6 %collective-permute-start.26 = (bf16[2,1,48,768]{3,2,1,0:T(8,128)(2,1)S(1)}, bf16[2,1,48,768]{3,2,1,0:T(8,128)(2,1)S(1)}, u32[]{:S(2)}, u32[]{:S(2)}) collective-permute-start(bf16[2,1,48,768]{3,2,1,0:T(8,128)(2,1)S(1)} %add_convert_fusion.14), channel_id=1, source_target_pairs={{0,8},{2,10},{4,12},{6,14},{8,0},{10,2},{12,4},{14,6},{16,24},{18,... | collective-permute-start | bytes 442376 | tf_op jit(solution)/shard_map/ppermute | solution.py:58
  300.6 37.7 %collective-permute-start.20 = (bf16[2,1,48,768]{3,2,1,0:T(8,128)(2,1)S(1)}, bf16[2,1,48,768]{3,2,1,0:T(8,128)(2,1)S(1)}, u32[]{:S(2)}, u32[]{:S(2)}) collective-permute-start(bf16[2,1,48,768]{3,2,1,0:T(8,128)(2,1)S(1)} %add_convert_fusion.15), channel_id=1, source_target_pairs={{0,8},{2,10},{4,12},{6,14},{8,0},{10,2},{12,4},{14,6},{16,24},{18,... | collective-permute-start | bytes 442376 | tf_op jit(solution)/shard_map/ppermute | solution.py:58
  302.8 10.9 %collective-permute-start.38 = (bf16[2,2,48,768]{3,2,1,0:T(8,128)(2,1)S(1)}, bf16[2,2,48,768]{3,2,1,0:T(8,128)(2,1)S(1)}, u32[]{:S(2)}, u32[]{:S(2)}) collective-permute-start(bf16[2,2,48,768]{3,2,1,0:T(8,128)(2,1)S(1)} %add_convert_fusion.6), channel_id=1, source_target_pairs={{0,8},{2,10},{4,12},{6,14},{8,0},{10,2},{12,4},{14,6},{16,24},{18,... | collective-permute-start | bytes 884744 | tf_op jit(solution)/shard_map/ppermute | solution.py:58
  305.0 14.7 %collective-permute-start.32 = (bf16[2,2,48,768]{3,2,1,0:T(8,128)(2,1)S(1)}, bf16[2,2,48,768]{3,2,1,0:T(8,128)(2,1)S(1)}, u32[]{:S(2)}, u32[]{:S(2)}) collective-permute-start(bf16[2,2,48,768]{3,2,1,0:T(8,128)(2,1)S(1)} %add_convert_fusion.7), channel_id=1, source_target_pairs={{0,8},{2,10},{4,12},{6,14},{8,0},{10,2},{12,4},{14,6},{16,24},{18,... | collective-permute-start | bytes 884744 | tf_op jit(solution)/shard_map/ppermute | solution.py:58
  313.7 43.2 %collective-permute-start.27 = (bf16[1,1,48,768]{3,2,1,0:T(8,128)(2,1)}, bf16[1,1,48,768]{3,2,1,0:T(8,128)(2,1)}, u32[]{:S(2)}, u32[]{:S(2)}) collective-permute-start(bf16[1,1,48,768]{3,2,1,0:T(8,128)(2,1)} %add_convert_fusion.18), channel_id=1, source_target_pairs={{0,16},{2,18},{4,20},{6,22},{8,24},{10,26},{12,28},{14,30},{16,0},... | collective-permute-start | bytes 221192 | tf_op jit(solution)/shard_map/ppermute | solution.py:58
  319.7 9.4 %collective-permute-start.39 = (bf16[1,2,48,768]{3,2,1,0:T(8,128)(2,1)S(1)}, bf16[1,2,48,768]{3,2,1,0:T(8,128)(2,1)S(1)}, u32[]{:S(2)}, u32[]{:S(2)}) collective-permute-start(bf16[1,2,48,768]{3,2,1,0:T(8,128)(2,1)S(1)} %add_convert_fusion.12), channel_id=1, source_target_pairs={{0,16},{2,18},{4,20},{6,22},{8,24},{10,26},{12,28},{14,30},{16,0},... | collective-permute-start | bytes 442376 | tf_op jit(solution)/shard_map/ppermute | solution.py:58
  329.1 6.6 %collective-permute-start.33 = (bf16[1,2,48,768]{3,2,1,0:T(8,128)(2,1)S(1)}, bf16[1,2,48,768]{3,2,1,0:T(8,128)(2,1)S(1)}, u32[]{:S(2)}, u32[]{:S(2)}) collective-permute-start(bf16[1,2,48,768]{3,2,1,0:T(8,128)(2,1)S(1)} %add_convert_fusion.13), channel_id=1, source_target_pairs={{0,16},{2,18},{4,20},{6,22},{8,24},{10,26},{12,28},{14,30},{16,0},... | collective-permute-start | bytes 442376 | tf_op jit(solution)/shard_map/ppermute | solution.py:58
  340.9 17.7 %collective-permute-start.21 = (bf16[1,1,48,768]{3,2,1,0:T(8,128)(2,1)}, bf16[1,1,48,768]{3,2,1,0:T(8,128)(2,1)}, u32[]{:S(2)}, u32[]{:S(2)}) collective-permute-start(bf16[1,1,48,768]{3,2,1,0:T(8,128)(2,1)} %add_convert_fusion.19), channel_id=1, source_target_pairs={{0,16},{2,18},{4,20},{6,22},{8,24},{10,26},{12,28},{14,30},{16,0},... | collective-permute-start | bytes 221192 | tf_op jit(solution)/shard_map/ppermute | solution.py:58
  353.1 17.7 %all-to-all-start.1 = ((bf16[16,48,192]{2,1,0:T(8,128)(2,1)}), bf16[16,48,192]{2,1,0:T(8,128)(2,1)S(1)}, u32[]{:S(2)}, u32[]{:S(2)}) async-start(bf16[16,48,192]{2,1,0:T(8,128)(2,1)} %bitcast.51), calls=%async_computation.1 | async-start | bytes 786432 | tf_op jit(solution)/shard_map/all_to_all | solution.py:981
  370.8 18.1 %all-to-all-start = ((bf16[16,48,192]{2,1,0:T(8,128)(2,1)}), bf16[16,48,192]{2,1,0:T(8,128)(2,1)S(1)}, u32[]{:S(2)}, u32[]{:S(2)}) async-start(bf16[16,48,192]{2,1,0:T(8,128)(2,1)} %bitcast.52), calls=%async_computation | async-start | bytes 786432 | tf_op jit(solution)/shard_map/all_to_all | solution.py:981
  398.9 14.8 %collective-permute-start.46 = (bf16[1,2,48,768]{3,2,1,0:T(8,128)(2,1)S(1)}, bf16[1,2,48,768]{3,2,1,0:T(8,128)(2,1)S(1)}, u32[]{:S(2)}, u32[]{:S(2)}) collective-permute-start(bf16[1,2,48,768]{3,2,1,0:T(8,128)(2,1)S(1)} %get-tuple-element.98), channel_id=1, source_target_pairs={{0,16},{2,18},{4,20},{6,22},{8,24},{10,26},{12,28},{14,30},{16,0},... | collective-permute-start | bytes 442376 | tf_op jit(solution)/shard_map/ppermute | solution.py:58
  400.7 14.8 %collective-permute-start.56 = (bf16[1,2,48,768]{3,2,1,0:T(8,128)(2,1)S(1)}, bf16[1,2,48,768]{3,2,1,0:T(8,128)(2,1)S(1)}, u32[]{:S(2)}, u32[]{:S(2)}) collective-permute-start(bf16[1,2,48,768]{3,2,1,0:T(8,128)(2,1)S(1)} %get-tuple-element.96), channel_id=1, source_target_pairs={{0,16},{2,18},{4,20},{6,22},{8,24},{10,26},{12,28},{14,30},{16,0},... | collective-permute-start | bytes 442376 | tf_op jit(solution)/shard_map/ppermute | solution.py:58
  411.9 10.2 %collective-permute-start.51 = (bf16[1,2,48,768]{3,2,1,0:T(8,128)(2,1)S(1)}, bf16[1,2,48,768]{3,2,1,0:T(8,128)(2,1)S(1)}, u32[]{:S(2)}, u32[]{:S(2)}) collective-permute-start(bf16[1,2,48,768]{3,2,1,0:T(8,128)(2,1)S(1)} %get-tuple-element.97), channel_id=1, source_target_pairs={{0,16},{2,18},{4,20},{6,22},{8,24},{10,26},{12,28},{14,30},{16,0},... | collective-permute-start | bytes 442376 | tf_op jit(solution)/shard_map/ppermute | solution.py:58
  413.7 15.8 %collective-permute-start.47 = (bf16[2,2,48,768]{3,2,1,0:T(8,128)(2,1)S(1)}, bf16[2,2,48,768]{3,2,1,0:T(8,128)(2,1)S(1)}, u32[]{:S(2)}, u32[]{:S(2)}) collective-permute-start(bf16[2,2,48,768]{3,2,1,0:T(8,128)(2,1)S(1)} %pad_maximum_fusion.12), channel_id=1, source_target_pairs={{0,8},{2,10},{4,12},{6,14},{8,0},{10,2},{12,4},{14,6},{16,24},{18,... | collective-permute-start | bytes 884744 | tf_op jit(solution)/shard_map/ppermute | solution.py:58
  415.5 18.7 %collective-permute-start.57 = (bf16[2,2,48,768]{3,2,1,0:T(8,128)(2,1)S(1)}, bf16[2,2,48,768]{3,2,1,0:T(8,128)(2,1)S(1)}, u32[]{:S(2)}, u32[]{:S(2)}) collective-permute-start(bf16[2,2,48,768]{3,2,1,0:T(8,128)(2,1)S(1)} %pad_maximum_fusion.14), channel_id=1, source_target_pairs={{0,8},{2,10},{4,12},{6,14},{8,0},{10,2},{12,4},{14,6},{16,24},{18,... | collective-permute-start | bytes 884744 | tf_op jit(solution)/shard_map/ppermute | solution.py:58
  416.0 20.5 %collective-permute-start.66 = (f32[8,768]{1,0:T(8,128)S(1)}, f32[8,768]{1,0:T(8,128)S(1)}, u32[]{:S(2)}, u32[]{:S(2)}) collective-permute-start(f32[8,768]{1,0:T(8,128)S(1)} %pad_maximum_fusion.18), channel_id=1, source_target_pairs={{0,1},{1,0},{2,3},{3,2},{4,5},{5,4},{6,7},{7,6},{8,9},{9,8},{10,11... | collective-permute-start | bytes 73736 | tf_op jit(solution)/shard_map/ppermute | solution.py:58
  417.6 17.7 %collective-permute-start.61 = (bf16[1,2,48,768]{3,2,1,0:T(8,128)(2,1)S(1)}, bf16[1,2,48,768]{3,2,1,0:T(8,128)(2,1)S(1)}, u32[]{:S(2)}, u32[]{:S(2)}) collective-permute-start(bf16[1,2,48,768]{3,2,1,0:T(8,128)(2,1)S(1)} %get-tuple-element.95), channel_id=1, source_target_pairs={{0,16},{2,18},{4,20},{6,22},{8,24},{10,26},{12,28},{14,30},{16,0},... | collective-permute-start | bytes 442376 | tf_op jit(solution)/shard_map/ppermute | solution.py:58
  422.2 40.3 %collective-permute-start.52 = (bf16[2,2,48,768]{3,2,1,0:T(8,128)(2,1)S(1)}, bf16[2,2,48,768]{3,2,1,0:T(8,128)(2,1)S(1)}, u32[]{:S(2)}, u32[]{:S(2)}) collective-permute-start(bf16[2,2,48,768]{3,2,1,0:T(8,128)(2,1)S(1)} %pad_maximum_fusion.13), channel_id=1, source_target_pairs={{0,4},{2,6},{4,0},{6,2},{8,12},{10,14},{12,8},{14,10},{16,20},{18,... | collective-permute-start | bytes 884744 | tf_op jit(solution)/shard_map/ppermute | solution.py:58
  429.6 35.2 %collective-permute-start.48 = (bf16[4,2,48,768]{3,2,1,0:T(8,128)(2,1)S(1)}, bf16[4,2,48,768]{3,2,1,0:T(8,128)(2,1)}, u32[]{:S(2)}, u32[]{:S(2)}) collective-permute-start(bf16[4,2,48,768]{3,2,1,0:T(8,128)(2,1)S(1)} %pad_maximum_fusion.5.refs_0_), channel_id=1, source_target_pairs={{0,4},{2,6},{4,0},{6,2},{8,12},{10,14},{12,8},{14,10},{16,20},{18,... | collective-permute-start | bytes 1769480 | tf_op jit(solution)/shard_map/ppermute | solution.py:58
  434.3 31.0 %collective-permute-start.58 = (bf16[4,2,48,768]{3,2,1,0:T(8,128)(2,1)S(1)}, bf16[4,2,48,768]{3,2,1,0:T(8,128)(2,1)S(1)}, u32[]{:S(2)}, u32[]{:S(2)}) collective-permute-start(bf16[4,2,48,768]{3,2,1,0:T(8,128)(2,1)S(1)} %pad_maximum_fusion.7.refs_0_), channel_id=1, source_target_pairs={{0,4},{2,6},{4,0},{6,2},{8,12},{10,14},{12,8},{14,10},{16,20},{18,... | collective-permute-start | bytes 1769480 | tf_op jit(solution)/shard_map/ppermute | solution.py:58
  435.3 27.4 %collective-permute-start.62 = (bf16[2,2,48,768]{3,2,1,0:T(8,128)(2,1)S(1)}, bf16[2,2,48,768]{3,2,1,0:T(8,128)(2,1)S(1)}, u32[]{:S(2)}, u32[]{:S(2)}) collective-permute-start(bf16[2,2,48,768]{3,2,1,0:T(8,128)(2,1)S(1)} %pad_maximum_fusion.15), channel_id=1, source_target_pairs={{0,4},{2,6},{4,0},{6,2},{8,12},{10,14},{12,8},{14,10},{16,20},{18,... | collective-permute-start | bytes 884744 | tf_op jit(solution)/shard_map/ppermute | solution.py:58
  445.1 17.2 %collective-permute-start.69 = (f32[8,768]{1,0:T(8,128)S(1)}, f32[8,768]{1,0:T(8,128)S(1)}, u32[]{:S(2)}, u32[]{:S(2)}) collective-permute-start(f32[8,768]{1,0:T(8,128)S(1)} %add.447), channel_id=1, source_target_pairs={{0,4},{2,6},{4,0},{6,2},{8,12},{10,14},{12,8},{14,10},{16,20},{18,... | collective-permute-start | bytes 73736 | tf_op jit(solution)/shard_map/ppermute | solution.py:58
  462.6 16.4 %collective-permute-start.53 = (bf16[4,2,48,768]{3,2,1,0:T(8,128)(2,1)S(1)}, bf16[4,2,48,768]{3,2,1,0:T(8,128)(2,1)}, u32[]{:S(2)}, u32[]{:S(2)}) collective-permute-start(bf16[4,2,48,768]{3,2,1,0:T(8,128)(2,1)S(1)} %pad_maximum_fusion.6.refs_4_), channel_id=1, source_target_pairs={{0,8},{2,10},{4,12},{6,14},{8,0},{10,2},{12,4},{14,6},{16,24},{18,... | collective-permute-start | bytes 1769480 | tf_op jit(solution)/shard_map/ppermute | solution.py:58
  462.7 28.3 %collective-permute-start.63 = (bf16[4,2,48,768]{3,2,1,0:T(8,128)(2,1)S(1)}, bf16[4,2,48,768]{3,2,1,0:T(8,128)(2,1)S(1)}, u32[]{:S(2)}, u32[]{:S(2)}) collective-permute-start(bf16[4,2,48,768]{3,2,1,0:T(8,128)(2,1)S(1)} %pad_maximum_fusion.8.refs_4_), channel_id=1, source_target_pairs={{0,8},{2,10},{4,12},{6,14},{8,0},{10,2},{12,4},{14,6},{16,24},{18,... | collective-permute-start | bytes 1769480 | tf_op jit(solution)/shard_map/ppermute | solution.py:58
  464.8 26.2 %collective-permute-start.59 = (bf16[4,2,48,768]{3,2,1,0:T(8,128)(2,1)S(1)}, bf16[4,2,48,768]{3,2,1,0:T(8,128)(2,1)S(1)}, u32[]{:S(2)}, u32[]{:S(2)}) collective-permute-start(bf16[4,2,48,768]{3,2,1,0:T(8,128)(2,1)S(1)} %pad_maximum_fusion.7.refs_0_), channel_id=1, source_target_pairs={{0,2},{2,0},{4,6},{6,4},{8,10},{10,8},{12,14},{14,12},{16,18},{18,... | collective-permute-start | bytes 1769480 | tf_op jit(solution)/shard_map/ppermute | solution.py:58
  464.8 26.7 %collective-permute-start.64 = (bf16[4,2,48,768]{3,2,1,0:T(8,128)(2,1)S(1)}, bf16[4,2,48,768]{3,2,1,0:T(8,128)(2,1)S(1)}, u32[]{:S(2)}, u32[]{:S(2)}) collective-permute-start(bf16[4,2,48,768]{3,2,1,0:T(8,128)(2,1)S(1)} %pad_maximum_fusion.8.refs_4_), channel_id=1, source_target_pairs={{0,2},{2,0},{4,6},{6,4},{8,10},{10,8},{12,14},{14,12},{16,18},{18,... | collective-permute-start | bytes 1769480 | tf_op jit(solution)/shard_map/ppermute | solution.py:58
  465.3 26.3 %collective-permute-start.60 = (bf16[4,2,48,768]{3,2,1,0:T(8,128)(2,1)S(1)}, bf16[4,2,48,768]{3,2,1,0:T(8,128)(2,1)S(1)}, u32[]{:S(2)}, u32[]{:S(2)}) collective-permute-start(bf16[4,2,48,768]{3,2,1,0:T(8,128)(2,1)S(1)} %collective-permute-done.58.refs_1_), channel_id=1, source_target_pairs={{0,2},{2,0},{4,6},{6,4},{8,10},{10,8},{12,14},{14,12},{16,18},{18,... | collective-permute-start | bytes 1769480 | tf_op jit(solution)/shard_map/ppermute | solution.py:58
  478.9 27.8 %collective-permute-start.49 = (bf16[4,2,48,768]{3,2,1,0:T(8,128)(2,1)S(1)}, bf16[4,2,48,768]{3,2,1,0:T(8,128)(2,1)}, u32[]{:S(2)}, u32[]{:S(2)}) collective-permute-start(bf16[4,2,48,768]{3,2,1,0:T(8,128)(2,1)S(1)} %pad_maximum_fusion.5.refs_0_), channel_id=1, source_target_pairs={{0,2},{2,0},{4,6},{6,4},{8,10},{10,8},{12,14},{14,12},{16,18},{18,... | collective-permute-start | bytes 1769480 | tf_op jit(solution)/shard_map/ppermute | solution.py:58
  491.0 15.7 %collective-permute-start.54 = (bf16[4,2,48,768]{3,2,1,0:T(8,128)(2,1)S(1)}, bf16[4,2,48,768]{3,2,1,0:T(8,128)(2,1)}, u32[]{:S(2)}, u32[]{:S(2)}) collective-permute-start(bf16[4,2,48,768]{3,2,1,0:T(8,128)(2,1)S(1)} %pad_maximum_fusion.6.refs_4_), channel_id=1, source_target_pairs={{0,2},{2,0},{4,6},{6,4},{8,10},{10,8},{12,14},{14,12},{16,18},{18,... | collective-permute-start | bytes 1769480 | tf_op jit(solution)/shard_map/ppermute | solution.py:58
  491.5 15.2 %collective-permute-start.50 = (bf16[4,2,48,768]{3,2,1,0:T(8,128)(2,1)}, bf16[4,2,48,768]{3,2,1,0:T(8,128)(2,1)}, u32[]{:S(2)}, u32[]{:S(2)}) collective-permute-start(bf16[4,2,48,768]{3,2,1,0:T(8,128)(2,1)} %collective-permute-done.48.refs_1_), channel_id=1, source_target_pairs={{0,2},{2,0},{4,6},{6,4},{8,10},{10,8},{12,14},{14,12},{16,18},{18,... | collective-permute-start | bytes 1769480 | tf_op jit(solution)/shard_map/ppermute | solution.py:58
  493.2 13.6 %collective-permute-start.55 = (bf16[4,2,48,768]{3,2,1,0:T(8,128)(2,1)}, bf16[4,2,48,768]{3,2,1,0:T(8,128)(2,1)}, u32[]{:S(2)}, u32[]{:S(2)}) collective-permute-start(bf16[4,2,48,768]{3,2,1,0:T(8,128)(2,1)} %collective-permute-done.53.refs_5_), channel_id=1, source_target_pairs={{0,2},{2,0},{4,6},{6,4},{8,10},{10,8},{12,14},{14,12},{16,18},{18,... | collective-permute-start | bytes 1769480 | tf_op jit(solution)/shard_map/ppermute | solution.py:58
  (57 other events, 850.9 us)
